TPU v7x, 128 devices: a whole 4x4x4 slice. The times are simulated.
128 devices in a mesh: row: 16 (over y, z), col: 8 (over x, core).
Axes of the slice: x: 4, y: 4, z: 4, core: 2. Of those that a mesh axis runs over, the one named last changes fastest.
Arguments:
- panel: float32 [1572864, 256], P(('row', 'col')), may hold values from -2000 to 2000, as said below
Outputs:
- basis: float32 [1572864, 256], P(('row', 'col'))
- factor: float32 [256, 256], replicated
Inputs may be any that keep to these rules, and one draw needn't show every extreme that they name: `panel`: Real-valued entries of full column rank.
All inputs are finite; a program needn't handle non-finite values.
Results may differ from a plain program's by a relative error of at most 0.0003.
Values sent between devices are 32-bit elements; how exact they have to be, the bound alone decides.
No kernel may reach another device: no remote copies, remote signals or barrier semaphores. Data moves between devices by JAX's collectives and lax.ppermute only.
A program may use at most 128 MiB of HBM per device.

v0:
```python
import functools
import jax
import jax.numpy as jnp
from jax import lax
from jax.experimental import pallas as pl
from jax.experimental.pallas import tpu as pltpu
from jax.sharding import PartitionSpec as P

K = 256
H = 128
HALF = 136
F32 = jnp.float32
BF16 = jnp.bfloat16
VMEM_WHOLE = pl.BlockSpec(memory_space=pltpu.VMEM)


def split2(x):
    hi = x.astype(BF16)
    return hi, (x - hi.astype(F32)).astype(BF16)


def split3(x):
    hi = x.astype(BF16)
    rest = x - hi.astype(F32)
    mid = rest.astype(BF16)
    return hi, mid, (rest - mid.astype(F32)).astype(BF16)


def dot_tn(a, b):
    return lax.dot_general(a, b, (((0,), (0,)), ((), ())), preferred_element_type=F32)


def dot_nn(a, b):
    return lax.dot_general(a, b, (((1,), (0,)), ((), ())), preferred_element_type=F32)


def dot_nt(a, b):
    return lax.dot_general(a, b, (((1,), (1,)), ((), ())), preferred_element_type=F32)


def iotas(shape):
    return lax.broadcasted_iota(jnp.int32, shape, 0), lax.broadcasted_iota(jnp.int32, shape, 1)


def core_index():
    return lax.rem(lax.axis_index("col"), 2)


def pack(gram, keep_ref, send_ref):
    i, j = iotas((H, H))
    low = gram[H:, H:]
    top = jnp.where(i >= j, gram[:H, :H], low)
    diag = jnp.sum(jnp.where(i == j, low, 0.0), axis=0, keepdims=True)
    tail = jnp.broadcast_to(diag, (8, H))
    core = core_index()

    def put(first_ref, second_ref):
        first_ref[0:H, :] = top
        first_ref[H:HALF, :] = tail
        second_ref[0:H, :] = gram[H:, :H]
        second_ref[H:HALF, :] = jnp.zeros((8, H), F32)

    @pl.when(core == 0)
    def _():
        put(keep_ref, send_ref)

    @pl.when(core == 1)
    def _():
        put(send_ref, keep_ref)


def unpack(mine_ref, other_ref, out_ref):
    core = core_index()
    i, j = iotas((H, H))

    def get(first_ref, second_ref):
        top = first_ref[0:H, :]
        topt = top.T
        diag = first_ref[H:H + 1, :]
        side = second_ref[0:H, :]
        out_ref[0:H, 0:H] = jnp.where(i >= j, top, topt)
        corner = jnp.where(i < j, top, topt)
        out_ref[H:, H:] = jnp.where(i == j, jnp.broadcast_to(diag, (H, H)), corner)
        out_ref[H:, 0:H] = side
        out_ref[0:H, H:] = side.T

    @pl.when(core == 0)
    def _():
        get(mine_ref, other_ref)

    @pl.when(core == 1)
    def _():
        get(other_ref, mine_ref)


def gram_kernel(steps, x_ref, keep_ref, send_ref, acc):
    step = pl.program_id(0)

    @pl.when(step == 0)
    def _():
        acc[...] = jnp.zeros_like(acc)

    h, m = split2(x_ref[...])
    acc[:, :2 * K] += dot_tn(h, jnp.concatenate([h, m], axis=1))
    acc[:, 2 * K:] += dot_tn(m, m)

    @pl.when(step == steps - 1)
    def _():
        cross = acc[:, K:2 * K]
        pack(acc[:, :K] + (cross + cross.T) + acc[:, 2 * K:], keep_ref, send_ref)


def gram_call(x, rows):
    steps = x.shape[0] // rows
    half = jax.ShapeDtypeStruct((HALF, H), F32)
    return pl.pallas_call(
        functools.partial(gram_kernel, steps),
        out_shape=(half, half),
        grid=(steps,),
        in_specs=[pl.BlockSpec((rows, K), lambda i: (i, 0))],
        out_specs=[pl.BlockSpec((HALF, H), lambda i: (0, 0))] * 2,
        scratch_shapes=[pltpu.VMEM((K, 3 * K), F32)],
        name="gram_one",
    )(x)


def first_kernel(steps, x_ref, w_ref, first_ref, keep_ref, send_ref, acc):
    step = pl.program_id(0)

    @pl.when(step == 0)
    def _():
        acc[...] = jnp.zeros_like(acc)

    h, m, l = split3(x_ref[...])
    first = dot_nn(jnp.concatenate([h, m, l, h, m], axis=1), w_ref[...])
    first_ref[...] = first
    fh, fm = split2(first)
    acc[...] += dot_tn(fh, jnp.concatenate([fh, fm], axis=1))

    @pl.when(step == steps - 1)
    def _():
        cross = acc[:, K:]
        pack(acc[:, :K] + (cross + cross.T), keep_ref, send_ref)


def first_call(x, w, rows):
    steps = x.shape[0] // rows
    half = jax.ShapeDtypeStruct((HALF, H), F32)
    return pl.pallas_call(
        functools.partial(first_kernel, steps),
        out_shape=(jax.ShapeDtypeStruct(x.shape, F32), half, half),
        grid=(steps,),
        in_specs=[pl.BlockSpec((rows, K), lambda i: (i, 0)), VMEM_WHOLE],
        out_specs=[pl.BlockSpec((rows, K), lambda i: (i, 0))] + [pl.BlockSpec((HALF, H), lambda i: (0, 0))] * 2,
        scratch_shapes=[pltpu.VMEM((K, 2 * K), F32)],
        name="first_and_gram_two",
    )(x, w)


def basis_kernel(scale, f_ref, c_ref, out_ref):
    first = f_ref[...]
    h, m = split2(first)
    out_ref[...] = (first + dot_nn(jnp.concatenate([h, m, h], axis=1), c_ref[...])) * scale


def basis_call(first, c, rows, scale):
    return pl.pallas_call(
        functools.partial(basis_kernel, scale),
        out_shape=jax.ShapeDtypeStruct(first.shape, F32),
        grid=(first.shape[0] // rows,),
        in_specs=[pl.BlockSpec((rows, K), lambda i: (i, 0)), VMEM_WHOLE],
        out_specs=pl.BlockSpec((rows, K), lambda i: (i, 0)),
        name="basis",
    )(first, c)


B = 32
S = 8


def eliminate(rows_a):
    rows_a = list(rows_a)
    width = rows_a[0].shape[1]
    sub = lax.broadcasted_iota(jnp.int32, (S, H), 0)
    for s in range(B // S):
        cols = [jnp.broadcast_to(rows_a[s][:, S * s + k:S * s + k + 1], (S, H)) for k in range(S)]
        x = rows_a[s]
        pivots, factors, us = [], [], []
        for j in range(S):
            r = jnp.broadcast_to(lax.rsqrt(cols[j][j:j + 1, :]), (S, H))
            lj = jnp.where(sub >= j, cols[j] * r, 0.0)
            fac = [None] * S
            for k in range(j + 1, S):
                fac[k] = jnp.broadcast_to(lj[k:k + 1, :], (S, H))
                cols[k] = cols[k] - lj * fac[k]
            u = jnp.broadcast_to(x[j:j + 1, :], (S, width)) * jnp.concatenate([r] * (width // H), axis=1)
            below = jnp.concatenate([jnp.where(sub > j, lj, 0.0)] * (width // H), axis=1)
            here = jnp.concatenate([sub == j] * (width // H), axis=1)
            x = jnp.where(here, u, x - below * u)
            pivots.append(r)
            factors.append(fac)
            us.append(u)
        rows_a[s] = x
        for q in range(s + 1, B // S):
            y = rows_a[q]
            c = [jnp.broadcast_to(y[:, S * s + k:S * s + k + 1], (S, H)) for k in range(S)]
            for j in range(S):
                lj = c[j] * pivots[j]
                for k in range(j + 1, S):
                    c[k] = c[k] - lj * factors[j][k]
                y = y - jnp.concatenate([lj] * (width // H), axis=1) * us[j]
            rows_a[q] = y
    return rows_a


def factorize(t_ref):
    def block(b, carry):
        r0 = pl.multiple_of(b * B, B)
        lane0 = pl.multiple_of(lax.div(b, H // B) * H, H)
        shift = lax.rem(b, H // B) * B
        d = t_ref[pl.ds(r0, B), pl.ds(lane0, H)]
        d = pltpu.roll(d, lax.rem(H - shift, H), 1)
        r = t_ref[pl.ds(r0, B), :]
        full = jnp.concatenate([d, r], axis=1)
        out = eliminate([full[S * s:S * s + S] for s in range(B // S)])
        u = jnp.concatenate([o[:, H:] for o in out], axis=0)
        t_ref[pl.ds(r0, B), :] = u
        lane = lax.broadcasted_iota(jnp.int32, (B, K), 1)
        left = jnp.where(lane >= r0 + B, u[:, :K], 0.0)
        lh, lm, ll = split3(left)
        uh, um, ul = split3(u)
        upd = dot_tn(
            jnp.concatenate([lh, lh, lm, lm, lh, ll], axis=0),
            jnp.concatenate([uh, um, uh, um, ul, uh], axis=0),
        )
        t_ref[...] -= upd
        return carry

    lax.fori_loop(0, K // B, block, 0)


def load_augmented(mine_ref, other_ref, t_ref):
    unpack(mine_ref, other_ref, t_ref.at[:, 0:K])
    i, j = iotas((K, K))
    t_ref[:, K:] = jnp.where(i == j, 1.0, 0.0)


def chol_one_kernel(mine_ref, other_ref, w_ref, upper_ref, t_ref):
    load_augmented(mine_ref, other_ref, t_ref)
    factorize(t_ref)
    i, j = iotas((K, K))
    upper_ref[...] = jnp.where(i <= j, t_ref[:, :K], 0.0)
    wt = jnp.where(i >= j, t_ref[:, K:], 0.0).T
    h, m = split2(wt)
    w_ref[0:K, :] = h
    w_ref[K:2 * K, :] = h
    w_ref[2 * K:3 * K, :] = h
    w_ref[3 * K:4 * K, :] = m
    w_ref[4 * K:5 * K, :] = m


def chol_one_call(mine, other):
    return pl.pallas_call(
        chol_one_kernel,
        out_shape=(jax.ShapeDtypeStruct((5 * K, K), BF16), jax.ShapeDtypeStruct((K, K), F32)),
        in_specs=[VMEM_WHOLE] * 2,
        out_specs=[VMEM_WHOLE] * 2,
        scratch_shapes=[pltpu.VMEM((K, 2 * K), F32)],
        name="factor_one",
    )(mine, other)


TOL = 1e-7


def largest(x):
    return jnp.max(jnp.abs(x))


def chol_two_kernel(scale, mine_ref, other_ref, upper_ref, c_ref, factor_ref, g_ref, x_ref, z_ref, t_ref):
    unpack(mine_ref, other_ref, g_ref)
    i, j = iotas((K, K))
    eye = jnp.where(i == j, 1.0, 0.0)
    half_low = jnp.where(i > j, 1.0, jnp.where(i == j, 0.5, 0.0))

    x_ref[...] = (g_ref[...] - eye) * half_low

    def x_more(state):
        step, change = state
        return jnp.logical_and(step < 10, jnp.logical_not(change <= TOL))

    def x_next(state):
        old = x_ref[...]
        h, m = split2(old)
        square = dot_nt(jnp.concatenate([h, h, m], axis=1), jnp.concatenate([h, m, h], axis=1))
        new = (g_ref[...] - eye - square) * half_low
        x_ref[...] = new
        return state[0] + 1, largest(new - old)

    _, change = lax.while_loop(x_more, x_next, (jnp.int32(0), jnp.float32(1.0)))
    x = x_ref[...]
    z_ref[...] = -x

    def residual():
        z = z_ref[...]
        xh, xm = split2(x_ref[...])
        zh, zm = split2(z)
        prod = dot_nn(jnp.concatenate([xh, xh, xm], axis=1), jnp.concatenate([zh, zm, zh], axis=0))
        return -(x_ref[...] + z + prod)

    def z_more(state):
        step, size = state
        return jnp.logical_and(step < 6, jnp.logical_not(size <= TOL))

    def z_next(state):
        r = residual()
        z = z_ref[...]
        rh, rm = split2(r)
        zh, zm = split2(z)
        z_ref[...] = z + r + dot_nn(jnp.concatenate([zh, zh, zm], axis=1), jnp.concatenate([rh, rm, rh], axis=0))
        return state[0] + 1, largest(r) * largest(r) * 256.0

    _, size = lax.while_loop(z_more, z_next, (jnp.int32(0), jnp.float32(1.0)))
    lowest = jnp.min(jnp.where(i == j, x, 0.0))
    good = jnp.logical_and(jnp.logical_and(change <= TOL, size <= TOL), lowest > -0.5)

    @pl.when(jnp.logical_not(good))
    def _():
        t_ref[:, :K] = g_ref[...]
        t_ref[:, K:] = eye
        factorize(t_ref)
        x_ref[...] = jnp.where(i <= j, t_ref[:, :K], 0.0).T - eye
        z_ref[...] = jnp.where(i >= j, t_ref[:, K:], 0.0) - eye

    ch, cm = split2(z_ref[...].T)
    c_ref[0:K, :] = ch
    c_ref[K:2 * K, :] = ch
    c_ref[2 * K:3 * K, :] = cm
    u1 = upper_ref[...]
    uh, um = split2(u1)
    xh, xm = split2(x_ref[...])
    prod = dot_tn(jnp.concatenate([xh, xh, xm], axis=0), jnp.concatenate([uh, um, uh], axis=0))
    factor_ref[...] = (u1 + prod) / scale


def chol_two_call(mine, other, upper, scale):
    return pl.pallas_call(
        functools.partial(chol_two_kernel, scale),
        out_shape=(jax.ShapeDtypeStruct((3 * K, K), BF16), jax.ShapeDtypeStruct((K, K), F32)),
        in_specs=[VMEM_WHOLE] * 3,
        out_specs=[VMEM_WHOLE] * 2,
        scratch_shapes=[pltpu.VMEM((K, K), F32)] * 3 + [pltpu.VMEM((K, 2 * K), F32)],
        name="factor_two",
    )(mine, other, upper)


def swap(value, axis, distance):
    return lax.ppermute(value, axis, [(i, i ^ distance) for i in range(lax.axis_size(axis))])


def sum_over(value, axis, step):
    a, b, c = [swap(value, axis, step * d) for d in (1, 2, 3)]
    return (value + a) + (b + c)


def reduce_gram(keep, send):
    value = keep + swap(send, "col", 1)
    value = sum_over(value, "col", 2)
    value = sum_over(value, "row", 1)
    value = sum_over(value, "row", 4)
    return value, swap(value, "col", 1)


ROWS_PER_STEP = 2048


def shards(panel):
    total_rows = panel.shape[0] * lax.axis_size("row") * lax.axis_size("col")
    scale = float(total_rows) ** 0.5
    mine, other = reduce_gram(*gram_call(panel, ROWS_PER_STEP))
    w, upper = chol_one_call(mine, other)
    first, keep, send = first_call(panel, w, ROWS_PER_STEP)
    mine, other = reduce_gram(keep, send)
    c, factor = chol_two_call(mine, other, upper, scale)
    return basis_call(first, c, ROWS_PER_STEP, scale), factor


def solution(mesh):
    return jax.shard_map(
        shards,
        mesh=mesh,
        in_specs=(P(("row", "col"), None),),
        out_specs=(P(("row", "col"), None), P()),
        check_vma=False,
    )
```

profile of v0, /device:TPU:1, one launch (start us, length us, event | category | flops | bytes accessed | tf_op | source)
XLA Modules:
  0.0 119.6 jit_solution(15537645952856996913)
XLA Ops:
  0.6 10.0 %gram_one.1 = (f32[136,128]{1,0:T(8,128)}, f32[136,128]{1,0:T(8,128)}) custom-call(f32[12288,256]{1,0:T(8,128)} %x_ref.3), custom_call_target="tpu_custom_call" | custom-call | tf_op jit(solution)/shard_map/gram_one/pallas_call | solution.py:116
  10.7 1.4 %collective-permute-start = (f32[136,128]{1,0:T(8,128)}, f32[136,128]{1,0:T(8,128)S(1)}, u32[]{:S(2)}, u32[]{:S(2)}) collective-permute-start(f32[136,128]{1,0:T(8,128)} %get-tuple-element.12), channel_id=1, source_target_pairs={{0,1},{1,0},{2,3},{3,2},{4,5},{5,4},{6,7},{7,6},{8,9},{9,8},{10,11... | collective-permute-start | bytes 208904 | tf_op jit(solution)/shard_map/ppermute | solution.py:358
  12.0 1.1 collective-permute-done
  13.1 0.9 add.60
  14.0 2.7 %collective-permute-start.3 = (f32[136,128]{1,0:T(8,128)S(1)}, f32[136,128]{1,0:T(8,128)S(1)}, u32[]{:S(2)}, u32[]{:S(2)}) collective-permute-start(f32[136,128]{1,0:T(8,128)S(1)} %add.60), channel_id=1, source_target_pairs={{0,6},{1,7},{2,4},{3,5},{4,2},{5,3},{6,0},{7,1},{8,14},{9,15},{10,... | collective-permute-start | bytes 208904 | tf_op jit(solution)/shard_map/ppermute | solution.py:358
  16.7 0.5 collective-permute-start.2
  17.2 0.2 collective-permute-start.1
  17.4 1.4 %collective-permute-done.3 = f32[136,128]{1,0:T(8,128)S(1)} collective-permute-done((f32[136,128]{1,0:T(8,128)S(1)}, f32[136,128]{1,0:T(8,128)S(1)}, u32[]{:S(2)}, u32[]{:S(2)}) %collective-permute-start.3) | collective-permute-done | bytes 69664 | tf_op jit(solution)/shard_map/ppermute | solution.py:358
  18.8 2.5 %collective-permute-done.2 = f32[136,128]{1,0:T(8,128)S(1)} collective-permute-done((f32[136,128]{1,0:T(8,128)S(1)}, f32[136,128]{1,0:T(8,128)S(1)}, u32[]{:S(2)}, u32[]{:S(2)}) %collective-permute-start.2) | collective-permute-done | bytes 69664 | tf_op jit(solution)/shard_map/ppermute | solution.py:358
  21.4 3.8 %collective-permute-start.6 = (f32[136,128]{1,0:T(8,128)S(1)}, f32[136,128]{1,0:T(8,128)S(1)}, u32[]{:S(2)}, u32[]{:S(2)}) collective-permute-start(f32[136,128]{1,0:T(8,128)S(1)} %add_add_fusion.5), channel_id=1, source_target_pairs={{0,24},{8,16},{16,8},{24,0},{32,56},{40,48},{48,40},{56,32},{64,88... | collective-permute-start | bytes 208904 | tf_op jit(solution)/shard_map/ppermute | solution.py:358
  25.2 0.7 collective-permute-start.4
  25.9 1.3 %collective-permute-done.6 = f32[136,128]{1,0:T(8,128)S(1)} collective-permute-done((f32[136,128]{1,0:T(8,128)S(1)}, f32[136,128]{1,0:T(8,128)S(1)}, u32[]{:S(2)}, u32[]{:S(2)}) %collective-permute-start.6) | collective-permute-done | bytes 69664 | tf_op jit(solution)/shard_map/ppermute | solution.py:358
  27.2 2.8 %collective-permute-done.5 = f32[136,128]{1,0:T(8,128)S(1)} collective-permute-done((f32[136,128]{1,0:T(8,128)S(1)}, f32[136,128]{1,0:T(8,128)S(1)}, u32[]{:S(2)}, u32[]{:S(2)}) %collective-permute-start.5) | collective-permute-done | bytes 69664 | tf_op jit(solution)/shard_map/ppermute | solution.py:358
  30.0 2.8 %collective-permute-start.9 = (f32[136,128]{1,0:T(8,128)S(1)}, f32[136,128]{1,0:T(8,128)S(1)}, u32[]{:S(2)}, u32[]{:S(2)}) collective-permute-start(f32[136,128]{1,0:T(8,128)S(1)} %add_add_fusion.4), channel_id=1, source_target_pairs={{0,96},{8,104},{16,112},{24,120},{32,64},{40,72},{48,80},{56,88},{... | collective-permute-start | bytes 208904 | tf_op jit(solution)/shard_map/ppermute | solution.py:358
  32.8 0.3 collective-permute-start.8
  33.2 0.3 collective-permute-start.7
  33.5 1.3 %collective-permute-done.9 = f32[136,128]{1,0:T(8,128)S(1)} collective-permute-done((f32[136,128]{1,0:T(8,128)S(1)}, f32[136,128]{1,0:T(8,128)S(1)}, u32[]{:S(2)}, u32[]{:S(2)}) %collective-permute-start.9) | collective-permute-done | bytes 69664 | tf_op jit(solution)/shard_map/ppermute | solution.py:358
  34.8 2.7 %collective-permute-done.8 = f32[136,128]{1,0:T(8,128)S(1)} collective-permute-done((f32[136,128]{1,0:T(8,128)S(1)}, f32[136,128]{1,0:T(8,128)S(1)}, u32[]{:S(2)}, u32[]{:S(2)}) %collective-permute-start.8) | collective-permute-done | bytes 69664 | tf_op jit(solution)/shard_map/ppermute | solution.py:358
  37.5 5.0 %collective-permute-start.10 = (f32[136,128]{1,0:T(8,128)S(1)}, f32[136,128]{1,0:T(8,128)S(1)}, u32[]{:S(2)}, u32[]{:S(2)}) collective-permute-start(f32[136,128]{1,0:T(8,128)S(1)} %add_add_fusion.3.mine_ref), channel_id=1, source_target_pairs={{0,1},{1,0},{2,3},{3,2},{4,5},{5,4},{6,7},{7,6},{8,9},{9,8},{10,11... | collective-permute-start | bytes 208904 | tf_op jit(solution)/shard_map/ppermute | solution.py:358
  42.6 0.9 collective-permute-done.10.other_ref
  43.5 0.6 copy-done.3
  44.1 10.4 %factor_one.1 = (bf16[1280,256]{1,0:T(8,128)(2,1)}, f32[256,256]{1,0:T(8,128)}) custom-call(f32[136,128]{1,0:T(8,128)} %copy-done.1, f32[136,128]{1,0:T(8,128)} %copy-done.3), custom_call_target="tpu_custom_call" | custom-call | tf_op jit(solution)/shard_map/factor_one/pallas_call | solution.py:263
  54.5 20.5 %first_and_gram_two.1 = (f32[12288,256]{1,0:T(8,128)}, f32[136,128]{1,0:T(8,128)}, f32[136,128]{1,0:T(8,128)}) custom-call(f32[12288,256]{1,0:T(8,128)} %x_ref.3, bf16[1280,256]{1,0:T(8,128)(2,1)} %get-tuple-element.13.w_ref), custom_call_target="tpu_custom_call" | custom-call | tf_op jit(solution)/shard_map/first_and_gram_two/pallas_call | solution.py:149
  75.0 0.3 collective-permute-start.11
  75.3 1.1 collective-permute-done.11
  76.4 0.9 add.70
  77.3 1.1 collective-permute-start.14
  78.4 0.9 collective-permute-start.13
  79.3 1.4 %collective-permute-start.12 = (f32[136,128]{1,0:T(8,128)S(1)}, f32[136,128]{1,0:T(8,128)S(1)}, u32[]{:S(2)}, u32[]{:S(2)}) collective-permute-start(f32[136,128]{1,0:T(8,128)S(1)} %add.70), channel_id=1, source_target_pairs={{0,2},{1,3},{2,0},{3,1},{4,6},{5,7},{6,4},{7,5},{8,10},{9,11},{10,... | collective-permute-start | bytes 208904 | tf_op jit(solution)/shard_map/ppermute | solution.py:358
  80.7 1.1 collective-permute-done.14
  81.8 1.4 %collective-permute-done.13 = f32[136,128]{1,0:T(8,128)S(1)} collective-permute-done((f32[136,128]{1,0:T(8,128)S(1)}, f32[136,128]{1,0:T(8,128)S(1)}, u32[]{:S(2)}, u32[]{:S(2)}) %collective-permute-start.13) | collective-permute-done | bytes 69664 | tf_op jit(solution)/shard_map/ppermute | solution.py:358
  83.2 0.6 collective-permute-done.12
  83.8 1.1 collective-permute-start.17
  84.9 0.8 collective-permute-start.16
  85.7 1.4 %collective-permute-start.15 = (f32[136,128]{1,0:T(8,128)S(1)}, f32[136,128]{1,0:T(8,128)S(1)}, u32[]{:S(2)}, u32[]{:S(2)}) collective-permute-start(f32[136,128]{1,0:T(8,128)S(1)} %add_add_fusion.2), channel_id=1, source_target_pairs={{0,8},{8,0},{16,24},{24,16},{32,40},{40,32},{48,56},{56,48},{64,72... | collective-permute-start | bytes 208904 | tf_op jit(solution)/shard_map/ppermute | solution.py:358
  87.2 1.1 collective-permute-done.17
  88.3 1.3 %collective-permute-done.16 = f32[136,128]{1,0:T(8,128)S(1)} collective-permute-done((f32[136,128]{1,0:T(8,128)S(1)}, f32[136,128]{1,0:T(8,128)S(1)}, u32[]{:S(2)}, u32[]{:S(2)}) %collective-permute-start.16) | collective-permute-done | bytes 69664 | tf_op jit(solution)/shard_map/ppermute | solution.py:358
  89.6 0.3 collective-permute-done.15
  89.9 1.1 collective-permute-start.20
  91.0 0.8 collective-permute-start.19
  91.8 1.4 %collective-permute-start.18 = (f32[136,128]{1,0:T(8,128)S(1)}, f32[136,128]{1,0:T(8,128)S(1)}, u32[]{:S(2)}, u32[]{:S(2)}) collective-permute-start(f32[136,128]{1,0:T(8,128)S(1)} %add_add_fusion.1), channel_id=1, source_target_pairs={{0,32},{8,40},{16,48},{24,56},{32,0},{40,8},{48,16},{56,24},{64,96... | collective-permute-start | bytes 208904 | tf_op jit(solution)/shard_map/ppermute | solution.py:358
  93.3 1.1 collective-permute-done.20
  94.4 1.3 %collective-permute-done.19 = f32[136,128]{1,0:T(8,128)S(1)} collective-permute-done((f32[136,128]{1,0:T(8,128)S(1)}, f32[136,128]{1,0:T(8,128)S(1)}, u32[]{:S(2)}, u32[]{:S(2)}) %collective-permute-start.19) | collective-permute-done | bytes 69664 | tf_op jit(solution)/shard_map/ppermute | solution.py:358
  95.7 4.1 %collective-permute-start.21 = (f32[136,128]{1,0:T(8,128)S(1)}, f32[136,128]{1,0:T(8,128)S(1)}, u32[]{:S(2)}, u32[]{:S(2)}) collective-permute-start(f32[136,128]{1,0:T(8,128)S(1)} %add_add_fusion.mine_ref), channel_id=1, source_target_pairs={{0,1},{1,0},{2,3},{3,2},{4,5},{5,4},{6,7},{7,6},{8,9},{9,8},{10,11... | collective-permute-start | bytes 208904 | tf_op jit(solution)/shard_map/ppermute | solution.py:358
  99.9 0.9 collective-permute-done.21.other_ref
  100.8 0.6 copy-done.2
  101.4 5.1 %factor_two.1 = (bf16[768,256]{1,0:T(8,128)(2,1)}, f32[256,256]{1,0:T(8,128)}) custom-call(f32[136,128]{1,0:T(8,128)} %copy-done, f32[136,128]{1,0:T(8,128)} %copy-done.2, f32[256,256]{1,0:T(8,128)} %get-tuple-element.17.upper_ref), custom_call_target="tpu_custom_call" | custom-call | tf_op jit(solution)/shard_map/factor_two/pallas_call | solution.py:347
  106.5 13.2 %basis.1 = f32[12288,256]{1,0:T(8,128)} custom-call(f32[12288,256]{1,0:T(8,128)} %get-tuple-element.14.f_ref, bf16[768,256]{1,0:T(8,128)(2,1)} %get-tuple-element.18.c_ref), custom_call_target="tpu_custom_call" | custom-call | tf_op jit(solution)/shard_map/basis/pallas_call | solution.py:167
  (17 shorter events, 0.1 us)
Async XLA Ops:
  10.7 2.5 %collective-permute-start = (f32[136,128]{1,0:T(8,128)}, f32[136,128]{1,0:T(8,128)S(1)}, u32[]{:S(2)}, u32[]{:S(2)}) collective-permute-start(f32[136,128]{1,0:T(8,128)} %get-tuple-element.12), channel_id=1, source_target_pairs={{0,1},{1,0},{2,3},{3,2},{4,5},{5,4},{6,7},{7,6},{8,9},{9,8},{10,11... | collective-permute-start | bytes 208904 | tf_op jit(solution)/shard_map/ppermute | solution.py:358
  14.0 4.8 %collective-permute-start.3 = (f32[136,128]{1,0:T(8,128)S(1)}, f32[136,128]{1,0:T(8,128)S(1)}, u32[]{:S(2)}, u32[]{:S(2)}) collective-permute-start(f32[136,128]{1,0:T(8,128)S(1)} %add.60), channel_id=1, source_target_pairs={{0,6},{1,7},{2,4},{3,5},{4,2},{5,3},{6,0},{7,1},{8,14},{9,15},{10,... | collective-permute-start | bytes 208904 | tf_op jit(solution)/shard_map/ppermute | solution.py:358
  16.7 4.7 %collective-permute-start.2 = (f32[136,128]{1,0:T(8,128)S(1)}, f32[136,128]{1,0:T(8,128)S(1)}, u32[]{:S(2)}, u32[]{:S(2)}) collective-permute-start(f32[136,128]{1,0:T(8,128)S(1)} %add.60), channel_id=1, source_target_pairs={{0,4},{1,5},{2,6},{3,7},{4,0},{5,1},{6,2},{7,3},{8,12},{9,13},{10,... | collective-permute-start | bytes 208904 | tf_op jit(solution)/shard_map/ppermute | solution.py:358
  17.2 4.1 %collective-permute-start.1 = (f32[136,128]{1,0:T(8,128)S(1)}, f32[136,128]{1,0:T(8,128)S(1)}, u32[]{:S(2)}, u32[]{:S(2)}) collective-permute-start(f32[136,128]{1,0:T(8,128)S(1)} %add.60), channel_id=1, source_target_pairs={{0,2},{1,3},{2,0},{3,1},{4,6},{5,7},{6,4},{7,5},{8,10},{9,11},{10,... | collective-permute-start | bytes 208904 | tf_op jit(solution)/shard_map/ppermute | solution.py:358
  21.4 5.8 %collective-permute-start.6 = (f32[136,128]{1,0:T(8,128)S(1)}, f32[136,128]{1,0:T(8,128)S(1)}, u32[]{:S(2)}, u32[]{:S(2)}) collective-permute-start(f32[136,128]{1,0:T(8,128)S(1)} %add_add_fusion.5), channel_id=1, source_target_pairs={{0,24},{8,16},{16,8},{24,0},{32,56},{40,48},{48,40},{56,32},{64,88... | collective-permute-start | bytes 208904 | tf_op jit(solution)/shard_map/ppermute | solution.py:358
  25.2 4.8 %collective-permute-start.5 = (f32[136,128]{1,0:T(8,128)S(1)}, f32[136,128]{1,0:T(8,128)S(1)}, u32[]{:S(2)}, u32[]{:S(2)}) collective-permute-start(f32[136,128]{1,0:T(8,128)S(1)} %add_add_fusion.5), channel_id=1, source_target_pairs={{0,16},{8,24},{16,0},{24,8},{32,48},{40,56},{48,32},{56,40},{64,80... | collective-permute-start | bytes 208904 | tf_op jit(solution)/shard_map/ppermute | solution.py:358
  25.2 4.8 %collective-permute-start.4 = (f32[136,128]{1,0:T(8,128)S(1)}, f32[136,128]{1,0:T(8,128)S(1)}, u32[]{:S(2)}, u32[]{:S(2)}) collective-permute-start(f32[136,128]{1,0:T(8,128)S(1)} %add_add_fusion.5), channel_id=1, source_target_pairs={{0,8},{8,0},{16,24},{24,16},{32,40},{40,32},{48,56},{56,48},{64,72... | collective-permute-start | bytes 208904 | tf_op jit(solution)/shard_map/ppermute | solution.py:358
  30.0 4.8 %collective-permute-start.9 = (f32[136,128]{1,0:T(8,128)S(1)}, f32[136,128]{1,0:T(8,128)S(1)}, u32[]{:S(2)}, u32[]{:S(2)}) collective-permute-start(f32[136,128]{1,0:T(8,128)S(1)} %add_add_fusion.4), channel_id=1, source_target_pairs={{0,96},{8,104},{16,112},{24,120},{32,64},{40,72},{48,80},{56,88},{... | collective-permute-start | bytes 208904 | tf_op jit(solution)/shard_map/ppermute | solution.py:358
  32.8 4.7 %collective-permute-start.8 = (f32[136,128]{1,0:T(8,128)S(1)}, f32[136,128]{1,0:T(8,128)S(1)}, u32[]{:S(2)}, u32[]{:S(2)}) collective-permute-start(f32[136,128]{1,0:T(8,128)S(1)} %add_add_fusion.4), channel_id=1, source_target_pairs={{0,64},{8,72},{16,80},{24,88},{32,96},{40,104},{48,112},{56,120},{... | collective-permute-start | bytes 208904 | tf_op jit(solution)/shard_map/ppermute | solution.py:358
  33.2 4.3 %collective-permute-start.7 = (f32[136,128]{1,0:T(8,128)S(1)}, f32[136,128]{1,0:T(8,128)S(1)}, u32[]{:S(2)}, u32[]{:S(2)}) collective-permute-start(f32[136,128]{1,0:T(8,128)S(1)} %add_add_fusion.4), channel_id=1, source_target_pairs={{0,32},{8,40},{16,48},{24,56},{32,0},{40,8},{48,16},{56,24},{64,96... | collective-permute-start | bytes 208904 | tf_op jit(solution)/shard_map/ppermute | solution.py:358
  37.5 5.9 %copy-start.1 = (f32[136,128]{1,0:T(8,128)}, f32[136,128]{1,0:T(8,128)S(1)}, u32[]{:S(2)}) copy-start(f32[136,128]{1,0:T(8,128)S(1)} %add_add_fusion.3.mine_ref) | copy-start | bytes 208900
  37.5 5.9 %collective-permute-start.10 = (f32[136,128]{1,0:T(8,128)S(1)}, f32[136,128]{1,0:T(8,128)S(1)}, u32[]{:S(2)}, u32[]{:S(2)}) collective-permute-start(f32[136,128]{1,0:T(8,128)S(1)} %add_add_fusion.3.mine_ref), channel_id=1, source_target_pairs={{0,1},{1,0},{2,3},{3,2},{4,5},{5,4},{6,7},{7,6},{8,9},{9,8},{10,11... | collective-permute-start | bytes 208904 | tf_op jit(solution)/shard_map/ppermute | solution.py:358
  43.5 0.6 copy-start.3
  75.0 1.5 %collective-permute-start.11 = (f32[136,128]{1,0:T(8,128)}, f32[136,128]{1,0:T(8,128)S(1)}, u32[]{:S(2)}, u32[]{:S(2)}) collective-permute-start(f32[136,128]{1,0:T(8,128)} %get-tuple-element.16), channel_id=1, source_target_pairs={{0,1},{1,0},{2,3},{3,2},{4,5},{5,4},{6,7},{7,6},{8,9},{9,8},{10,11... | collective-permute-start | bytes 208904 | tf_op jit(solution)/shard_map/ppermute | solution.py:358
  77.3 4.4 %collective-permute-start.14 = (f32[136,128]{1,0:T(8,128)S(1)}, f32[136,128]{1,0:T(8,128)S(1)}, u32[]{:S(2)}, u32[]{:S(2)}) collective-permute-start(f32[136,128]{1,0:T(8,128)S(1)} %add.70), channel_id=1, source_target_pairs={{0,6},{1,7},{2,4},{3,5},{4,2},{5,3},{6,0},{7,1},{8,14},{9,15},{10,... | collective-permute-start | bytes 208904 | tf_op jit(solution)/shard_map/ppermute | solution.py:358
  78.4 4.8 %collective-permute-start.13 = (f32[136,128]{1,0:T(8,128)S(1)}, f32[136,128]{1,0:T(8,128)S(1)}, u32[]{:S(2)}, u32[]{:S(2)}) collective-permute-start(f32[136,128]{1,0:T(8,128)S(1)} %add.70), channel_id=1, source_target_pairs={{0,4},{1,5},{2,6},{3,7},{4,0},{5,1},{6,2},{7,3},{8,12},{9,13},{10,... | collective-permute-start | bytes 208904 | tf_op jit(solution)/shard_map/ppermute | solution.py:358
  79.3 4.5 %collective-permute-start.12 = (f32[136,128]{1,0:T(8,128)S(1)}, f32[136,128]{1,0:T(8,128)S(1)}, u32[]{:S(2)}, u32[]{:S(2)}) collective-permute-start(f32[136,128]{1,0:T(8,128)S(1)} %add.70), channel_id=1, source_target_pairs={{0,2},{1,3},{2,0},{3,1},{4,6},{5,7},{6,4},{7,5},{8,10},{9,11},{10,... | collective-permute-start | bytes 208904 | tf_op jit(solution)/shard_map/ppermute | solution.py:358
  83.8 4.5 %collective-permute-start.17 = (f32[136,128]{1,0:T(8,128)S(1)}, f32[136,128]{1,0:T(8,128)S(1)}, u32[]{:S(2)}, u32[]{:S(2)}) collective-permute-start(f32[136,128]{1,0:T(8,128)S(1)} %add_add_fusion.2), channel_id=1, source_target_pairs={{0,24},{8,16},{16,8},{24,0},{32,56},{40,48},{48,40},{56,32},{64,88... | collective-permute-start | bytes 208904 | tf_op jit(solution)/shard_map/ppermute | solution.py:358
  84.9 4.7 %collective-permute-start.16 = (f32[136,128]{1,0:T(8,128)S(1)}, f32[136,128]{1,0:T(8,128)S(1)}, u32[]{:S(2)}, u32[]{:S(2)}) collective-permute-start(f32[136,128]{1,0:T(8,128)S(1)} %add_add_fusion.2), channel_id=1, source_target_pairs={{0,16},{8,24},{16,0},{24,8},{32,48},{40,56},{48,32},{56,40},{64,80... | collective-permute-start | bytes 208904 | tf_op jit(solution)/shard_map/ppermute | solution.py:358
  85.7 4.2 %collective-permute-start.15 = (f32[136,128]{1,0:T(8,128)S(1)}, f32[136,128]{1,0:T(8,128)S(1)}, u32[]{:S(2)}, u32[]{:S(2)}) collective-permute-start(f32[136,128]{1,0:T(8,128)S(1)} %add_add_fusion.2), channel_id=1, source_target_pairs={{0,8},{8,0},{16,24},{24,16},{32,40},{40,32},{48,56},{56,48},{64,72... | collective-permute-start | bytes 208904 | tf_op jit(solution)/shard_map/ppermute | solution.py:358
  89.9 4.5 %collective-permute-start.20 = (f32[136,128]{1,0:T(8,128)S(1)}, f32[136,128]{1,0:T(8,128)S(1)}, u32[]{:S(2)}, u32[]{:S(2)}) collective-permute-start(f32[136,128]{1,0:T(8,128)S(1)} %add_add_fusion.1), channel_id=1, source_target_pairs={{0,96},{8,104},{16,112},{24,120},{32,64},{40,72},{48,80},{56,88},{... | collective-permute-start | bytes 208904 | tf_op jit(solution)/shard_map/ppermute | solution.py:358
  91.0 4.7 %collective-permute-start.19 = (f32[136,128]{1,0:T(8,128)S(1)}, f32[136,128]{1,0:T(8,128)S(1)}, u32[]{:S(2)}, u32[]{:S(2)}) collective-permute-start(f32[136,128]{1,0:T(8,128)S(1)} %add_add_fusion.1), channel_id=1, source_target_pairs={{0,64},{8,72},{16,80},{24,88},{32,96},{40,104},{48,112},{56,120},{... | collective-permute-start | bytes 208904 | tf_op jit(solution)/shard_map/ppermute | solution.py:358
  91.8 3.9 %collective-permute-start.18 = (f32[136,128]{1,0:T(8,128)S(1)}, f32[136,128]{1,0:T(8,128)S(1)}, u32[]{:S(2)}, u32[]{:S(2)}) collective-permute-start(f32[136,128]{1,0:T(8,128)S(1)} %add_add_fusion.1), channel_id=1, source_target_pairs={{0,32},{8,40},{16,48},{24,56},{32,0},{40,8},{48,16},{56,24},{64,96... | collective-permute-start | bytes 208904 | tf_op jit(solution)/shard_map/ppermute | solution.py:358
  95.7 5.0 %copy-start = (f32[136,128]{1,0:T(8,128)}, f32[136,128]{1,0:T(8,128)S(1)}, u32[]{:S(2)}) copy-start(f32[136,128]{1,0:T(8,128)S(1)} %add_add_fusion.mine_ref) | copy-start | bytes 208900
  95.7 5.0 %collective-permute-start.21 = (f32[136,128]{1,0:T(8,128)S(1)}, f32[136,128]{1,0:T(8,128)S(1)}, u32[]{:S(2)}, u32[]{:S(2)}) collective-permute-start(f32[136,128]{1,0:T(8,128)S(1)} %add_add_fusion.mine_ref), channel_id=1, source_target_pairs={{0,1},{1,0},{2,3},{3,2},{4,5},{5,4},{6,7},{7,6},{8,9},{9,8},{10,11... | collective-permute-start | bytes 208904 | tf_op jit(solution)/shard_map/ppermute | solution.py:358
  100.8 0.6 copy-start.2
where the time goes:
time: 120 us
  Pallas kernels  59.2 us (49%)
  starting transfers between devices  32.2 us (27%)
  waiting for transfers between devices  24.5 us (20%)
  other arithmetic  1.89 us (2%)
  local copies, waits for them, and re-layouts  1.27 us (1%)
    ppermute x22, starting transfers between devices, swap(): lax.ppermute(value, axis, [(i, i ^ distance) for i in range(lax.axis_size...  32.2 us
    ppermute x22, waiting for transfers between devices, swap(): lax.ppermute(value, axis, [(i, i ^ distance) for i in range(lax.axis_size...  24.5 us
    pallas_call x1, Pallas kernels, first_call(): pl.pallas_call(functools.partial(first_kernel, steps), out_shape=(jax.Sha...  20.5 us
    pallas_call x1, Pallas kernels, basis_call(): pl.pallas_call(functools.partial(basis_kernel, scale), out_shape=jax.Shap...  13.2 us
    pallas_call x1, Pallas kernels, chol_one_call(): pl.pallas_call(chol_one_kernel, out_shape=(jax.ShapeDtypeStruct((5 * K, K...  10.4 us
    pallas_call x1, Pallas kernels, gram_call(): pl.pallas_call(functools.partial(gram_kernel, steps), out_shape=(half, ha...  10 us
    pallas_call x1, Pallas kernels, chol_two_call(): pl.pallas_call(functools.partial(chol_two_kernel, scale), out_shape=(jax....  5.08 us
  transfers between devices with their start and end apart: 22, of which 18 were waited for; matrix products, arithmetic and copies ran while one was open for 0% of the time, Pallas kernels for 0%

commit v1 on v0

--- a/solution.py
+++ b/solution.py
@@ -12,6 +12,10 @@
 F32 = jnp.float32
 BF16 = jnp.bfloat16
 VMEM_WHOLE = pl.BlockSpec(memory_space=pltpu.VMEM)
+
+
+def params(mib):
+    return pltpu.CompilerParams(vmem_limit_bytes=mib << 20)
 
 
 def split2(x):
@@ -118,8 +122,9 @@
         out_shape=(half, half),
         grid=(steps,),
         in_specs=[pl.BlockSpec((rows, K), lambda i: (i, 0))],
-        out_specs=[pl.BlockSpec((HALF, H), lambda i: (0, 0))] * 2,
+        out_specs=[VMEM_WHOLE] * 2,
         scratch_shapes=[pltpu.VMEM((K, 3 * K), F32)],
+        compiler_params=params(58),
         name="gram_one",
     )(x)
 
@@ -133,7 +138,7 @@
 
     h, m, l = split3(x_ref[...])
     first = dot_nn(jnp.concatenate([h, m, l, h, m], axis=1), w_ref[...])
-    first_ref[...] = first
+    first_ref[pl.ds(pl.multiple_of(step * x_ref.shape[0], x_ref.shape[0]), x_ref.shape[0]), :] = first
     fh, fm = split2(first)
     acc[...] += dot_tn(fh, jnp.concatenate([fh, fm], axis=1))
 
@@ -151,14 +156,16 @@
         out_shape=(jax.ShapeDtypeStruct(x.shape, F32), half, half),
         grid=(steps,),
         in_specs=[pl.BlockSpec((rows, K), lambda i: (i, 0)), VMEM_WHOLE],
-        out_specs=[pl.BlockSpec((rows, K), lambda i: (i, 0))] + [pl.BlockSpec((HALF, H), lambda i: (0, 0))] * 2,
+        out_specs=[VMEM_WHOLE] * 3,
         scratch_shapes=[pltpu.VMEM((K, 2 * K), F32)],
+        compiler_params=params(30),
         name="first_and_gram_two",
     )(x, w)
 
 
 def basis_kernel(scale, f_ref, c_ref, out_ref):
-    first = f_ref[...]
+    rows = out_ref.shape[0]
+    first = f_ref[pl.ds(pl.multiple_of(pl.program_id(0) * rows, rows), rows), :]
     h, m = split2(first)
     out_ref[...] = (first + dot_nn(jnp.concatenate([h, m, h], axis=1), c_ref[...])) * scale
 
@@ -168,8 +175,9 @@
         functools.partial(basis_kernel, scale),
         out_shape=jax.ShapeDtypeStruct(first.shape, F32),
         grid=(first.shape[0] // rows,),
-        in_specs=[pl.BlockSpec((rows, K), lambda i: (i, 0)), VMEM_WHOLE],
+        in_specs=[VMEM_WHOLE] * 2,
         out_specs=pl.BlockSpec((rows, K), lambda i: (i, 0)),
+        compiler_params=params(30),
         name="basis",
     )(first, c)
 
@@ -266,6 +274,7 @@
         in_specs=[VMEM_WHOLE] * 2,
         out_specs=[VMEM_WHOLE] * 2,
         scratch_shapes=[pltpu.VMEM((K, 2 * K), F32)],
+        compiler_params=params(16),
         name="factor_one",
     )(mine, other)
 
@@ -350,6 +359,7 @@
         in_specs=[VMEM_WHOLE] * 3,
         out_specs=[VMEM_WHOLE] * 2,
         scratch_shapes=[pltpu.VMEM((K, K), F32)] * 3 + [pltpu.VMEM((K, 2 * K), F32)],
+        compiler_params=params(16),
         name="factor_two",
     )(mine, other, upper)
 

time: 120 us -> 108 us (0.900)
  Pallas kernels: 59.2 us -> 49.7 us
  local copies, waits for them, and re-layouts: 1.27 us -> 0 us
    pallas_call x1, Pallas kernels: 13.2 us -> 8.1 us  [basis_call(): pl.pallas_call(functools.partial(basis_kernel, scale), out_shape=jax.Shap...]
    pallas_call x1, Pallas kernels: 10.4 us -> 8.63 us  [chol_one_call(): pl.pallas_call(chol_one_kernel, out_shape=(jax.ShapeDtypeStruct((5 * K, K...]
    pallas_call x1, Pallas kernels: 20.5 us -> 18.9 us  [first_call(): pl.pallas_call(functools.partial(first_kernel, steps), out_shape=(jax.Sha...]
    unnamed x8 -> x0, local copies, waits for them, and re-layouts: 1.27 us -> none
where the time goes in v1:
time: 108 us
  Pallas kernels  49.7 us (46%)
  starting transfers between devices  32.3 us (30%)
  waiting for transfers between devices  24.2 us (22%)
    ppermute x22, starting transfers between devices, swap(): lax.ppermute(value, axis, [(i, i ^ distance) for i in range(lax.axis_size...  32.3 us
    ppermute x22, waiting for transfers between devices, swap(): lax.ppermute(value, axis, [(i, i ^ distance) for i in range(lax.axis_size...  24.2 us
    pallas_call x1, Pallas kernels, first_call(): pl.pallas_call(functools.partial(first_kernel, steps), out_shape=(jax.Sha...  18.9 us
    pallas_call x1, Pallas kernels, gram_call(): pl.pallas_call(functools.partial(gram_kernel, steps), out_shape=(half, ha...  10 us
    pallas_call x1, Pallas kernels, chol_one_call(): pl.pallas_call(chol_one_kernel, out_shape=(jax.ShapeDtypeStruct((5 * K, K...  8.63 us
    pallas_call x1, Pallas kernels, basis_call(): pl.pallas_call(functools.partial(basis_kernel, scale), out_shape=jax.Shap...  8.1 us
    pallas_call x1, Pallas kernels, chol_two_call(): pl.pallas_call(functools.partial(chol_two_kernel, scale), out_shape=(jax....  3.99 us
  transfers between devices with their start and end apart: 22, of which 18 were waited for; matrix products, arithmetic and copies ran while one was open for 0% of the time, Pallas kernels for 0%

profile of v1, /device:TPU:1, one launch (start us, length us, event | category | flops | bytes accessed | tf_op | source)
XLA Modules:
  0.0 107.9 jit_solution(4249878349372407481)
XLA Ops:
  0.6 10.0 %gram_one.1 = (f32[136,128]{1,0:T(8,128)}, f32[136,128]{1,0:T(8,128)}) custom-call(f32[12288,256]{1,0:T(8,128)} %x_ref.3), custom_call_target="tpu_custom_call" | custom-call | tf_op jit(solution)/shard_map/gram_one/pallas_call | solution.py:120
  10.7 1.4 %collective-permute-start = (f32[136,128]{1,0:T(8,128)}, f32[136,128]{1,0:T(8,128)S(1)}, u32[]{:S(2)}, u32[]{:S(2)}) collective-permute-start(f32[136,128]{1,0:T(8,128)} %get-tuple-element.12), channel_id=1, source_target_pairs={{0,1},{1,0},{2,3},{3,2},{4,5},{5,4},{6,7},{7,6},{8,9},{9,8},{10,11... | collective-permute-start | bytes 208904 | tf_op jit(solution)/shard_map/ppermute | solution.py:368
  12.0 1.1 %collective-permute-done = f32[136,128]{1,0:T(8,128)S(1)} collective-permute-done((f32[136,128]{1,0:T(8,128)}, f32[136,128]{1,0:T(8,128)S(1)}, u32[]{:S(2)}, u32[]{:S(2)}) %collective-permute-start) | collective-permute-done | bytes 69664 | tf_op jit(solution)/shard_map/ppermute | solution.py:368
  13.1 0.9 add.60
  14.0 2.7 %collective-permute-start.3 = (f32[136,128]{1,0:T(8,128)S(1)}, f32[136,128]{1,0:T(8,128)S(1)}, u32[]{:S(2)}, u32[]{:S(2)}) collective-permute-start(f32[136,128]{1,0:T(8,128)S(1)} %add.60), channel_id=1, source_target_pairs={{0,6},{1,7},{2,4},{3,5},{4,2},{5,3},{6,0},{7,1},{8,14},{9,15},{10,... | collective-permute-start | bytes 208904 | tf_op jit(solution)/shard_map/ppermute | solution.py:368
  16.7 0.5 collective-permute-start.2
  17.2 0.2 collective-permute-start.1
  17.4 1.4 %collective-permute-done.3 = f32[136,128]{1,0:T(8,128)S(1)} collective-permute-done((f32[136,128]{1,0:T(8,128)S(1)}, f32[136,128]{1,0:T(8,128)S(1)}, u32[]{:S(2)}, u32[]{:S(2)}) %collective-permute-start.3) | collective-permute-done | bytes 69664 | tf_op jit(solution)/shard_map/ppermute | solution.py:368
  18.8 2.5 %collective-permute-done.2 = f32[136,128]{1,0:T(8,128)S(1)} collective-permute-done((f32[136,128]{1,0:T(8,128)S(1)}, f32[136,128]{1,0:T(8,128)S(1)}, u32[]{:S(2)}, u32[]{:S(2)}) %collective-permute-start.2) | collective-permute-done | bytes 69664 | tf_op jit(solution)/shard_map/ppermute | solution.py:368
  21.4 0.0 collective-permute-done.1
  21.4 3.8 %collective-permute-start.6 = (f32[136,128]{1,0:T(8,128)S(1)}, f32[136,128]{1,0:T(8,128)S(1)}, u32[]{:S(2)}, u32[]{:S(2)}) collective-permute-start(f32[136,128]{1,0:T(8,128)S(1)} %add_add_fusion.5), channel_id=1, source_target_pairs={{0,24},{8,16},{16,8},{24,0},{32,56},{40,48},{48,40},{56,32},{64,88... | collective-permute-start | bytes 208904 | tf_op jit(solution)/shard_map/ppermute | solution.py:368
  25.2 0.0 collective-permute-start.5
  25.2 0.7 collective-permute-start.4
  25.9 1.3 %collective-permute-done.6 = f32[136,128]{1,0:T(8,128)S(1)} collective-permute-done((f32[136,128]{1,0:T(8,128)S(1)}, f32[136,128]{1,0:T(8,128)S(1)}, u32[]{:S(2)}, u32[]{:S(2)}) %collective-permute-start.6) | collective-permute-done | bytes 69664 | tf_op jit(solution)/shard_map/ppermute | solution.py:368
  27.2 2.8 %collective-permute-done.5 = f32[136,128]{1,0:T(8,128)S(1)} collective-permute-done((f32[136,128]{1,0:T(8,128)S(1)}, f32[136,128]{1,0:T(8,128)S(1)}, u32[]{:S(2)}, u32[]{:S(2)}) %collective-permute-start.5) | collective-permute-done | bytes 69664 | tf_op jit(solution)/shard_map/ppermute | solution.py:368
  30.0 2.8 %collective-permute-start.9 = (f32[136,128]{1,0:T(8,128)S(1)}, f32[136,128]{1,0:T(8,128)S(1)}, u32[]{:S(2)}, u32[]{:S(2)}) collective-permute-start(f32[136,128]{1,0:T(8,128)S(1)} %add_add_fusion.4), channel_id=1, source_target_pairs={{0,96},{8,104},{16,112},{24,120},{32,64},{40,72},{48,80},{56,88},{... | collective-permute-start | bytes 208904 | tf_op jit(solution)/shard_map/ppermute | solution.py:368
  32.8 0.3 collective-permute-start.8
  33.2 0.3 collective-permute-start.7
  33.5 1.3 %collective-permute-done.9 = f32[136,128]{1,0:T(8,128)S(1)} collective-permute-done((f32[136,128]{1,0:T(8,128)S(1)}, f32[136,128]{1,0:T(8,128)S(1)}, u32[]{:S(2)}, u32[]{:S(2)}) %collective-permute-start.9) | collective-permute-done | bytes 69664 | tf_op jit(solution)/shard_map/ppermute | solution.py:368
  34.8 2.7 %collective-permute-done.8 = f32[136,128]{1,0:T(8,128)S(1)} collective-permute-done((f32[136,128]{1,0:T(8,128)S(1)}, f32[136,128]{1,0:T(8,128)S(1)}, u32[]{:S(2)}, u32[]{:S(2)}) %collective-permute-start.8) | collective-permute-done | bytes 69664 | tf_op jit(solution)/shard_map/ppermute | solution.py:368
  37.5 5.0 %collective-permute-start.10 = (f32[136,128]{1,0:T(8,128)S(1)}, f32[136,128]{1,0:T(8,128)S(1)}, u32[]{:S(2)}, u32[]{:S(2)}) collective-permute-start(f32[136,128]{1,0:T(8,128)S(1)} %add_add_fusion.3.mine_ref), channel_id=1, source_target_pairs={{0,1},{1,0},{2,3},{3,2},{4,5},{5,4},{6,7},{7,6},{8,9},{9,8},{10,11... | collective-permute-start | bytes 208904 | tf_op jit(solution)/shard_map/ppermute | solution.py:368
  42.5 0.9 collective-permute-done.10.other_ref
  43.5 8.6 %factor_one.1 = (bf16[1280,256]{1,0:T(8,128)(2,1)S(1)}, f32[256,256]{1,0:T(8,128)S(1)}) custom-call(f32[136,128]{1,0:T(8,128)S(1)} %add_add_fusion.3.mine_ref, f32[136,128]{1,0:T(8,128)S(1)} %collective-permute-done.10.other_ref), custom_call_target="tpu_custom_call" | custom-call | tf_op jit(solution)/shard_map/factor_one/pallas_call | solution.py:271
  52.1 18.9 %first_and_gram_two.1 = (f32[12288,256]{1,0:T(8,128)S(1)}, f32[136,128]{1,0:T(8,128)S(1)}, f32[136,128]{1,0:T(8,128)S(1)}) custom-call(f32[12288,256]{1,0:T(8,128)} %x_ref.3, bf16[1280,256]{1,0:T(8,128)(2,1)S(1)} %get-tuple-element.13.w_ref), custom_call_target="tpu_custom_call" | custom-call | tf_op jit(solution)/shard_map/first_and_gram_two/pallas_call | solution.py:154
  71.0 0.4 collective-permute-start.11
  71.5 0.9 collective-permute-done.11
  72.4 1.1 %collective-permute-start.14 = (f32[136,128]{1,0:T(8,128)S(1)}, f32[136,128]{1,0:T(8,128)S(1)}, u32[]{:S(2)}, u32[]{:S(2)}) collective-permute-start(f32[136,128]{1,0:T(8,128)S(1)} %add.70), channel_id=1, source_target_pairs={{0,6},{1,7},{2,4},{3,5},{4,2},{5,3},{6,0},{7,1},{8,14},{9,15},{10,... | collective-permute-start | bytes 208904 | tf_op jit(solution)/shard_map/ppermute | solution.py:368
  73.5 0.9 collective-permute-start.13
  74.4 1.4 %collective-permute-start.12 = (f32[136,128]{1,0:T(8,128)S(1)}, f32[136,128]{1,0:T(8,128)S(1)}, u32[]{:S(2)}, u32[]{:S(2)}) collective-permute-start(f32[136,128]{1,0:T(8,128)S(1)} %add.70), channel_id=1, source_target_pairs={{0,2},{1,3},{2,0},{3,1},{4,6},{5,7},{6,4},{7,5},{8,10},{9,11},{10,... | collective-permute-start | bytes 208904 | tf_op jit(solution)/shard_map/ppermute | solution.py:368
  75.7 1.1 %collective-permute-done.14 = f32[136,128]{1,0:T(8,128)S(1)} collective-permute-done((f32[136,128]{1,0:T(8,128)S(1)}, f32[136,128]{1,0:T(8,128)S(1)}, u32[]{:S(2)}, u32[]{:S(2)}) %collective-permute-start.14) | collective-permute-done | bytes 69664 | tf_op jit(solution)/shard_map/ppermute | solution.py:368
  76.8 1.4 %collective-permute-done.13 = f32[136,128]{1,0:T(8,128)S(1)} collective-permute-done((f32[136,128]{1,0:T(8,128)S(1)}, f32[136,128]{1,0:T(8,128)S(1)}, u32[]{:S(2)}, u32[]{:S(2)}) %collective-permute-start.13) | collective-permute-done | bytes 69664 | tf_op jit(solution)/shard_map/ppermute | solution.py:368
  78.3 0.6 collective-permute-done.12
  78.9 1.1 %collective-permute-start.17 = (f32[136,128]{1,0:T(8,128)S(1)}, f32[136,128]{1,0:T(8,128)S(1)}, u32[]{:S(2)}, u32[]{:S(2)}) collective-permute-start(f32[136,128]{1,0:T(8,128)S(1)} %add_add_fusion.2), channel_id=1, source_target_pairs={{0,24},{8,16},{16,8},{24,0},{32,56},{40,48},{48,40},{56,32},{64,88... | collective-permute-start | bytes 208904 | tf_op jit(solution)/shard_map/ppermute | solution.py:368
  80.0 0.8 collective-permute-start.16
  80.8 1.4 %collective-permute-start.15 = (f32[136,128]{1,0:T(8,128)S(1)}, f32[136,128]{1,0:T(8,128)S(1)}, u32[]{:S(2)}, u32[]{:S(2)}) collective-permute-start(f32[136,128]{1,0:T(8,128)S(1)} %add_add_fusion.2), channel_id=1, source_target_pairs={{0,8},{8,0},{16,24},{24,16},{32,40},{40,32},{48,56},{56,48},{64,72... | collective-permute-start | bytes 208904 | tf_op jit(solution)/shard_map/ppermute | solution.py:368
  82.2 1.1 %collective-permute-done.17 = f32[136,128]{1,0:T(8,128)S(1)} collective-permute-done((f32[136,128]{1,0:T(8,128)S(1)}, f32[136,128]{1,0:T(8,128)S(1)}, u32[]{:S(2)}, u32[]{:S(2)}) %collective-permute-start.17) | collective-permute-done | bytes 69664 | tf_op jit(solution)/shard_map/ppermute | solution.py:368
  83.3 1.3 %collective-permute-done.16 = f32[136,128]{1,0:T(8,128)S(1)} collective-permute-done((f32[136,128]{1,0:T(8,128)S(1)}, f32[136,128]{1,0:T(8,128)S(1)}, u32[]{:S(2)}, u32[]{:S(2)}) %collective-permute-start.16) | collective-permute-done | bytes 69664 | tf_op jit(solution)/shard_map/ppermute | solution.py:368
  84.7 0.3 collective-permute-done.15
  85.0 1.1 %collective-permute-start.20 = (f32[136,128]{1,0:T(8,128)S(1)}, f32[136,128]{1,0:T(8,128)S(1)}, u32[]{:S(2)}, u32[]{:S(2)}) collective-permute-start(f32[136,128]{1,0:T(8,128)S(1)} %add_add_fusion.1), channel_id=1, source_target_pairs={{0,96},{8,104},{16,112},{24,120},{32,64},{40,72},{48,80},{56,88},{... | collective-permute-start | bytes 208904 | tf_op jit(solution)/shard_map/ppermute | solution.py:368
  86.1 0.8 collective-permute-start.19
  86.9 1.4 %collective-permute-start.18 = (f32[136,128]{1,0:T(8,128)S(1)}, f32[136,128]{1,0:T(8,128)S(1)}, u32[]{:S(2)}, u32[]{:S(2)}) collective-permute-start(f32[136,128]{1,0:T(8,128)S(1)} %add_add_fusion.1), channel_id=1, source_target_pairs={{0,32},{8,40},{16,48},{24,56},{32,0},{40,8},{48,16},{56,24},{64,96... | collective-permute-start | bytes 208904 | tf_op jit(solution)/shard_map/ppermute | solution.py:368
  88.3 1.1 %collective-permute-done.20 = f32[136,128]{1,0:T(8,128)S(1)} collective-permute-done((f32[136,128]{1,0:T(8,128)S(1)}, f32[136,128]{1,0:T(8,128)S(1)}, u32[]{:S(2)}, u32[]{:S(2)}) %collective-permute-start.20) | collective-permute-done | bytes 69664 | tf_op jit(solution)/shard_map/ppermute | solution.py:368
  89.4 1.3 %collective-permute-done.19 = f32[136,128]{1,0:T(8,128)S(1)} collective-permute-done((f32[136,128]{1,0:T(8,128)S(1)}, f32[136,128]{1,0:T(8,128)S(1)}, u32[]{:S(2)}, u32[]{:S(2)}) %collective-permute-start.19) | collective-permute-done | bytes 69664 | tf_op jit(solution)/shard_map/ppermute | solution.py:368
  90.7 0.0 collective-permute-done.18
  90.8 4.1 %collective-permute-start.21 = (f32[136,128]{1,0:T(8,128)S(1)}, f32[136,128]{1,0:T(8,128)S(1)}, u32[]{:S(2)}, u32[]{:S(2)}) collective-permute-start(f32[136,128]{1,0:T(8,128)S(1)} %add_add_fusion.mine_ref), channel_id=1, source_target_pairs={{0,1},{1,0},{2,3},{3,2},{4,5},{5,4},{6,7},{7,6},{8,9},{9,8},{10,11... | collective-permute-start | bytes 208904 | tf_op jit(solution)/shard_map/ppermute | solution.py:368
  94.9 0.9 collective-permute-done.21.other_ref
  95.8 4.0 %factor_two.1 = (bf16[768,256]{1,0:T(8,128)(2,1)S(1)}, f32[256,256]{1,0:T(8,128)}) custom-call(f32[136,128]{1,0:T(8,128)S(1)} %add_add_fusion.mine_ref, f32[136,128]{1,0:T(8,128)S(1)} %collective-permute-done.21.other_ref, f32[256,256]{1,0:T(8,128)S(1)} %get-tuple-element.17.upper_ref), custom_call_target="tpu_custom_call" | custom-call | tf_op jit(solution)/shard_map/factor_two/pallas_call | solution.py:356
  99.8 8.1 %basis.1 = f32[12288,256]{1,0:T(8,128)} custom-call(f32[12288,256]{1,0:T(8,128)S(1)} %get-tuple-element.14.f_ref, bf16[768,256]{1,0:T(8,128)(2,1)S(1)} %get-tuple-element.18.c_ref), custom_call_target="tpu_custom_call" | custom-call | tf_op jit(solution)/shard_map/basis/pallas_call | solution.py:174
  (9 shorter events, 0.1 us)
Async XLA Ops:
  10.7 2.5 %collective-permute-start = (f32[136,128]{1,0:T(8,128)}, f32[136,128]{1,0:T(8,128)S(1)}, u32[]{:S(2)}, u32[]{:S(2)}) collective-permute-start(f32[136,128]{1,0:T(8,128)} %get-tuple-element.12), channel_id=1, source_target_pairs={{0,1},{1,0},{2,3},{3,2},{4,5},{5,4},{6,7},{7,6},{8,9},{9,8},{10,11... | collective-permute-start | bytes 208904 | tf_op jit(solution)/shard_map/ppermute | solution.py:368
  14.0 4.8 %collective-permute-start.3 = (f32[136,128]{1,0:T(8,128)S(1)}, f32[136,128]{1,0:T(8,128)S(1)}, u32[]{:S(2)}, u32[]{:S(2)}) collective-permute-start(f32[136,128]{1,0:T(8,128)S(1)} %add.60), channel_id=1, source_target_pairs={{0,6},{1,7},{2,4},{3,5},{4,2},{5,3},{6,0},{7,1},{8,14},{9,15},{10,... | collective-permute-start | bytes 208904 | tf_op jit(solution)/shard_map/ppermute | solution.py:368
  16.7 4.7 %collective-permute-start.2 = (f32[136,128]{1,0:T(8,128)S(1)}, f32[136,128]{1,0:T(8,128)S(1)}, u32[]{:S(2)}, u32[]{:S(2)}) collective-permute-start(f32[136,128]{1,0:T(8,128)S(1)} %add.60), channel_id=1, source_target_pairs={{0,4},{1,5},{2,6},{3,7},{4,0},{5,1},{6,2},{7,3},{8,12},{9,13},{10,... | collective-permute-start | bytes 208904 | tf_op jit(solution)/shard_map/ppermute | solution.py:368
  17.2 4.1 %collective-permute-start.1 = (f32[136,128]{1,0:T(8,128)S(1)}, f32[136,128]{1,0:T(8,128)S(1)}, u32[]{:S(2)}, u32[]{:S(2)}) collective-permute-start(f32[136,128]{1,0:T(8,128)S(1)} %add.60), channel_id=1, source_target_pairs={{0,2},{1,3},{2,0},{3,1},{4,6},{5,7},{6,4},{7,5},{8,10},{9,11},{10,... | collective-permute-start | bytes 208904 | tf_op jit(solution)/shard_map/ppermute | solution.py:368
  21.4 5.8 %collective-permute-start.6 = (f32[136,128]{1,0:T(8,128)S(1)}, f32[136,128]{1,0:T(8,128)S(1)}, u32[]{:S(2)}, u32[]{:S(2)}) collective-permute-start(f32[136,128]{1,0:T(8,128)S(1)} %add_add_fusion.5), channel_id=1, source_target_pairs={{0,24},{8,16},{16,8},{24,0},{32,56},{40,48},{48,40},{56,32},{64,88... | collective-permute-start | bytes 208904 | tf_op jit(solution)/shard_map/ppermute | solution.py:368
  25.2 4.8 %collective-permute-start.5 = (f32[136,128]{1,0:T(8,128)S(1)}, f32[136,128]{1,0:T(8,128)S(1)}, u32[]{:S(2)}, u32[]{:S(2)}) collective-permute-start(f32[136,128]{1,0:T(8,128)S(1)} %add_add_fusion.5), channel_id=1, source_target_pairs={{0,16},{8,24},{16,0},{24,8},{32,48},{40,56},{48,32},{56,40},{64,80... | collective-permute-start | bytes 208904 | tf_op jit(solution)/shard_map/ppermute | solution.py:368
  25.2 4.8 %collective-permute-start.4 = (f32[136,128]{1,0:T(8,128)S(1)}, f32[136,128]{1,0:T(8,128)S(1)}, u32[]{:S(2)}, u32[]{:S(2)}) collective-permute-start(f32[136,128]{1,0:T(8,128)S(1)} %add_add_fusion.5), channel_id=1, source_target_pairs={{0,8},{8,0},{16,24},{24,16},{32,40},{40,32},{48,56},{56,48},{64,72... | collective-permute-start | bytes 208904 | tf_op jit(solution)/shard_map/ppermute | solution.py:368
  30.0 4.8 %collective-permute-start.9 = (f32[136,128]{1,0:T(8,128)S(1)}, f32[136,128]{1,0:T(8,128)S(1)}, u32[]{:S(2)}, u32[]{:S(2)}) collective-permute-start(f32[136,128]{1,0:T(8,128)S(1)} %add_add_fusion.4), channel_id=1, source_target_pairs={{0,96},{8,104},{16,112},{24,120},{32,64},{40,72},{48,80},{56,88},{... | collective-permute-start | bytes 208904 | tf_op jit(solution)/shard_map/ppermute | solution.py:368
  32.8 4.7 %collective-permute-start.8 = (f32[136,128]{1,0:T(8,128)S(1)}, f32[136,128]{1,0:T(8,128)S(1)}, u32[]{:S(2)}, u32[]{:S(2)}) collective-permute-start(f32[136,128]{1,0:T(8,128)S(1)} %add_add_fusion.4), channel_id=1, source_target_pairs={{0,64},{8,72},{16,80},{24,88},{32,96},{40,104},{48,112},{56,120},{... | collective-permute-start | bytes 208904 | tf_op jit(solution)/shard_map/ppermute | solution.py:368
  33.2 4.3 %collective-permute-start.7 = (f32[136,128]{1,0:T(8,128)S(1)}, f32[136,128]{1,0:T(8,128)S(1)}, u32[]{:S(2)}, u32[]{:S(2)}) collective-permute-start(f32[136,128]{1,0:T(8,128)S(1)} %add_add_fusion.4), channel_id=1, source_target_pairs={{0,32},{8,40},{16,48},{24,56},{32,0},{40,8},{48,16},{56,24},{64,96... | collective-permute-start | bytes 208904 | tf_op jit(solution)/shard_map/ppermute | solution.py:368
  37.5 5.9 %collective-permute-start.10 = (f32[136,128]{1,0:T(8,128)S(1)}, f32[136,128]{1,0:T(8,128)S(1)}, u32[]{:S(2)}, u32[]{:S(2)}) collective-permute-start(f32[136,128]{1,0:T(8,128)S(1)} %add_add_fusion.3.mine_ref), channel_id=1, source_target_pairs={{0,1},{1,0},{2,3},{3,2},{4,5},{5,4},{6,7},{7,6},{8,9},{9,8},{10,11... | collective-permute-start | bytes 208904 | tf_op jit(solution)/shard_map/ppermute | solution.py:368
  71.0 1.3 %collective-permute-start.11 = (f32[136,128]{1,0:T(8,128)S(1)}, f32[136,128]{1,0:T(8,128)S(1)}, u32[]{:S(2)}, u32[]{:S(2)}) collective-permute-start(f32[136,128]{1,0:T(8,128)S(1)} %get-tuple-element.16), channel_id=1, source_target_pairs={{0,1},{1,0},{2,3},{3,2},{4,5},{5,4},{6,7},{7,6},{8,9},{9,8},{10,11... | collective-permute-start | bytes 208904 | tf_op jit(solution)/shard_map/ppermute | solution.py:368
  72.4 4.5 %collective-permute-start.14 = (f32[136,128]{1,0:T(8,128)S(1)}, f32[136,128]{1,0:T(8,128)S(1)}, u32[]{:S(2)}, u32[]{:S(2)}) collective-permute-start(f32[136,128]{1,0:T(8,128)S(1)} %add.70), channel_id=1, source_target_pairs={{0,6},{1,7},{2,4},{3,5},{4,2},{5,3},{6,0},{7,1},{8,14},{9,15},{10,... | collective-permute-start | bytes 208904 | tf_op jit(solution)/shard_map/ppermute | solution.py:368
  73.5 4.8 %collective-permute-start.13 = (f32[136,128]{1,0:T(8,128)S(1)}, f32[136,128]{1,0:T(8,128)S(1)}, u32[]{:S(2)}, u32[]{:S(2)}) collective-permute-start(f32[136,128]{1,0:T(8,128)S(1)} %add.70), channel_id=1, source_target_pairs={{0,4},{1,5},{2,6},{3,7},{4,0},{5,1},{6,2},{7,3},{8,12},{9,13},{10,... | collective-permute-start | bytes 208904 | tf_op jit(solution)/shard_map/ppermute | solution.py:368
  74.4 4.5 %collective-permute-start.12 = (f32[136,128]{1,0:T(8,128)S(1)}, f32[136,128]{1,0:T(8,128)S(1)}, u32[]{:S(2)}, u32[]{:S(2)}) collective-permute-start(f32[136,128]{1,0:T(8,128)S(1)} %add.70), channel_id=1, source_target_pairs={{0,2},{1,3},{2,0},{3,1},{4,6},{5,7},{6,4},{7,5},{8,10},{9,11},{10,... | collective-permute-start | bytes 208904 | tf_op jit(solution)/shard_map/ppermute | solution.py:368
  78.9 4.5 %collective-permute-start.17 = (f32[136,128]{1,0:T(8,128)S(1)}, f32[136,128]{1,0:T(8,128)S(1)}, u32[]{:S(2)}, u32[]{:S(2)}) collective-permute-start(f32[136,128]{1,0:T(8,128)S(1)} %add_add_fusion.2), channel_id=1, source_target_pairs={{0,24},{8,16},{16,8},{24,0},{32,56},{40,48},{48,40},{56,32},{64,88... | collective-permute-start | bytes 208904 | tf_op jit(solution)/shard_map/ppermute | solution.py:368
  80.0 4.7 %collective-permute-start.16 = (f32[136,128]{1,0:T(8,128)S(1)}, f32[136,128]{1,0:T(8,128)S(1)}, u32[]{:S(2)}, u32[]{:S(2)}) collective-permute-start(f32[136,128]{1,0:T(8,128)S(1)} %add_add_fusion.2), channel_id=1, source_target_pairs={{0,16},{8,24},{16,0},{24,8},{32,48},{40,56},{48,32},{56,40},{64,80... | collective-permute-start | bytes 208904 | tf_op jit(solution)/shard_map/ppermute | solution.py:368
  80.8 4.2 %collective-permute-start.15 = (f32[136,128]{1,0:T(8,128)S(1)}, f32[136,128]{1,0:T(8,128)S(1)}, u32[]{:S(2)}, u32[]{:S(2)}) collective-permute-start(f32[136,128]{1,0:T(8,128)S(1)} %add_add_fusion.2), channel_id=1, source_target_pairs={{0,8},{8,0},{16,24},{24,16},{32,40},{40,32},{48,56},{56,48},{64,72... | collective-permute-start | bytes 208904 | tf_op jit(solution)/shard_map/ppermute | solution.py:368
  85.0 4.5 %collective-permute-start.20 = (f32[136,128]{1,0:T(8,128)S(1)}, f32[136,128]{1,0:T(8,128)S(1)}, u32[]{:S(2)}, u32[]{:S(2)}) collective-permute-start(f32[136,128]{1,0:T(8,128)S(1)} %add_add_fusion.1), channel_id=1, source_target_pairs={{0,96},{8,104},{16,112},{24,120},{32,64},{40,72},{48,80},{56,88},{... | collective-permute-start | bytes 208904 | tf_op jit(solution)/shard_map/ppermute | solution.py:368
  86.1 4.7 %collective-permute-start.19 = (f32[136,128]{1,0:T(8,128)S(1)}, f32[136,128]{1,0:T(8,128)S(1)}, u32[]{:S(2)}, u32[]{:S(2)}) collective-permute-start(f32[136,128]{1,0:T(8,128)S(1)} %add_add_fusion.1), channel_id=1, source_target_pairs={{0,64},{8,72},{16,80},{24,88},{32,96},{40,104},{48,112},{56,120},{... | collective-permute-start | bytes 208904 | tf_op jit(solution)/shard_map/ppermute | solution.py:368
  86.9 3.9 %collective-permute-start.18 = (f32[136,128]{1,0:T(8,128)S(1)}, f32[136,128]{1,0:T(8,128)S(1)}, u32[]{:S(2)}, u32[]{:S(2)}) collective-permute-start(f32[136,128]{1,0:T(8,128)S(1)} %add_add_fusion.1), channel_id=1, source_target_pairs={{0,32},{8,40},{16,48},{24,56},{32,0},{40,8},{48,16},{56,24},{64,96... | collective-permute-start | bytes 208904 | tf_op jit(solution)/shard_map/ppermute | solution.py:368
  90.8 5.0 %collective-permute-start.21 = (f32[136,128]{1,0:T(8,128)S(1)}, f32[136,128]{1,0:T(8,128)S(1)}, u32[]{:S(2)}, u32[]{:S(2)}) collective-permute-start(f32[136,128]{1,0:T(8,128)S(1)} %add_add_fusion.mine_ref), channel_id=1, source_target_pairs={{0,1},{1,0},{2,3},{3,2},{4,5},{5,4},{6,7},{7,6},{8,9},{9,8},{10,11... | collective-permute-start | bytes 208904 | tf_op jit(solution)/shard_map/ppermute | solution.py:368

commit v2 on v1

--- a/solution.py
+++ b/solution.py
@@ -97,89 +97,123 @@
         get(other_ref, mine_ref)
 
 
-def gram_kernel(steps, x_ref, keep_ref, send_ref, acc):
-    step = pl.program_id(0)
-
-    @pl.when(step == 0)
-    def _():
-        acc[...] = jnp.zeros_like(acc)
-
-    h, m = split2(x_ref[...])
-    acc[:, :2 * K] += dot_tn(h, jnp.concatenate([h, m], axis=1))
-    acc[:, 2 * K:] += dot_tn(m, m)
-
-    @pl.when(step == steps - 1)
-    def _():
-        cross = acc[:, K:2 * K]
-        pack(acc[:, :K] + (cross + cross.T) + acc[:, 2 * K:], keep_ref, send_ref)
+def gram_kernel(rows, x_hbm, keep_ref, send_ref, x_ref, acc, sems):
+    steps = x_hbm.shape[0] // rows
+
+    def part(step):
+        return pl.ds(pl.multiple_of(step * rows, rows), rows)
+
+    def copy(step):
+        return pltpu.make_async_copy(x_hbm.at[part(step)], x_ref.at[part(step)], sems.at[step])
+
+    for step in range(steps):
+        copy(step).start()
+    acc[...] = jnp.zeros_like(acc)
+
+    def body(step, carry):
+        copy(step).wait()
+        h, m = split2(x_ref[part(step), :])
+        acc[:, : 2 * K] += dot_tn(h, jnp.concatenate([h, m], axis=1))
+        acc[:, 2 * K :] += dot_tn(m, m)
+        return carry
+
+    lax.fori_loop(0, steps, body, 0)
+    cross = acc[:, K : 2 * K]
+    pack(acc[:, :K] + (cross + cross.T) + acc[:, 2 * K :], keep_ref, send_ref)
 
 
 def gram_call(x, rows):
-    steps = x.shape[0] // rows
     half = jax.ShapeDtypeStruct((HALF, H), F32)
     return pl.pallas_call(
-        functools.partial(gram_kernel, steps),
+        functools.partial(gram_kernel, rows),
         out_shape=(half, half),
-        grid=(steps,),
-        in_specs=[pl.BlockSpec((rows, K), lambda i: (i, 0))],
+        in_specs=[pl.BlockSpec(memory_space=pltpu.HBM)],
         out_specs=[VMEM_WHOLE] * 2,
-        scratch_shapes=[pltpu.VMEM((K, 3 * K), F32)],
-        compiler_params=params(58),
+        scratch_shapes=[
+            pltpu.VMEM(x.shape, F32),
+            pltpu.VMEM((K, 3 * K), F32),
+            pltpu.SemaphoreType.DMA((x.shape[0] // rows,)),
+        ],
+        compiler_params=params(52),
         name="gram_one",
     )(x)
 
 
-def first_kernel(steps, x_ref, w_ref, first_ref, keep_ref, send_ref, acc):
-    step = pl.program_id(0)
-
-    @pl.when(step == 0)
-    def _():
-        acc[...] = jnp.zeros_like(acc)
-
-    h, m, l = split3(x_ref[...])
-    first = dot_nn(jnp.concatenate([h, m, l, h, m], axis=1), w_ref[...])
-    first_ref[pl.ds(pl.multiple_of(step * x_ref.shape[0], x_ref.shape[0]), x_ref.shape[0]), :] = first
-    fh, fm = split2(first)
-    acc[...] += dot_tn(fh, jnp.concatenate([fh, fm], axis=1))
-
-    @pl.when(step == steps - 1)
-    def _():
-        cross = acc[:, K:]
-        pack(acc[:, :K] + (cross + cross.T), keep_ref, send_ref)
+def first_kernel(rows, x_hbm, w_ref, first_ref, keep_ref, send_ref, x_ref, acc, sems):
+    steps = x_hbm.shape[0] // rows
+
+    def copy(step):
+        part = pl.ds(pl.multiple_of(step * rows, rows), rows)
+        return pltpu.make_async_copy(x_hbm.at[part], x_ref.at[part], sems.at[step])
+
+    for step in range(steps):
+        copy(step).start()
+    acc[...] = jnp.zeros_like(acc)
+
+    def body(step, carry):
+        copy(step).wait()
+        total = None
+        for n in range(2):
+            part = pl.ds(pl.multiple_of(step * rows + n * (rows // 2), rows // 2), rows // 2)
+            h, m, l = split3(x_ref[part, :])
+            upper = jnp.concatenate([h[:, :H], m[:, :H], h[:, :H], m[:, :H], l], axis=1)
+            lower = jnp.concatenate([h[:, H:], m[:, H:]], axis=1)
+            first = dot_nn(upper, w_ref[: 3 * K, :])
+            more = dot_nn(lower, w_ref[3 * K :, :])
+            first = jnp.concatenate([first[:, :H], first[:, H:] + (more[:, :H] + more[:, H:])], axis=1)
+            first_ref[part, :] = first
+            fh, fm = split2(first)
+            gram = dot_tn(fh, jnp.concatenate([fh, fm], axis=1))
+            total = gram if total is None else total + gram
+        acc[...] += total
+        return carry
+
+    lax.fori_loop(0, steps, body, 0)
+    cross = acc[:, K:]
+    pack(acc[:, :K] + (cross + cross.T), keep_ref, send_ref)
 
 
 def first_call(x, w, rows):
-    steps = x.shape[0] // rows
     half = jax.ShapeDtypeStruct((HALF, H), F32)
     return pl.pallas_call(
-        functools.partial(first_kernel, steps),
+        functools.partial(first_kernel, rows),
         out_shape=(jax.ShapeDtypeStruct(x.shape, F32), half, half),
-        grid=(steps,),
-        in_specs=[pl.BlockSpec((rows, K), lambda i: (i, 0)), VMEM_WHOLE],
+        in_specs=[pl.BlockSpec(memory_space=pltpu.HBM), VMEM_WHOLE],
         out_specs=[VMEM_WHOLE] * 3,
-        scratch_shapes=[pltpu.VMEM((K, 2 * K), F32)],
-        compiler_params=params(30),
+        scratch_shapes=[
+            pltpu.VMEM(x.shape, F32),
+            pltpu.VMEM((K, 2 * K), F32),
+            pltpu.SemaphoreType.DMA((x.shape[0] // rows,)),
+        ],
+        compiler_params=params(36),
         name="first_and_gram_two",
     )(x, w)
 
 
-def basis_kernel(scale, f_ref, c_ref, out_ref):
+def basis_kernel(scale, small_ref, f_ref, c_ref, out_ref):
     rows = out_ref.shape[0]
     first = f_ref[pl.ds(pl.multiple_of(pl.program_id(0) * rows, rows), rows), :]
-    h, m = split2(first)
-    out_ref[...] = (first + dot_nn(jnp.concatenate([h, m, h], axis=1), c_ref[...])) * scale
-
-
-def basis_call(first, c, rows, scale):
+
+    @pl.when(small_ref[0] == 1)
+    def _():
+        out_ref[...] = (first + dot_nn(first.astype(BF16), c_ref[:K, :])) * scale
+
+    @pl.when(small_ref[0] == 0)
+    def _():
+        h, m = split2(first)
+        out_ref[...] = (first + dot_nn(jnp.concatenate([h, m, h], axis=1), c_ref[...])) * scale
+
+
+def basis_call(small, first, c, rows, scale):
     return pl.pallas_call(
         functools.partial(basis_kernel, scale),
         out_shape=jax.ShapeDtypeStruct(first.shape, F32),
         grid=(first.shape[0] // rows,),
-        in_specs=[VMEM_WHOLE] * 2,
+        in_specs=[pl.BlockSpec(memory_space=pltpu.SMEM)] + [VMEM_WHOLE] * 2,
         out_specs=pl.BlockSpec((rows, K), lambda i: (i, 0)),
         compiler_params=params(30),
         name="basis",
-    )(first, c)
+    )(small, first, c)
 
 
 B = 32
@@ -247,30 +281,24 @@
     lax.fori_loop(0, K // B, block, 0)
 
 
-def load_augmented(mine_ref, other_ref, t_ref):
+def chol_one_kernel(mine_ref, other_ref, w_ref, upper_ref, t_ref):
     unpack(mine_ref, other_ref, t_ref.at[:, 0:K])
     i, j = iotas((K, K))
     t_ref[:, K:] = jnp.where(i == j, 1.0, 0.0)
-
-
-def chol_one_kernel(mine_ref, other_ref, w_ref, upper_ref, t_ref):
-    load_augmented(mine_ref, other_ref, t_ref)
     factorize(t_ref)
-    i, j = iotas((K, K))
     upper_ref[...] = jnp.where(i <= j, t_ref[:, :K], 0.0)
-    wt = jnp.where(i >= j, t_ref[:, K:], 0.0).T
-    h, m = split2(wt)
-    w_ref[0:K, :] = h
-    w_ref[K:2 * K, :] = h
-    w_ref[2 * K:3 * K, :] = h
-    w_ref[3 * K:4 * K, :] = m
-    w_ref[4 * K:5 * K, :] = m
+    h, m = split2(jnp.where(i >= j, t_ref[:, K:], 0.0).T)
+    for n in range(2):
+        w_ref[n * H : (n + 1) * H, :] = h[:H]
+        w_ref[(2 + n) * H : (3 + n) * H, :] = m[:H]
+        w_ref[(6 + n) * H : (7 + n) * H, :] = jnp.concatenate([h[H:, H:], m[H:, H:]], axis=1)
+    w_ref[2 * K : 3 * K, :] = h
 
 
 def chol_one_call(mine, other):
     return pl.pallas_call(
         chol_one_kernel,
-        out_shape=(jax.ShapeDtypeStruct((5 * K, K), BF16), jax.ShapeDtypeStruct((K, K), F32)),
+        out_shape=(jax.ShapeDtypeStruct((4 * K, K), BF16), jax.ShapeDtypeStruct((K, K), F32)),
         in_specs=[VMEM_WHOLE] * 2,
         out_specs=[VMEM_WHOLE] * 2,
         scratch_shapes=[pltpu.VMEM((K, 2 * K), F32)],
@@ -280,13 +308,14 @@
 
 
 TOL = 1e-7
+SMALL = 4e-3
 
 
 def largest(x):
     return jnp.max(jnp.abs(x))
 
 
-def chol_two_kernel(scale, mine_ref, other_ref, upper_ref, c_ref, factor_ref, g_ref, x_ref, z_ref, t_ref):
+def chol_two_kernel(scale, mine_ref, other_ref, upper_ref, small_ref, c_ref, factor_ref, g_ref, x_ref, z_ref, t_ref):
     unpack(mine_ref, other_ref, g_ref)
     i, j = iotas((K, K))
     eye = jnp.where(i == j, 1.0, 0.0)
@@ -341,7 +370,9 @@
         x_ref[...] = jnp.where(i <= j, t_ref[:, :K], 0.0).T - eye
         z_ref[...] = jnp.where(i >= j, t_ref[:, K:], 0.0) - eye
 
-    ch, cm = split2(z_ref[...].T)
+    z = z_ref[...]
+    small_ref[0] = (jnp.sum(z * z) <= SMALL * SMALL * K).astype(jnp.int32)
+    ch, cm = split2(z.T)
     c_ref[0:K, :] = ch
     c_ref[K:2 * K, :] = ch
     c_ref[2 * K:3 * K, :] = cm
@@ -355,9 +386,13 @@
 def chol_two_call(mine, other, upper, scale):
     return pl.pallas_call(
         functools.partial(chol_two_kernel, scale),
-        out_shape=(jax.ShapeDtypeStruct((3 * K, K), BF16), jax.ShapeDtypeStruct((K, K), F32)),
+        out_shape=(
+            jax.ShapeDtypeStruct((1,), jnp.int32),
+            jax.ShapeDtypeStruct((3 * K, K), BF16),
+            jax.ShapeDtypeStruct((K, K), F32),
+        ),
         in_specs=[VMEM_WHOLE] * 3,
-        out_specs=[VMEM_WHOLE] * 2,
+        out_specs=[pl.BlockSpec(memory_space=pltpu.SMEM)] + [VMEM_WHOLE] * 2,
         scratch_shapes=[pltpu.VMEM((K, K), F32)] * 3 + [pltpu.VMEM((K, 2 * K), F32)],
         compiler_params=params(16),
         name="factor_two",
@@ -382,17 +417,17 @@
 
 
 ROWS_PER_STEP = 2048
+FIRST_ROWS_PER_STEP = 3072
 
 
 def shards(panel):
     total_rows = panel.shape[0] * lax.axis_size("row") * lax.axis_size("col")
     scale = float(total_rows) ** 0.5
-    mine, other = reduce_gram(*gram_call(panel, ROWS_PER_STEP))
-    w, upper = chol_one_call(mine, other)
-    first, keep, send = first_call(panel, w, ROWS_PER_STEP)
-    mine, other = reduce_gram(keep, send)
-    c, factor = chol_two_call(mine, other, upper, scale)
-    return basis_call(first, c, ROWS_PER_STEP, scale), factor
+    keep, send = gram_call(panel, ROWS_PER_STEP)
+    w, upper = chol_one_call(*reduce_gram(keep, send))
+    first, keep, send = first_call(panel, w, FIRST_ROWS_PER_STEP)
+    small, c, factor = chol_two_call(*reduce_gram(keep, send), upper, scale)
+    return basis_call(small, first, c, ROWS_PER_STEP, scale), factor
 
 
 def solution(mesh):

time: 108 us -> 97.8 us (0.906)
  Pallas kernels: 49.7 us -> 40.4 us
    pallas_call x3, Pallas kernels: 37.6 us -> 29.2 us  [the longest x1 12.6 us: first_call(): pl.pallas_call(functools.partial(first_kernel, rows), out_shape=(jax.Shap...]
where the time goes in v2:
time: 97.8 us; the launch traced here: 97.7 us
  Pallas kernels  40.4 us (41%)
  starting transfers between devices  32.4 us (33%)
  waiting for transfers between devices  24 us (25%)
    ppermute x22, starting transfers between devices, swap(): lax.ppermute(value, axis, [(i, i ^ distance) for i in range(lax.axis_size...  32.4 us
    ppermute x22, waiting for transfers between devices, swap(): lax.ppermute(value, axis, [(i, i ^ distance) for i in range(lax.axis_size...  24 us
    pallas_call x1, Pallas kernels, first_call(): pl.pallas_call(functools.partial(first_kernel, rows), out_shape=(jax.Shap...  12.6 us
    pallas_call x1, Pallas kernels, chol_one_call(): pl.pallas_call(chol_one_kernel, out_shape=(jax.ShapeDtypeStruct((4 * K, K...  8.63 us
    pallas_call x1, Pallas kernels, gram_call(): pl.pallas_call(functools.partial(gram_kernel, rows), out_shape=(half, hal...  7.95 us
    pallas_call x1, Pallas kernels, basis_call(): pl.pallas_call(functools.partial(basis_kernel, scale), out_shape=jax.Shap...  7.09 us
    pallas_call x1, Pallas kernels, chol_two_call(): pl.pallas_call(functools.partial(chol_two_kernel, scale), out_shape=(jax....  4.17 us
  transfers between devices with their start and end apart: 22, of which 18 were waited for; matrix products, arithmetic and copies ran while one was open for 0% of the time, Pallas kernels for 0%

profile of v2, /device:TPU:1, one launch (start us, length us, event | category | flops | bytes accessed | tf_op | source)
XLA Modules:
  0.0 97.7 jit_solution(14450598150890292766)
XLA Ops:
  0.6 7.9 %gram_one.1 = (f32[136,128]{1,0:T(8,128)S(1)}, f32[136,128]{1,0:T(8,128)S(1)}) custom-call(f32[12288,256]{1,0:T(8,128)} %x_hbm.3), custom_call_target="tpu_custom_call" | custom-call | tf_op jit(solution)/shard_map/gram_one/pallas_call | solution.py:127
  8.6 1.5 %collective-permute-start = (f32[136,128]{1,0:T(8,128)S(1)}, f32[136,128]{1,0:T(8,128)S(1)}, u32[]{:S(2)}, u32[]{:S(2)}) collective-permute-start(f32[136,128]{1,0:T(8,128)S(1)} %get-tuple-element.13), channel_id=1, source_target_pairs={{0,1},{1,0},{2,3},{3,2},{4,5},{5,4},{6,7},{7,6},{8,9},{9,8},{10,11... | collective-permute-start | bytes 208904 | tf_op jit(solution)/shard_map/ppermute | solution.py:403
  10.0 0.9 collective-permute-done
  11.0 2.7 %collective-permute-start.3 = (f32[136,128]{1,0:T(8,128)S(1)}, f32[136,128]{1,0:T(8,128)S(1)}, u32[]{:S(2)}, u32[]{:S(2)}) collective-permute-start(f32[136,128]{1,0:T(8,128)S(1)} %add.60), channel_id=1, source_target_pairs={{0,6},{1,7},{2,4},{3,5},{4,2},{5,3},{6,0},{7,1},{8,14},{9,15},{10,... | collective-permute-start | bytes 208904 | tf_op jit(solution)/shard_map/ppermute | solution.py:403
  13.6 0.5 collective-permute-start.2
  14.2 0.1 collective-permute-start.1
  14.3 1.4 %collective-permute-done.3 = f32[136,128]{1,0:T(8,128)S(1)} collective-permute-done((f32[136,128]{1,0:T(8,128)S(1)}, f32[136,128]{1,0:T(8,128)S(1)}, u32[]{:S(2)}, u32[]{:S(2)}) %collective-permute-start.3) | collective-permute-done | bytes 69664 | tf_op jit(solution)/shard_map/ppermute | solution.py:403
  15.7 2.5 %collective-permute-done.2 = f32[136,128]{1,0:T(8,128)S(1)} collective-permute-done((f32[136,128]{1,0:T(8,128)S(1)}, f32[136,128]{1,0:T(8,128)S(1)}, u32[]{:S(2)}, u32[]{:S(2)}) %collective-permute-start.2) | collective-permute-done | bytes 69664 | tf_op jit(solution)/shard_map/ppermute | solution.py:403
  18.3 0.0 collective-permute-done.1
  18.3 3.8 %collective-permute-start.6 = (f32[136,128]{1,0:T(8,128)S(1)}, f32[136,128]{1,0:T(8,128)S(1)}, u32[]{:S(2)}, u32[]{:S(2)}) collective-permute-start(f32[136,128]{1,0:T(8,128)S(1)} %add_add_fusion.5), channel_id=1, source_target_pairs={{0,24},{8,16},{16,8},{24,0},{32,56},{40,48},{48,40},{56,32},{64,88... | collective-permute-start | bytes 208904 | tf_op jit(solution)/shard_map/ppermute | solution.py:403
  22.2 0.0 collective-permute-start.5
  22.2 0.7 collective-permute-start.4
  22.8 1.3 %collective-permute-done.6 = f32[136,128]{1,0:T(8,128)S(1)} collective-permute-done((f32[136,128]{1,0:T(8,128)S(1)}, f32[136,128]{1,0:T(8,128)S(1)}, u32[]{:S(2)}, u32[]{:S(2)}) %collective-permute-start.6) | collective-permute-done | bytes 69664 | tf_op jit(solution)/shard_map/ppermute | solution.py:403
  24.2 2.8 %collective-permute-done.5 = f32[136,128]{1,0:T(8,128)S(1)} collective-permute-done((f32[136,128]{1,0:T(8,128)S(1)}, f32[136,128]{1,0:T(8,128)S(1)}, u32[]{:S(2)}, u32[]{:S(2)}) %collective-permute-start.5) | collective-permute-done | bytes 69664 | tf_op jit(solution)/shard_map/ppermute | solution.py:403
  26.9 0.0 collective-permute-done.4
  26.9 2.8 %collective-permute-start.9 = (f32[136,128]{1,0:T(8,128)S(1)}, f32[136,128]{1,0:T(8,128)S(1)}, u32[]{:S(2)}, u32[]{:S(2)}) collective-permute-start(f32[136,128]{1,0:T(8,128)S(1)} %add_add_fusion.4), channel_id=1, source_target_pairs={{0,96},{8,104},{16,112},{24,120},{32,64},{40,72},{48,80},{56,88},{... | collective-permute-start | bytes 208904 | tf_op jit(solution)/shard_map/ppermute | solution.py:403
  29.8 0.4 collective-permute-start.8
  30.1 0.3 collective-permute-start.7
  30.4 1.3 %collective-permute-done.9 = f32[136,128]{1,0:T(8,128)S(1)} collective-permute-done((f32[136,128]{1,0:T(8,128)S(1)}, f32[136,128]{1,0:T(8,128)S(1)}, u32[]{:S(2)}, u32[]{:S(2)}) %collective-permute-start.9) | collective-permute-done | bytes 69664 | tf_op jit(solution)/shard_map/ppermute | solution.py:403
  31.8 2.7 %collective-permute-done.8 = f32[136,128]{1,0:T(8,128)S(1)} collective-permute-done((f32[136,128]{1,0:T(8,128)S(1)}, f32[136,128]{1,0:T(8,128)S(1)}, u32[]{:S(2)}, u32[]{:S(2)}) %collective-permute-start.8) | collective-permute-done | bytes 69664 | tf_op jit(solution)/shard_map/ppermute | solution.py:403
  34.4 5.0 %collective-permute-start.10 = (f32[136,128]{1,0:T(8,128)S(1)}, f32[136,128]{1,0:T(8,128)S(1)}, u32[]{:S(2)}, u32[]{:S(2)}) collective-permute-start(f32[136,128]{1,0:T(8,128)S(1)} %add_add_fusion.3.mine_ref), channel_id=1, source_target_pairs={{0,1},{1,0},{2,3},{3,2},{4,5},{5,4},{6,7},{7,6},{8,9},{9,8},{10,11... | collective-permute-start | bytes 208904 | tf_op jit(solution)/shard_map/ppermute | solution.py:403
  39.5 0.9 collective-permute-done.10.other_ref
  40.4 8.6 %factor_one.1 = (bf16[1024,256]{1,0:T(8,128)(2,1)S(1)}, f32[256,256]{1,0:T(8,128)S(1)}) custom-call(f32[136,128]{1,0:T(8,128)S(1)} %add_add_fusion.3.mine_ref, f32[136,128]{1,0:T(8,128)S(1)} %collective-permute-done.10.other_ref), custom_call_target="tpu_custom_call" | custom-call | tf_op jit(solution)/shard_map/factor_one/pallas_call | solution.py:299
  49.0 12.6 %first_and_gram_two.1 = (f32[12288,256]{1,0:T(8,128)S(1)}, f32[136,128]{1,0:T(8,128)S(1)}, f32[136,128]{1,0:T(8,128)S(1)}) custom-call(f32[12288,256]{1,0:T(8,128)} %x_hbm.3, bf16[1024,256]{1,0:T(8,128)(2,1)S(1)} %get-tuple-element.14.w_ref), custom_call_target="tpu_custom_call" | custom-call | tf_op jit(solution)/shard_map/first_and_gram_two/pallas_call | solution.py:178
  61.6 0.4 collective-permute-start.11
  62.0 0.9 collective-permute-done.11
  63.0 1.1 %collective-permute-start.14 = (f32[136,128]{1,0:T(8,128)S(1)}, f32[136,128]{1,0:T(8,128)S(1)}, u32[]{:S(2)}, u32[]{:S(2)}) collective-permute-start(f32[136,128]{1,0:T(8,128)S(1)} %add.70), channel_id=1, source_target_pairs={{0,6},{1,7},{2,4},{3,5},{4,2},{5,3},{6,0},{7,1},{8,14},{9,15},{10,... | collective-permute-start | bytes 208904 | tf_op jit(solution)/shard_map/ppermute | solution.py:403
  64.1 0.9 collective-permute-start.13
  65.0 1.4 %collective-permute-start.12 = (f32[136,128]{1,0:T(8,128)S(1)}, f32[136,128]{1,0:T(8,128)S(1)}, u32[]{:S(2)}, u32[]{:S(2)}) collective-permute-start(f32[136,128]{1,0:T(8,128)S(1)} %add.70), channel_id=1, source_target_pairs={{0,2},{1,3},{2,0},{3,1},{4,6},{5,7},{6,4},{7,5},{8,10},{9,11},{10,... | collective-permute-start | bytes 208904 | tf_op jit(solution)/shard_map/ppermute | solution.py:403
  66.3 1.1 %collective-permute-done.14 = f32[136,128]{1,0:T(8,128)S(1)} collective-permute-done((f32[136,128]{1,0:T(8,128)S(1)}, f32[136,128]{1,0:T(8,128)S(1)}, u32[]{:S(2)}, u32[]{:S(2)}) %collective-permute-start.14) | collective-permute-done | bytes 69664 | tf_op jit(solution)/shard_map/ppermute | solution.py:403
  67.4 1.4 %collective-permute-done.13 = f32[136,128]{1,0:T(8,128)S(1)} collective-permute-done((f32[136,128]{1,0:T(8,128)S(1)}, f32[136,128]{1,0:T(8,128)S(1)}, u32[]{:S(2)}, u32[]{:S(2)}) %collective-permute-start.13) | collective-permute-done | bytes 69664 | tf_op jit(solution)/shard_map/ppermute | solution.py:403
  68.8 0.6 collective-permute-done.12
  69.5 1.1 %collective-permute-start.17 = (f32[136,128]{1,0:T(8,128)S(1)}, f32[136,128]{1,0:T(8,128)S(1)}, u32[]{:S(2)}, u32[]{:S(2)}) collective-permute-start(f32[136,128]{1,0:T(8,128)S(1)} %add_add_fusion.2), channel_id=1, source_target_pairs={{0,24},{8,16},{16,8},{24,0},{32,56},{40,48},{48,40},{56,32},{64,88... | collective-permute-start | bytes 208904 | tf_op jit(solution)/shard_map/ppermute | solution.py:403
  70.6 0.8 collective-permute-start.16
  71.4 1.4 %collective-permute-start.15 = (f32[136,128]{1,0:T(8,128)S(1)}, f32[136,128]{1,0:T(8,128)S(1)}, u32[]{:S(2)}, u32[]{:S(2)}) collective-permute-start(f32[136,128]{1,0:T(8,128)S(1)} %add_add_fusion.2), channel_id=1, source_target_pairs={{0,8},{8,0},{16,24},{24,16},{32,40},{40,32},{48,56},{56,48},{64,72... | collective-permute-start | bytes 208904 | tf_op jit(solution)/shard_map/ppermute | solution.py:403
  72.8 1.1 %collective-permute-done.17 = f32[136,128]{1,0:T(8,128)S(1)} collective-permute-done((f32[136,128]{1,0:T(8,128)S(1)}, f32[136,128]{1,0:T(8,128)S(1)}, u32[]{:S(2)}, u32[]{:S(2)}) %collective-permute-start.17) | collective-permute-done | bytes 69664 | tf_op jit(solution)/shard_map/ppermute | solution.py:403
  73.9 1.3 %collective-permute-done.16 = f32[136,128]{1,0:T(8,128)S(1)} collective-permute-done((f32[136,128]{1,0:T(8,128)S(1)}, f32[136,128]{1,0:T(8,128)S(1)}, u32[]{:S(2)}, u32[]{:S(2)}) %collective-permute-start.16) | collective-permute-done | bytes 69664 | tf_op jit(solution)/shard_map/ppermute | solution.py:403
  75.2 0.3 collective-permute-done.15
  75.6 1.1 %collective-permute-start.20 = (f32[136,128]{1,0:T(8,128)S(1)}, f32[136,128]{1,0:T(8,128)S(1)}, u32[]{:S(2)}, u32[]{:S(2)}) collective-permute-start(f32[136,128]{1,0:T(8,128)S(1)} %add_add_fusion.1), channel_id=1, source_target_pairs={{0,96},{8,104},{16,112},{24,120},{32,64},{40,72},{48,80},{56,88},{... | collective-permute-start | bytes 208904 | tf_op jit(solution)/shard_map/ppermute | solution.py:403
  76.7 0.8 collective-permute-start.19
  77.5 1.4 %collective-permute-start.18 = (f32[136,128]{1,0:T(8,128)S(1)}, f32[136,128]{1,0:T(8,128)S(1)}, u32[]{:S(2)}, u32[]{:S(2)}) collective-permute-start(f32[136,128]{1,0:T(8,128)S(1)} %add_add_fusion.1), channel_id=1, source_target_pairs={{0,32},{8,40},{16,48},{24,56},{32,0},{40,8},{48,16},{56,24},{64,96... | collective-permute-start | bytes 208904 | tf_op jit(solution)/shard_map/ppermute | solution.py:403
  78.9 1.1 %collective-permute-done.20 = f32[136,128]{1,0:T(8,128)S(1)} collective-permute-done((f32[136,128]{1,0:T(8,128)S(1)}, f32[136,128]{1,0:T(8,128)S(1)}, u32[]{:S(2)}, u32[]{:S(2)}) %collective-permute-start.20) | collective-permute-done | bytes 69664 | tf_op jit(solution)/shard_map/ppermute | solution.py:403
  80.0 1.3 %collective-permute-done.19 = f32[136,128]{1,0:T(8,128)S(1)} collective-permute-done((f32[136,128]{1,0:T(8,128)S(1)}, f32[136,128]{1,0:T(8,128)S(1)}, u32[]{:S(2)}, u32[]{:S(2)}) %collective-permute-start.19) | collective-permute-done | bytes 69664 | tf_op jit(solution)/shard_map/ppermute | solution.py:403
  81.3 0.0 collective-permute-done.18
  81.4 4.1 %collective-permute-start.21 = (f32[136,128]{1,0:T(8,128)S(1)}, f32[136,128]{1,0:T(8,128)S(1)}, u32[]{:S(2)}, u32[]{:S(2)}) collective-permute-start(f32[136,128]{1,0:T(8,128)S(1)} %add_add_fusion.mine_ref), channel_id=1, source_target_pairs={{0,1},{1,0},{2,3},{3,2},{4,5},{5,4},{6,7},{7,6},{8,9},{9,8},{10,11... | collective-permute-start | bytes 208904 | tf_op jit(solution)/shard_map/ppermute | solution.py:403
  85.5 0.9 collective-permute-done.21.other_ref
  86.4 4.2 %factor_two.1 = (s32[1]{0:T(128)}, bf16[768,256]{1,0:T(8,128)(2,1)S(1)}, f32[256,256]{1,0:T(8,128)}) custom-call(f32[136,128]{1,0:T(8,128)S(1)} %add_add_fusion.mine_ref, f32[136,128]{1,0:T(8,128)S(1)} %collective-permute-done.21.other_ref, f32[256,256]{1,0:T(8,128)S(1)} %get-tuple-element.17.upper_ref), custom_call_target="tpu_custom_call" | custom-call | tf_op jit(solution)/shard_map/factor_two/pallas_call | solution.py:387
  90.6 7.1 %basis.1 = f32[12288,256]{1,0:T(8,128)} custom-call(s32[1]{0:T(128)} %get-tuple-element.18.small_ref, f32[12288,256]{1,0:T(8,128)S(1)} %get-tuple-element.19.f_ref, bf16[768,256]{1,0:T(8,128)(2,1)S(1)} %get-tuple-element.20.c_ref), custom_call_target="tpu_custom_call" | custom-call | tf_op jit(solution)/shard_map/basis/pallas_call | solution.py:208
  (9 shorter events, 0.1 us)
Async XLA Ops:
  8.6 2.4 %collective-permute-start = (f32[136,128]{1,0:T(8,128)S(1)}, f32[136,128]{1,0:T(8,128)S(1)}, u32[]{:S(2)}, u32[]{:S(2)}) collective-permute-start(f32[136,128]{1,0:T(8,128)S(1)} %get-tuple-element.13), channel_id=1, source_target_pairs={{0,1},{1,0},{2,3},{3,2},{4,5},{5,4},{6,7},{7,6},{8,9},{9,8},{10,11... | collective-permute-start | bytes 208904 | tf_op jit(solution)/shard_map/ppermute | solution.py:403
  11.0 4.8 %collective-permute-start.3 = (f32[136,128]{1,0:T(8,128)S(1)}, f32[136,128]{1,0:T(8,128)S(1)}, u32[]{:S(2)}, u32[]{:S(2)}) collective-permute-start(f32[136,128]{1,0:T(8,128)S(1)} %add.60), channel_id=1, source_target_pairs={{0,6},{1,7},{2,4},{3,5},{4,2},{5,3},{6,0},{7,1},{8,14},{9,15},{10,... | collective-permute-start | bytes 208904 | tf_op jit(solution)/shard_map/ppermute | solution.py:403
  13.6 4.7 %collective-permute-start.2 = (f32[136,128]{1,0:T(8,128)S(1)}, f32[136,128]{1,0:T(8,128)S(1)}, u32[]{:S(2)}, u32[]{:S(2)}) collective-permute-start(f32[136,128]{1,0:T(8,128)S(1)} %add.60), channel_id=1, source_target_pairs={{0,4},{1,5},{2,6},{3,7},{4,0},{5,1},{6,2},{7,3},{8,12},{9,13},{10,... | collective-permute-start | bytes 208904 | tf_op jit(solution)/shard_map/ppermute | solution.py:403
  14.2 4.1 %collective-permute-start.1 = (f32[136,128]{1,0:T(8,128)S(1)}, f32[136,128]{1,0:T(8,128)S(1)}, u32[]{:S(2)}, u32[]{:S(2)}) collective-permute-start(f32[136,128]{1,0:T(8,128)S(1)} %add.60), channel_id=1, source_target_pairs={{0,2},{1,3},{2,0},{3,1},{4,6},{5,7},{6,4},{7,5},{8,10},{9,11},{10,... | collective-permute-start | bytes 208904 | tf_op jit(solution)/shard_map/ppermute | solution.py:403
  18.3 5.8 %collective-permute-start.6 = (f32[136,128]{1,0:T(8,128)S(1)}, f32[136,128]{1,0:T(8,128)S(1)}, u32[]{:S(2)}, u32[]{:S(2)}) collective-permute-start(f32[136,128]{1,0:T(8,128)S(1)} %add_add_fusion.5), channel_id=1, source_target_pairs={{0,24},{8,16},{16,8},{24,0},{32,56},{40,48},{48,40},{56,32},{64,88... | collective-permute-start | bytes 208904 | tf_op jit(solution)/shard_map/ppermute | solution.py:403
  22.2 4.8 %collective-permute-start.5 = (f32[136,128]{1,0:T(8,128)S(1)}, f32[136,128]{1,0:T(8,128)S(1)}, u32[]{:S(2)}, u32[]{:S(2)}) collective-permute-start(f32[136,128]{1,0:T(8,128)S(1)} %add_add_fusion.5), channel_id=1, source_target_pairs={{0,16},{8,24},{16,0},{24,8},{32,48},{40,56},{48,32},{56,40},{64,80... | collective-permute-start | bytes 208904 | tf_op jit(solution)/shard_map/ppermute | solution.py:403
  22.2 4.8 %collective-permute-start.4 = (f32[136,128]{1,0:T(8,128)S(1)}, f32[136,128]{1,0:T(8,128)S(1)}, u32[]{:S(2)}, u32[]{:S(2)}) collective-permute-start(f32[136,128]{1,0:T(8,128)S(1)} %add_add_fusion.5), channel_id=1, source_target_pairs={{0,8},{8,0},{16,24},{24,16},{32,40},{40,32},{48,56},{56,48},{64,72... | collective-permute-start | bytes 208904 | tf_op jit(solution)/shard_map/ppermute | solution.py:403
  26.9 4.8 %collective-permute-start.9 = (f32[136,128]{1,0:T(8,128)S(1)}, f32[136,128]{1,0:T(8,128)S(1)}, u32[]{:S(2)}, u32[]{:S(2)}) collective-permute-start(f32[136,128]{1,0:T(8,128)S(1)} %add_add_fusion.4), channel_id=1, source_target_pairs={{0,96},{8,104},{16,112},{24,120},{32,64},{40,72},{48,80},{56,88},{... | collective-permute-start | bytes 208904 | tf_op jit(solution)/shard_map/ppermute | solution.py:403
  29.8 4.7 %collective-permute-start.8 = (f32[136,128]{1,0:T(8,128)S(1)}, f32[136,128]{1,0:T(8,128)S(1)}, u32[]{:S(2)}, u32[]{:S(2)}) collective-permute-start(f32[136,128]{1,0:T(8,128)S(1)} %add_add_fusion.4), channel_id=1, source_target_pairs={{0,64},{8,72},{16,80},{24,88},{32,96},{40,104},{48,112},{56,120},{... | collective-permute-start | bytes 208904 | tf_op jit(solution)/shard_map/ppermute | solution.py:403
  30.1 4.3 %collective-permute-start.7 = (f32[136,128]{1,0:T(8,128)S(1)}, f32[136,128]{1,0:T(8,128)S(1)}, u32[]{:S(2)}, u32[]{:S(2)}) collective-permute-start(f32[136,128]{1,0:T(8,128)S(1)} %add_add_fusion.4), channel_id=1, source_target_pairs={{0,32},{8,40},{16,48},{24,56},{32,0},{40,8},{48,16},{56,24},{64,96... | collective-permute-start | bytes 208904 | tf_op jit(solution)/shard_map/ppermute | solution.py:403
  34.4 5.9 %collective-permute-start.10 = (f32[136,128]{1,0:T(8,128)S(1)}, f32[136,128]{1,0:T(8,128)S(1)}, u32[]{:S(2)}, u32[]{:S(2)}) collective-permute-start(f32[136,128]{1,0:T(8,128)S(1)} %add_add_fusion.3.mine_ref), channel_id=1, source_target_pairs={{0,1},{1,0},{2,3},{3,2},{4,5},{5,4},{6,7},{7,6},{8,9},{9,8},{10,11... | collective-permute-start | bytes 208904 | tf_op jit(solution)/shard_map/ppermute | solution.py:403
  61.6 1.3 %collective-permute-start.11 = (f32[136,128]{1,0:T(8,128)S(1)}, f32[136,128]{1,0:T(8,128)S(1)}, u32[]{:S(2)}, u32[]{:S(2)}) collective-permute-start(f32[136,128]{1,0:T(8,128)S(1)} %get-tuple-element.16), channel_id=1, source_target_pairs={{0,1},{1,0},{2,3},{3,2},{4,5},{5,4},{6,7},{7,6},{8,9},{9,8},{10,11... | collective-permute-start | bytes 208904 | tf_op jit(solution)/shard_map/ppermute | solution.py:403
  63.0 4.5 %collective-permute-start.14 = (f32[136,128]{1,0:T(8,128)S(1)}, f32[136,128]{1,0:T(8,128)S(1)}, u32[]{:S(2)}, u32[]{:S(2)}) collective-permute-start(f32[136,128]{1,0:T(8,128)S(1)} %add.70), channel_id=1, source_target_pairs={{0,6},{1,7},{2,4},{3,5},{4,2},{5,3},{6,0},{7,1},{8,14},{9,15},{10,... | collective-permute-start | bytes 208904 | tf_op jit(solution)/shard_map/ppermute | solution.py:403
  64.1 4.8 %collective-permute-start.13 = (f32[136,128]{1,0:T(8,128)S(1)}, f32[136,128]{1,0:T(8,128)S(1)}, u32[]{:S(2)}, u32[]{:S(2)}) collective-permute-start(f32[136,128]{1,0:T(8,128)S(1)} %add.70), channel_id=1, source_target_pairs={{0,4},{1,5},{2,6},{3,7},{4,0},{5,1},{6,2},{7,3},{8,12},{9,13},{10,... | collective-permute-start | bytes 208904 | tf_op jit(solution)/shard_map/ppermute | solution.py:403
  65.0 4.5 %collective-permute-start.12 = (f32[136,128]{1,0:T(8,128)S(1)}, f32[136,128]{1,0:T(8,128)S(1)}, u32[]{:S(2)}, u32[]{:S(2)}) collective-permute-start(f32[136,128]{1,0:T(8,128)S(1)} %add.70), channel_id=1, source_target_pairs={{0,2},{1,3},{2,0},{3,1},{4,6},{5,7},{6,4},{7,5},{8,10},{9,11},{10,... | collective-permute-start | bytes 208904 | tf_op jit(solution)/shard_map/ppermute | solution.py:403
  69.5 4.5 %collective-permute-start.17 = (f32[136,128]{1,0:T(8,128)S(1)}, f32[136,128]{1,0:T(8,128)S(1)}, u32[]{:S(2)}, u32[]{:S(2)}) collective-permute-start(f32[136,128]{1,0:T(8,128)S(1)} %add_add_fusion.2), channel_id=1, source_target_pairs={{0,24},{8,16},{16,8},{24,0},{32,56},{40,48},{48,40},{56,32},{64,88... | collective-permute-start | bytes 208904 | tf_op jit(solution)/shard_map/ppermute | solution.py:403
  70.6 4.7 %collective-permute-start.16 = (f32[136,128]{1,0:T(8,128)S(1)}, f32[136,128]{1,0:T(8,128)S(1)}, u32[]{:S(2)}, u32[]{:S(2)}) collective-permute-start(f32[136,128]{1,0:T(8,128)S(1)} %add_add_fusion.2), channel_id=1, source_target_pairs={{0,16},{8,24},{16,0},{24,8},{32,48},{40,56},{48,32},{56,40},{64,80... | collective-permute-start | bytes 208904 | tf_op jit(solution)/shard_map/ppermute | solution.py:403
  71.4 4.2 %collective-permute-start.15 = (f32[136,128]{1,0:T(8,128)S(1)}, f32[136,128]{1,0:T(8,128)S(1)}, u32[]{:S(2)}, u32[]{:S(2)}) collective-permute-start(f32[136,128]{1,0:T(8,128)S(1)} %add_add_fusion.2), channel_id=1, source_target_pairs={{0,8},{8,0},{16,24},{24,16},{32,40},{40,32},{48,56},{56,48},{64,72... | collective-permute-start | bytes 208904 | tf_op jit(solution)/shard_map/ppermute | solution.py:403
  75.6 4.5 %collective-permute-start.20 = (f32[136,128]{1,0:T(8,128)S(1)}, f32[136,128]{1,0:T(8,128)S(1)}, u32[]{:S(2)}, u32[]{:S(2)}) collective-permute-start(f32[136,128]{1,0:T(8,128)S(1)} %add_add_fusion.1), channel_id=1, source_target_pairs={{0,96},{8,104},{16,112},{24,120},{32,64},{40,72},{48,80},{56,88},{... | collective-permute-start | bytes 208904 | tf_op jit(solution)/shard_map/ppermute | solution.py:403
  76.7 4.7 %collective-permute-start.19 = (f32[136,128]{1,0:T(8,128)S(1)}, f32[136,128]{1,0:T(8,128)S(1)}, u32[]{:S(2)}, u32[]{:S(2)}) collective-permute-start(f32[136,128]{1,0:T(8,128)S(1)} %add_add_fusion.1), channel_id=1, source_target_pairs={{0,64},{8,72},{16,80},{24,88},{32,96},{40,104},{48,112},{56,120},{... | collective-permute-start | bytes 208904 | tf_op jit(solution)/shard_map/ppermute | solution.py:403
  77.5 3.9 %collective-permute-start.18 = (f32[136,128]{1,0:T(8,128)S(1)}, f32[136,128]{1,0:T(8,128)S(1)}, u32[]{:S(2)}, u32[]{:S(2)}) collective-permute-start(f32[136,128]{1,0:T(8,128)S(1)} %add_add_fusion.1), channel_id=1, source_target_pairs={{0,32},{8,40},{16,48},{24,56},{32,0},{40,8},{48,16},{56,24},{64,96... | collective-permute-start | bytes 208904 | tf_op jit(solution)/shard_map/ppermute | solution.py:403
  81.4 5.0 %collective-permute-start.21 = (f32[136,128]{1,0:T(8,128)S(1)}, f32[136,128]{1,0:T(8,128)S(1)}, u32[]{:S(2)}, u32[]{:S(2)}) collective-permute-start(f32[136,128]{1,0:T(8,128)S(1)} %add_add_fusion.mine_ref), channel_id=1, source_target_pairs={{0,1},{1,0},{2,3},{3,2},{4,5},{5,4},{6,7},{7,6},{8,9},{9,8},{10,11... | collective-permute-start | bytes 208904 | tf_op jit(solution)/shard_map/ppermute | solution.py:403

commit v3 on v2

--- a/solution.py
+++ b/solution.py
@@ -190,28 +190,51 @@
     )(x, w)
 
 
-def basis_kernel(scale, small_ref, f_ref, c_ref, out_ref):
-    rows = out_ref.shape[0]
-    first = f_ref[pl.ds(pl.multiple_of(pl.program_id(0) * rows, rows), rows), :]
+def basis_kernel(rows, scale, small_ref, f_ref, c_ref, out_hbm, out_ref, sems):
+    steps = f_ref.shape[0] // rows
+
+    def part(step):
+        return pl.ds(pl.multiple_of(step * rows, rows), rows)
+
+    def copy(step):
+        return pltpu.make_async_copy(out_ref.at[part(step)], out_hbm.at[part(step)], sems.at[step])
+
+    def run(correction):
+        def body(step, carry):
+            first = f_ref[part(step), :]
+            out_ref[part(step), :] = (first + correction(first)) * scale
+            copy(step).start()
+            return carry
+
+        lax.fori_loop(0, steps, body, 0)
+
+    def one_product(first):
+        return dot_nn(first.astype(BF16), c_ref[:K, :])
+
+    def three_products(first):
+        h, m = split2(first)
+        return dot_nn(jnp.concatenate([h, m, h], axis=1), c_ref[...])
 
     @pl.when(small_ref[0] == 1)
     def _():
-        out_ref[...] = (first + dot_nn(first.astype(BF16), c_ref[:K, :])) * scale
+        run(one_product)
 
     @pl.when(small_ref[0] == 0)
     def _():
-        h, m = split2(first)
-        out_ref[...] = (first + dot_nn(jnp.concatenate([h, m, h], axis=1), c_ref[...])) * scale
+        run(three_products)
+
+    for step in range(steps):
+        copy(step).wait()
 
 
 def basis_call(small, first, c, rows, scale):
     return pl.pallas_call(
-        functools.partial(basis_kernel, scale),
+        functools.partial(basis_kernel, rows, scale),
         out_shape=jax.ShapeDtypeStruct(first.shape, F32),
-        grid=(first.shape[0] // rows,),
         in_specs=[pl.BlockSpec(memory_space=pltpu.SMEM)] + [VMEM_WHOLE] * 2,
-        out_specs=pl.BlockSpec((rows, K), lambda i: (i, 0)),
-        compiler_params=params(30),
+        out_specs=pl.BlockSpec(memory_space=pltpu.HBM),
+        scratch_shapes=[pltpu.VMEM(first.shape, F32), pltpu.SemaphoreType.DMA((first.shape[0] // rows,))],
+        compiler_params=params(34),
         name="basis",
     )(small, first, c)
 
@@ -256,29 +279,31 @@
 
 
 def factorize(t_ref):
-    def block(b, carry):
-        r0 = pl.multiple_of(b * B, B)
-        lane0 = pl.multiple_of(lax.div(b, H // B) * H, H)
-        shift = lax.rem(b, H // B) * B
-        d = t_ref[pl.ds(r0, B), pl.ds(lane0, H)]
-        d = pltpu.roll(d, lax.rem(H - shift, H), 1)
-        r = t_ref[pl.ds(r0, B), :]
-        full = jnp.concatenate([d, r], axis=1)
-        out = eliminate([full[S * s:S * s + S] for s in range(B // S)])
-        u = jnp.concatenate([o[:, H:] for o in out], axis=0)
-        t_ref[pl.ds(r0, B), :] = u
-        lane = lax.broadcasted_iota(jnp.int32, (B, K), 1)
-        left = jnp.where(lane >= r0 + B, u[:, :K], 0.0)
-        lh, lm, ll = split3(left)
-        uh, um, ul = split3(u)
-        upd = dot_tn(
-            jnp.concatenate([lh, lh, lm, lm, lh, ll], axis=0),
-            jnp.concatenate([uh, um, uh, um, ul, uh], axis=0),
-        )
-        t_ref[...] -= upd
-        return carry
-
-    lax.fori_loop(0, K // B, block, 0)
+    for side in range(2):
+        lanes = slice(side * H, side * H + 3 * H)
+        below = slice(side * H, K)
+        width = K - side * H
+
+        def block(b, carry):
+            r0 = pl.multiple_of(b * B, B)
+            shift = r0 - side * H
+            r = t_ref[pl.ds(r0, B), lanes]
+            d = pltpu.roll(r[:, :H], lax.rem(H - shift, H), 1)
+            full = jnp.concatenate([d, r], axis=1)
+            out = eliminate([full[S * s : S * s + S] for s in range(B // S)])
+            u = jnp.concatenate([o[:, H:] for o in out], axis=0)
+            t_ref[pl.ds(r0, B), lanes] = u
+            lane = lax.broadcasted_iota(jnp.int32, (B, width), 1)
+            left = jnp.where(lane >= shift + B, u[:, :width], 0.0)
+            lh, lm, ll = split3(left)
+            uh, um, ul = split3(u)
+            t_ref[below, lanes] -= dot_tn(
+                jnp.concatenate([lh, lh, lm, lm, lh, ll], axis=0),
+                jnp.concatenate([uh, um, uh, um, ul, uh], axis=0),
+            )
+            return carry
+
+        lax.fori_loop(side * (H // B), (side + 1) * (H // B), block, 0)
 
 
 def chol_one_kernel(mine_ref, other_ref, w_ref, upper_ref, t_ref):
@@ -418,6 +443,7 @@
 
 ROWS_PER_STEP = 2048
 FIRST_ROWS_PER_STEP = 3072
+BASIS_ROWS_PER_STEP = 1536
 
 
 def shards(panel):
@@ -427,7 +453,7 @@
     w, upper = chol_one_call(*reduce_gram(keep, send))
     first, keep, send = first_call(panel, w, FIRST_ROWS_PER_STEP)
     small, c, factor = chol_two_call(*reduce_gram(keep, send), upper, scale)
-    return basis_call(small, first, c, ROWS_PER_STEP, scale), factor
+    return basis_call(small, first, c, BASIS_ROWS_PER_STEP, scale), factor
 
 
 def solution(mesh):

time: 97.8 us -> 96.4 us (0.986)
  Pallas kernels: 40.4 us -> 38.9 us
    pallas_call x1, Pallas kernels: 7.09 us -> 5.71 us  [basis_call(): pl.pallas_call(functools.partial(basis_kernel, rows, scale), out_shape=ja...]
where the time goes in v3:
time: 96.4 us; the launch traced here: 96.3 us
  Pallas kernels  38.9 us (40%)
  starting transfers between devices  32.4 us (34%)
  waiting for transfers between devices  24 us (25%)
    ppermute x22, starting transfers between devices, swap(): lax.ppermute(value, axis, [(i, i ^ distance) for i in range(lax.axis_size...  32.4 us
    ppermute x22, waiting for transfers between devices, swap(): lax.ppermute(value, axis, [(i, i ^ distance) for i in range(lax.axis_size...  24 us
    pallas_call x1, Pallas kernels, first_call(): pl.pallas_call(functools.partial(first_kernel, rows), out_shape=(jax.Shap...  12.6 us
    pallas_call x1, Pallas kernels, chol_one_call(): pl.pallas_call(chol_one_kernel, out_shape=(jax.ShapeDtypeStruct((4 * K, K...  8.43 us
    pallas_call x1, Pallas kernels, gram_call(): pl.pallas_call(functools.partial(gram_kernel, rows), out_shape=(half, hal...  7.95 us
    pallas_call x1, Pallas kernels, basis_call(): pl.pallas_call(functools.partial(basis_kernel, rows, scale), out_shape=ja...  5.71 us
    pallas_call x1, Pallas kernels, chol_two_call(): pl.pallas_call(functools.partial(chol_two_kernel, scale), out_shape=(jax....  4.18 us
  transfers between devices with their start and end apart: 22, of which 18 were waited for; matrix products, arithmetic and copies ran while one was open for 0% of the time, Pallas kernels for 0%

profile of v3, /device:TPU:1, one launch (start us, length us, event | category | flops | bytes accessed | tf_op | source)
XLA Modules:
  0.0 96.3 jit_solution(332003817093197153)
XLA Ops:
  0.6 7.9 %gram_one.1 = (f32[136,128]{1,0:T(8,128)S(1)}, f32[136,128]{1,0:T(8,128)S(1)}) custom-call(f32[12288,256]{1,0:T(8,128)} %x_hbm.3), custom_call_target="tpu_custom_call" | custom-call | tf_op jit(solution)/shard_map/gram_one/pallas_call | solution.py:127
  8.6 1.5 %collective-permute-start = (f32[136,128]{1,0:T(8,128)S(1)}, f32[136,128]{1,0:T(8,128)S(1)}, u32[]{:S(2)}, u32[]{:S(2)}) collective-permute-start(f32[136,128]{1,0:T(8,128)S(1)} %get-tuple-element.13), channel_id=1, source_target_pairs={{0,1},{1,0},{2,3},{3,2},{4,5},{5,4},{6,7},{7,6},{8,9},{9,8},{10,11... | collective-permute-start | bytes 208904 | tf_op jit(solution)/shard_map/ppermute | solution.py:428
  10.0 0.9 collective-permute-done
  11.0 2.7 %collective-permute-start.3 = (f32[136,128]{1,0:T(8,128)S(1)}, f32[136,128]{1,0:T(8,128)S(1)}, u32[]{:S(2)}, u32[]{:S(2)}) collective-permute-start(f32[136,128]{1,0:T(8,128)S(1)} %add.60), channel_id=1, source_target_pairs={{0,6},{1,7},{2,4},{3,5},{4,2},{5,3},{6,0},{7,1},{8,14},{9,15},{10,... | collective-permute-start | bytes 208904 | tf_op jit(solution)/shard_map/ppermute | solution.py:428
  13.6 0.5 collective-permute-start.2
  14.2 0.1 collective-permute-start.1
  14.3 1.4 %collective-permute-done.3 = f32[136,128]{1,0:T(8,128)S(1)} collective-permute-done((f32[136,128]{1,0:T(8,128)S(1)}, f32[136,128]{1,0:T(8,128)S(1)}, u32[]{:S(2)}, u32[]{:S(2)}) %collective-permute-start.3) | collective-permute-done | bytes 69664 | tf_op jit(solution)/shard_map/ppermute | solution.py:428
  15.7 2.5 %collective-permute-done.2 = f32[136,128]{1,0:T(8,128)S(1)} collective-permute-done((f32[136,128]{1,0:T(8,128)S(1)}, f32[136,128]{1,0:T(8,128)S(1)}, u32[]{:S(2)}, u32[]{:S(2)}) %collective-permute-start.2) | collective-permute-done | bytes 69664 | tf_op jit(solution)/shard_map/ppermute | solution.py:428
  18.3 0.0 collective-permute-done.1
  18.3 3.8 %collective-permute-start.6 = (f32[136,128]{1,0:T(8,128)S(1)}, f32[136,128]{1,0:T(8,128)S(1)}, u32[]{:S(2)}, u32[]{:S(2)}) collective-permute-start(f32[136,128]{1,0:T(8,128)S(1)} %add_add_fusion.5), channel_id=1, source_target_pairs={{0,24},{8,16},{16,8},{24,0},{32,56},{40,48},{48,40},{56,32},{64,88... | collective-permute-start | bytes 208904 | tf_op jit(solution)/shard_map/ppermute | solution.py:428
  22.2 0.0 collective-permute-start.5
  22.2 0.7 collective-permute-start.4
  22.8 1.3 %collective-permute-done.6 = f32[136,128]{1,0:T(8,128)S(1)} collective-permute-done((f32[136,128]{1,0:T(8,128)S(1)}, f32[136,128]{1,0:T(8,128)S(1)}, u32[]{:S(2)}, u32[]{:S(2)}) %collective-permute-start.6) | collective-permute-done | bytes 69664 | tf_op jit(solution)/shard_map/ppermute | solution.py:428
  24.2 2.8 %collective-permute-done.5 = f32[136,128]{1,0:T(8,128)S(1)} collective-permute-done((f32[136,128]{1,0:T(8,128)S(1)}, f32[136,128]{1,0:T(8,128)S(1)}, u32[]{:S(2)}, u32[]{:S(2)}) %collective-permute-start.5) | collective-permute-done | bytes 69664 | tf_op jit(solution)/shard_map/ppermute | solution.py:428
  26.9 0.0 collective-permute-done.4
  26.9 2.8 %collective-permute-start.9 = (f32[136,128]{1,0:T(8,128)S(1)}, f32[136,128]{1,0:T(8,128)S(1)}, u32[]{:S(2)}, u32[]{:S(2)}) collective-permute-start(f32[136,128]{1,0:T(8,128)S(1)} %add_add_fusion.4), channel_id=1, source_target_pairs={{0,96},{8,104},{16,112},{24,120},{32,64},{40,72},{48,80},{56,88},{... | collective-permute-start | bytes 208904 | tf_op jit(solution)/shard_map/ppermute | solution.py:428
  29.8 0.4 collective-permute-start.8
  30.1 0.3 collective-permute-start.7
  30.4 1.3 %collective-permute-done.9 = f32[136,128]{1,0:T(8,128)S(1)} collective-permute-done((f32[136,128]{1,0:T(8,128)S(1)}, f32[136,128]{1,0:T(8,128)S(1)}, u32[]{:S(2)}, u32[]{:S(2)}) %collective-permute-start.9) | collective-permute-done | bytes 69664 | tf_op jit(solution)/shard_map/ppermute | solution.py:428
  31.8 2.7 %collective-permute-done.8 = f32[136,128]{1,0:T(8,128)S(1)} collective-permute-done((f32[136,128]{1,0:T(8,128)S(1)}, f32[136,128]{1,0:T(8,128)S(1)}, u32[]{:S(2)}, u32[]{:S(2)}) %collective-permute-start.8) | collective-permute-done | bytes 69664 | tf_op jit(solution)/shard_map/ppermute | solution.py:428
  34.4 5.0 %collective-permute-start.10 = (f32[136,128]{1,0:T(8,128)S(1)}, f32[136,128]{1,0:T(8,128)S(1)}, u32[]{:S(2)}, u32[]{:S(2)}) collective-permute-start(f32[136,128]{1,0:T(8,128)S(1)} %add_add_fusion.3.mine_ref), channel_id=1, source_target_pairs={{0,1},{1,0},{2,3},{3,2},{4,5},{5,4},{6,7},{7,6},{8,9},{9,8},{10,11... | collective-permute-start | bytes 208904 | tf_op jit(solution)/shard_map/ppermute | solution.py:428
  39.5 0.9 collective-permute-done.10.other_ref
  40.4 8.4 %factor_one.1 = (bf16[1024,256]{1,0:T(8,128)(2,1)S(1)}, f32[256,256]{1,0:T(8,128)S(1)}) custom-call(f32[136,128]{1,0:T(8,128)S(1)} %add_add_fusion.3.mine_ref, f32[136,128]{1,0:T(8,128)S(1)} %collective-permute-done.10.other_ref), custom_call_target="tpu_custom_call" | custom-call | tf_op jit(solution)/shard_map/factor_one/pallas_call | solution.py:324
  48.8 12.6 %first_and_gram_two.1 = (f32[12288,256]{1,0:T(8,128)S(1)}, f32[136,128]{1,0:T(8,128)S(1)}, f32[136,128]{1,0:T(8,128)S(1)}) custom-call(f32[12288,256]{1,0:T(8,128)} %x_hbm.3, bf16[1024,256]{1,0:T(8,128)(2,1)S(1)} %get-tuple-element.14.w_ref), custom_call_target="tpu_custom_call" | custom-call | tf_op jit(solution)/shard_map/first_and_gram_two/pallas_call | solution.py:178
  61.4 0.4 collective-permute-start.11
  61.9 0.9 collective-permute-done.11
  62.8 1.1 %collective-permute-start.14 = (f32[136,128]{1,0:T(8,128)S(1)}, f32[136,128]{1,0:T(8,128)S(1)}, u32[]{:S(2)}, u32[]{:S(2)}) collective-permute-start(f32[136,128]{1,0:T(8,128)S(1)} %add.70), channel_id=1, source_target_pairs={{0,6},{1,7},{2,4},{3,5},{4,2},{5,3},{6,0},{7,1},{8,14},{9,15},{10,... | collective-permute-start | bytes 208904 | tf_op jit(solution)/shard_map/ppermute | solution.py:428
  63.9 0.9 collective-permute-start.13
  64.8 1.4 %collective-permute-start.12 = (f32[136,128]{1,0:T(8,128)S(1)}, f32[136,128]{1,0:T(8,128)S(1)}, u32[]{:S(2)}, u32[]{:S(2)}) collective-permute-start(f32[136,128]{1,0:T(8,128)S(1)} %add.70), channel_id=1, source_target_pairs={{0,2},{1,3},{2,0},{3,1},{4,6},{5,7},{6,4},{7,5},{8,10},{9,11},{10,... | collective-permute-start | bytes 208904 | tf_op jit(solution)/shard_map/ppermute | solution.py:428
  66.1 1.1 %collective-permute-done.14 = f32[136,128]{1,0:T(8,128)S(1)} collective-permute-done((f32[136,128]{1,0:T(8,128)S(1)}, f32[136,128]{1,0:T(8,128)S(1)}, u32[]{:S(2)}, u32[]{:S(2)}) %collective-permute-start.14) | collective-permute-done | bytes 69664 | tf_op jit(solution)/shard_map/ppermute | solution.py:428
  67.2 1.4 %collective-permute-done.13 = f32[136,128]{1,0:T(8,128)S(1)} collective-permute-done((f32[136,128]{1,0:T(8,128)S(1)}, f32[136,128]{1,0:T(8,128)S(1)}, u32[]{:S(2)}, u32[]{:S(2)}) %collective-permute-start.13) | collective-permute-done | bytes 69664 | tf_op jit(solution)/shard_map/ppermute | solution.py:428
  68.7 0.6 collective-permute-done.12
  69.3 1.1 %collective-permute-start.17 = (f32[136,128]{1,0:T(8,128)S(1)}, f32[136,128]{1,0:T(8,128)S(1)}, u32[]{:S(2)}, u32[]{:S(2)}) collective-permute-start(f32[136,128]{1,0:T(8,128)S(1)} %add_add_fusion.2), channel_id=1, source_target_pairs={{0,24},{8,16},{16,8},{24,0},{32,56},{40,48},{48,40},{56,32},{64,88... | collective-permute-start | bytes 208904 | tf_op jit(solution)/shard_map/ppermute | solution.py:428
  70.4 0.8 collective-permute-start.16
  71.2 1.4 %collective-permute-start.15 = (f32[136,128]{1,0:T(8,128)S(1)}, f32[136,128]{1,0:T(8,128)S(1)}, u32[]{:S(2)}, u32[]{:S(2)}) collective-permute-start(f32[136,128]{1,0:T(8,128)S(1)} %add_add_fusion.2), channel_id=1, source_target_pairs={{0,8},{8,0},{16,24},{24,16},{32,40},{40,32},{48,56},{56,48},{64,72... | collective-permute-start | bytes 208904 | tf_op jit(solution)/shard_map/ppermute | solution.py:428
  72.6 1.1 %collective-permute-done.17 = f32[136,128]{1,0:T(8,128)S(1)} collective-permute-done((f32[136,128]{1,0:T(8,128)S(1)}, f32[136,128]{1,0:T(8,128)S(1)}, u32[]{:S(2)}, u32[]{:S(2)}) %collective-permute-start.17) | collective-permute-done | bytes 69664 | tf_op jit(solution)/shard_map/ppermute | solution.py:428
  73.7 1.3 %collective-permute-done.16 = f32[136,128]{1,0:T(8,128)S(1)} collective-permute-done((f32[136,128]{1,0:T(8,128)S(1)}, f32[136,128]{1,0:T(8,128)S(1)}, u32[]{:S(2)}, u32[]{:S(2)}) %collective-permute-start.16) | collective-permute-done | bytes 69664 | tf_op jit(solution)/shard_map/ppermute | solution.py:428
  75.1 0.3 collective-permute-done.15
  75.4 1.1 %collective-permute-start.20 = (f32[136,128]{1,0:T(8,128)S(1)}, f32[136,128]{1,0:T(8,128)S(1)}, u32[]{:S(2)}, u32[]{:S(2)}) collective-permute-start(f32[136,128]{1,0:T(8,128)S(1)} %add_add_fusion.1), channel_id=1, source_target_pairs={{0,96},{8,104},{16,112},{24,120},{32,64},{40,72},{48,80},{56,88},{... | collective-permute-start | bytes 208904 | tf_op jit(solution)/shard_map/ppermute | solution.py:428
  76.5 0.8 collective-permute-start.19
  77.3 1.4 %collective-permute-start.18 = (f32[136,128]{1,0:T(8,128)S(1)}, f32[136,128]{1,0:T(8,128)S(1)}, u32[]{:S(2)}, u32[]{:S(2)}) collective-permute-start(f32[136,128]{1,0:T(8,128)S(1)} %add_add_fusion.1), channel_id=1, source_target_pairs={{0,32},{8,40},{16,48},{24,56},{32,0},{40,8},{48,16},{56,24},{64,96... | collective-permute-start | bytes 208904 | tf_op jit(solution)/shard_map/ppermute | solution.py:428
  78.7 1.1 %collective-permute-done.20 = f32[136,128]{1,0:T(8,128)S(1)} collective-permute-done((f32[136,128]{1,0:T(8,128)S(1)}, f32[136,128]{1,0:T(8,128)S(1)}, u32[]{:S(2)}, u32[]{:S(2)}) %collective-permute-start.20) | collective-permute-done | bytes 69664 | tf_op jit(solution)/shard_map/ppermute | solution.py:428
  79.8 1.3 %collective-permute-done.19 = f32[136,128]{1,0:T(8,128)S(1)} collective-permute-done((f32[136,128]{1,0:T(8,128)S(1)}, f32[136,128]{1,0:T(8,128)S(1)}, u32[]{:S(2)}, u32[]{:S(2)}) %collective-permute-start.19) | collective-permute-done | bytes 69664 | tf_op jit(solution)/shard_map/ppermute | solution.py:428
  81.1 0.0 collective-permute-done.18
  81.2 4.1 %collective-permute-start.21 = (f32[136,128]{1,0:T(8,128)S(1)}, f32[136,128]{1,0:T(8,128)S(1)}, u32[]{:S(2)}, u32[]{:S(2)}) collective-permute-start(f32[136,128]{1,0:T(8,128)S(1)} %add_add_fusion.mine_ref), channel_id=1, source_target_pairs={{0,1},{1,0},{2,3},{3,2},{4,5},{5,4},{6,7},{7,6},{8,9},{9,8},{10,11... | collective-permute-start | bytes 208904 | tf_op jit(solution)/shard_map/ppermute | solution.py:428
  85.3 0.9 collective-permute-done.21.other_ref
  86.2 4.2 %factor_two.1 = (s32[1]{0:T(128)}, bf16[768,256]{1,0:T(8,128)(2,1)S(1)}, f32[256,256]{1,0:T(8,128)}) custom-call(f32[136,128]{1,0:T(8,128)S(1)} %add_add_fusion.mine_ref, f32[136,128]{1,0:T(8,128)S(1)} %collective-permute-done.21.other_ref, f32[256,256]{1,0:T(8,128)S(1)} %get-tuple-element.17.upper_ref), custom_call_target="tpu_custom_call" | custom-call | tf_op jit(solution)/shard_map/factor_two/pallas_call | solution.py:412
  90.4 5.7 %basis.1 = f32[12288,256]{1,0:T(8,128)} custom-call(s32[1]{0:T(128)} %get-tuple-element.18.small_ref, f32[12288,256]{1,0:T(8,128)S(1)} %get-tuple-element.19.f_ref, bf16[768,256]{1,0:T(8,128)(2,1)S(1)} %get-tuple-element.20.c_ref), custom_call_target="tpu_custom_call" | custom-call | tf_op jit(solution)/shard_map/basis/pallas_call | solution.py:231
  (9 shorter events, 0.1 us)
Async XLA Ops:
  8.6 2.4 %collective-permute-start = (f32[136,128]{1,0:T(8,128)S(1)}, f32[136,128]{1,0:T(8,128)S(1)}, u32[]{:S(2)}, u32[]{:S(2)}) collective-permute-start(f32[136,128]{1,0:T(8,128)S(1)} %get-tuple-element.13), channel_id=1, source_target_pairs={{0,1},{1,0},{2,3},{3,2},{4,5},{5,4},{6,7},{7,6},{8,9},{9,8},{10,11... | collective-permute-start | bytes 208904 | tf_op jit(solution)/shard_map/ppermute | solution.py:428
  11.0 4.8 %collective-permute-start.3 = (f32[136,128]{1,0:T(8,128)S(1)}, f32[136,128]{1,0:T(8,128)S(1)}, u32[]{:S(2)}, u32[]{:S(2)}) collective-permute-start(f32[136,128]{1,0:T(8,128)S(1)} %add.60), channel_id=1, source_target_pairs={{0,6},{1,7},{2,4},{3,5},{4,2},{5,3},{6,0},{7,1},{8,14},{9,15},{10,... | collective-permute-start | bytes 208904 | tf_op jit(solution)/shard_map/ppermute | solution.py:428
  13.6 4.7 %collective-permute-start.2 = (f32[136,128]{1,0:T(8,128)S(1)}, f32[136,128]{1,0:T(8,128)S(1)}, u32[]{:S(2)}, u32[]{:S(2)}) collective-permute-start(f32[136,128]{1,0:T(8,128)S(1)} %add.60), channel_id=1, source_target_pairs={{0,4},{1,5},{2,6},{3,7},{4,0},{5,1},{6,2},{7,3},{8,12},{9,13},{10,... | collective-permute-start | bytes 208904 | tf_op jit(solution)/shard_map/ppermute | solution.py:428
  14.2 4.1 %collective-permute-start.1 = (f32[136,128]{1,0:T(8,128)S(1)}, f32[136,128]{1,0:T(8,128)S(1)}, u32[]{:S(2)}, u32[]{:S(2)}) collective-permute-start(f32[136,128]{1,0:T(8,128)S(1)} %add.60), channel_id=1, source_target_pairs={{0,2},{1,3},{2,0},{3,1},{4,6},{5,7},{6,4},{7,5},{8,10},{9,11},{10,... | collective-permute-start | bytes 208904 | tf_op jit(solution)/shard_map/ppermute | solution.py:428
  18.3 5.8 %collective-permute-start.6 = (f32[136,128]{1,0:T(8,128)S(1)}, f32[136,128]{1,0:T(8,128)S(1)}, u32[]{:S(2)}, u32[]{:S(2)}) collective-permute-start(f32[136,128]{1,0:T(8,128)S(1)} %add_add_fusion.5), channel_id=1, source_target_pairs={{0,24},{8,16},{16,8},{24,0},{32,56},{40,48},{48,40},{56,32},{64,88... | collective-permute-start | bytes 208904 | tf_op jit(solution)/shard_map/ppermute | solution.py:428
  22.2 4.8 %collective-permute-start.5 = (f32[136,128]{1,0:T(8,128)S(1)}, f32[136,128]{1,0:T(8,128)S(1)}, u32[]{:S(2)}, u32[]{:S(2)}) collective-permute-start(f32[136,128]{1,0:T(8,128)S(1)} %add_add_fusion.5), channel_id=1, source_target_pairs={{0,16},{8,24},{16,0},{24,8},{32,48},{40,56},{48,32},{56,40},{64,80... | collective-permute-start | bytes 208904 | tf_op jit(solution)/shard_map/ppermute | solution.py:428
  22.2 4.8 %collective-permute-start.4 = (f32[136,128]{1,0:T(8,128)S(1)}, f32[136,128]{1,0:T(8,128)S(1)}, u32[]{:S(2)}, u32[]{:S(2)}) collective-permute-start(f32[136,128]{1,0:T(8,128)S(1)} %add_add_fusion.5), channel_id=1, source_target_pairs={{0,8},{8,0},{16,24},{24,16},{32,40},{40,32},{48,56},{56,48},{64,72... | collective-permute-start | bytes 208904 | tf_op jit(solution)/shard_map/ppermute | solution.py:428
  26.9 4.8 %collective-permute-start.9 = (f32[136,128]{1,0:T(8,128)S(1)}, f32[136,128]{1,0:T(8,128)S(1)}, u32[]{:S(2)}, u32[]{:S(2)}) collective-permute-start(f32[136,128]{1,0:T(8,128)S(1)} %add_add_fusion.4), channel_id=1, source_target_pairs={{0,96},{8,104},{16,112},{24,120},{32,64},{40,72},{48,80},{56,88},{... | collective-permute-start | bytes 208904 | tf_op jit(solution)/shard_map/ppermute | solution.py:428
  29.8 4.7 %collective-permute-start.8 = (f32[136,128]{1,0:T(8,128)S(1)}, f32[136,128]{1,0:T(8,128)S(1)}, u32[]{:S(2)}, u32[]{:S(2)}) collective-permute-start(f32[136,128]{1,0:T(8,128)S(1)} %add_add_fusion.4), channel_id=1, source_target_pairs={{0,64},{8,72},{16,80},{24,88},{32,96},{40,104},{48,112},{56,120},{... | collective-permute-start | bytes 208904 | tf_op jit(solution)/shard_map/ppermute | solution.py:428
  30.1 4.3 %collective-permute-start.7 = (f32[136,128]{1,0:T(8,128)S(1)}, f32[136,128]{1,0:T(8,128)S(1)}, u32[]{:S(2)}, u32[]{:S(2)}) collective-permute-start(f32[136,128]{1,0:T(8,128)S(1)} %add_add_fusion.4), channel_id=1, source_target_pairs={{0,32},{8,40},{16,48},{24,56},{32,0},{40,8},{48,16},{56,24},{64,96... | collective-permute-start | bytes 208904 | tf_op jit(solution)/shard_map/ppermute | solution.py:428
  34.4 5.9 %collective-permute-start.10 = (f32[136,128]{1,0:T(8,128)S(1)}, f32[136,128]{1,0:T(8,128)S(1)}, u32[]{:S(2)}, u32[]{:S(2)}) collective-permute-start(f32[136,128]{1,0:T(8,128)S(1)} %add_add_fusion.3.mine_ref), channel_id=1, source_target_pairs={{0,1},{1,0},{2,3},{3,2},{4,5},{5,4},{6,7},{7,6},{8,9},{9,8},{10,11... | collective-permute-start | bytes 208904 | tf_op jit(solution)/shard_map/ppermute | solution.py:428
  61.4 1.3 %collective-permute-start.11 = (f32[136,128]{1,0:T(8,128)S(1)}, f32[136,128]{1,0:T(8,128)S(1)}, u32[]{:S(2)}, u32[]{:S(2)}) collective-permute-start(f32[136,128]{1,0:T(8,128)S(1)} %get-tuple-element.16), channel_id=1, source_target_pairs={{0,1},{1,0},{2,3},{3,2},{4,5},{5,4},{6,7},{7,6},{8,9},{9,8},{10,11... | collective-permute-start | bytes 208904 | tf_op jit(solution)/shard_map/ppermute | solution.py:428
  62.8 4.5 %collective-permute-start.14 = (f32[136,128]{1,0:T(8,128)S(1)}, f32[136,128]{1,0:T(8,128)S(1)}, u32[]{:S(2)}, u32[]{:S(2)}) collective-permute-start(f32[136,128]{1,0:T(8,128)S(1)} %add.70), channel_id=1, source_target_pairs={{0,6},{1,7},{2,4},{3,5},{4,2},{5,3},{6,0},{7,1},{8,14},{9,15},{10,... | collective-permute-start | bytes 208904 | tf_op jit(solution)/shard_map/ppermute | solution.py:428
  63.9 4.8 %collective-permute-start.13 = (f32[136,128]{1,0:T(8,128)S(1)}, f32[136,128]{1,0:T(8,128)S(1)}, u32[]{:S(2)}, u32[]{:S(2)}) collective-permute-start(f32[136,128]{1,0:T(8,128)S(1)} %add.70), channel_id=1, source_target_pairs={{0,4},{1,5},{2,6},{3,7},{4,0},{5,1},{6,2},{7,3},{8,12},{9,13},{10,... | collective-permute-start | bytes 208904 | tf_op jit(solution)/shard_map/ppermute | solution.py:428
  64.8 4.5 %collective-permute-start.12 = (f32[136,128]{1,0:T(8,128)S(1)}, f32[136,128]{1,0:T(8,128)S(1)}, u32[]{:S(2)}, u32[]{:S(2)}) collective-permute-start(f32[136,128]{1,0:T(8,128)S(1)} %add.70), channel_id=1, source_target_pairs={{0,2},{1,3},{2,0},{3,1},{4,6},{5,7},{6,4},{7,5},{8,10},{9,11},{10,... | collective-permute-start | bytes 208904 | tf_op jit(solution)/shard_map/ppermute | solution.py:428
  69.3 4.5 %collective-permute-start.17 = (f32[136,128]{1,0:T(8,128)S(1)}, f32[136,128]{1,0:T(8,128)S(1)}, u32[]{:S(2)}, u32[]{:S(2)}) collective-permute-start(f32[136,128]{1,0:T(8,128)S(1)} %add_add_fusion.2), channel_id=1, source_target_pairs={{0,24},{8,16},{16,8},{24,0},{32,56},{40,48},{48,40},{56,32},{64,88... | collective-permute-start | bytes 208904 | tf_op jit(solution)/shard_map/ppermute | solution.py:428
  70.4 4.7 %collective-permute-start.16 = (f32[136,128]{1,0:T(8,128)S(1)}, f32[136,128]{1,0:T(8,128)S(1)}, u32[]{:S(2)}, u32[]{:S(2)}) collective-permute-start(f32[136,128]{1,0:T(8,128)S(1)} %add_add_fusion.2), channel_id=1, source_target_pairs={{0,16},{8,24},{16,0},{24,8},{32,48},{40,56},{48,32},{56,40},{64,80... | collective-permute-start | bytes 208904 | tf_op jit(solution)/shard_map/ppermute | solution.py:428
  71.2 4.1 %collective-permute-start.15 = (f32[136,128]{1,0:T(8,128)S(1)}, f32[136,128]{1,0:T(8,128)S(1)}, u32[]{:S(2)}, u32[]{:S(2)}) collective-permute-start(f32[136,128]{1,0:T(8,128)S(1)} %add_add_fusion.2), channel_id=1, source_target_pairs={{0,8},{8,0},{16,24},{24,16},{32,40},{40,32},{48,56},{56,48},{64,72... | collective-permute-start | bytes 208904 | tf_op jit(solution)/shard_map/ppermute | solution.py:428
  75.4 4.5 %collective-permute-start.20 = (f32[136,128]{1,0:T(8,128)S(1)}, f32[136,128]{1,0:T(8,128)S(1)}, u32[]{:S(2)}, u32[]{:S(2)}) collective-permute-start(f32[136,128]{1,0:T(8,128)S(1)} %add_add_fusion.1), channel_id=1, source_target_pairs={{0,96},{8,104},{16,112},{24,120},{32,64},{40,72},{48,80},{56,88},{... | collective-permute-start | bytes 208904 | tf_op jit(solution)/shard_map/ppermute | solution.py:428
  76.5 4.7 %collective-permute-start.19 = (f32[136,128]{1,0:T(8,128)S(1)}, f32[136,128]{1,0:T(8,128)S(1)}, u32[]{:S(2)}, u32[]{:S(2)}) collective-permute-start(f32[136,128]{1,0:T(8,128)S(1)} %add_add_fusion.1), channel_id=1, source_target_pairs={{0,64},{8,72},{16,80},{24,88},{32,96},{40,104},{48,112},{56,120},{... | collective-permute-start | bytes 208904 | tf_op jit(solution)/shard_map/ppermute | solution.py:428
  77.3 3.9 %collective-permute-start.18 = (f32[136,128]{1,0:T(8,128)S(1)}, f32[136,128]{1,0:T(8,128)S(1)}, u32[]{:S(2)}, u32[]{:S(2)}) collective-permute-start(f32[136,128]{1,0:T(8,128)S(1)} %add_add_fusion.1), channel_id=1, source_target_pairs={{0,32},{8,40},{16,48},{24,56},{32,0},{40,8},{48,16},{56,24},{64,96... | collective-permute-start | bytes 208904 | tf_op jit(solution)/shard_map/ppermute | solution.py:428
  81.2 5.0 %collective-permute-start.21 = (f32[136,128]{1,0:T(8,128)S(1)}, f32[136,128]{1,0:T(8,128)S(1)}, u32[]{:S(2)}, u32[]{:S(2)}) collective-permute-start(f32[136,128]{1,0:T(8,128)S(1)} %add_add_fusion.mine_ref), channel_id=1, source_target_pairs={{0,1},{1,0},{2,3},{3,2},{4,5},{5,4},{6,7},{7,6},{8,9},{9,8},{10,11... | collective-permute-start | bytes 208904 | tf_op jit(solution)/shard_map/ppermute | solution.py:428

commit v4 on v3

--- a/solution.py
+++ b/solution.py
@@ -243,67 +243,69 @@
 S = 8
 
 
-def eliminate(rows_a):
+def eliminate(rows_a, lane0):
     rows_a = list(rows_a)
     width = rows_a[0].shape[1]
     sub = lax.broadcasted_iota(jnp.int32, (S, H), 0)
+
+    def wide(v):
+        return jnp.concatenate([v] * (width // H), axis=1)
+
+    def columns(rows, s):
+        return [jnp.broadcast_to(rows[:, lane0 + S * s + k : lane0 + S * s + k + 1], (S, H)) for k in range(S)]
+
     for s in range(B // S):
-        cols = [jnp.broadcast_to(rows_a[s][:, S * s + k:S * s + k + 1], (S, H)) for k in range(S)]
         x = rows_a[s]
+        cols = columns(x, s)
         pivots, factors, us = [], [], []
+        scales = None
         for j in range(S):
-            r = jnp.broadcast_to(lax.rsqrt(cols[j][j:j + 1, :]), (S, H))
-            lj = jnp.where(sub >= j, cols[j] * r, 0.0)
+            r = jnp.broadcast_to(lax.rsqrt(cols[j][j : j + 1, :]), (S, H))
+            lj = cols[j] * r
             fac = [None] * S
             for k in range(j + 1, S):
-                fac[k] = jnp.broadcast_to(lj[k:k + 1, :], (S, H))
+                fac[k] = jnp.broadcast_to(lj[k : k + 1, :], (S, H))
                 cols[k] = cols[k] - lj * fac[k]
-            u = jnp.broadcast_to(x[j:j + 1, :], (S, width)) * jnp.concatenate([r] * (width // H), axis=1)
-            below = jnp.concatenate([jnp.where(sub > j, lj, 0.0)] * (width // H), axis=1)
-            here = jnp.concatenate([sub == j] * (width // H), axis=1)
-            x = jnp.where(here, u, x - below * u)
+            u = jnp.broadcast_to(x[j : j + 1, :], (S, width)) * wide(r)
+            if j < S - 1:
+                x = x - wide(jnp.where(sub > j, lj, 0.0)) * u
+            scales = r if scales is None else jnp.where(sub == j, r, scales)
             pivots.append(r)
             factors.append(fac)
             us.append(u)
-        rows_a[s] = x
+        rows_a[s] = x * wide(scales)
         for q in range(s + 1, B // S):
             y = rows_a[q]
-            c = [jnp.broadcast_to(y[:, S * s + k:S * s + k + 1], (S, H)) for k in range(S)]
+            c = columns(y, s)
             for j in range(S):
                 lj = c[j] * pivots[j]
                 for k in range(j + 1, S):
                     c[k] = c[k] - lj * factors[j][k]
-                y = y - jnp.concatenate([lj] * (width // H), axis=1) * us[j]
+                y = y - wide(lj) * us[j]
             rows_a[q] = y
-    return rows_a
+    return jnp.concatenate(rows_a, axis=0)
 
 
 def factorize(t_ref):
     for side in range(2):
         lanes = slice(side * H, side * H + 3 * H)
-        below = slice(side * H, K)
         width = K - side * H
-
-        def block(b, carry):
-            r0 = pl.multiple_of(b * B, B)
-            shift = r0 - side * H
-            r = t_ref[pl.ds(r0, B), lanes]
-            d = pltpu.roll(r[:, :H], lax.rem(H - shift, H), 1)
-            full = jnp.concatenate([d, r], axis=1)
-            out = eliminate([full[S * s : S * s + S] for s in range(B // S)])
-            u = jnp.concatenate([o[:, H:] for o in out], axis=0)
-            t_ref[pl.ds(r0, B), lanes] = u
-            lane = lax.broadcasted_iota(jnp.int32, (B, width), 1)
-            left = jnp.where(lane >= shift + B, u[:, :width], 0.0)
-            lh, lm, ll = split3(left)
+        for lane0 in range(0, H, B):
+            r0 = side * H + lane0
+            r = t_ref[r0 : r0 + B, lanes]
+            u = eliminate([r[S * s : S * s + S] for s in range(B // S)], lane0)
+            t_ref[r0 : r0 + B, lanes] = u
+            if r0 + B == K:
+                break
+            below = slice((r0 + B) // H * H, K)
+            left = u[:, below.start - side * H : width]
+            lane = lax.broadcasted_iota(jnp.int32, left.shape, 1) + below.start
+            lh, lm, ll = split3(jnp.where(lane >= r0 + B, left, 0.0))
             uh, um, ul = split3(u)
             t_ref[below, lanes] -= dot_tn(
                 jnp.concatenate([lh, lh, lm, lm, lh, ll], axis=0),
                 jnp.concatenate([uh, um, uh, um, ul, uh], axis=0),
             )
-            return carry
-
-        lax.fori_loop(side * (H // B), (side + 1) * (H // B), block, 0)
 
 
 def chol_one_kernel(mine_ref, other_ref, w_ref, upper_ref, t_ref):
@@ -349,8 +351,8 @@
     x_ref[...] = (g_ref[...] - eye) * half_low
 
     def x_more(state):
-        step, change = state
-        return jnp.logical_and(step < 10, jnp.logical_not(change <= TOL))
+        step, ahead = state
+        return jnp.logical_and(step < 10, jnp.logical_not(ahead <= TOL))
 
     def x_next(state):
         old = x_ref[...]
@@ -358,9 +360,10 @@
         square = dot_nt(jnp.concatenate([h, h, m], axis=1), jnp.concatenate([h, m, h], axis=1))
         new = (g_ref[...] - eye - square) * half_low
         x_ref[...] = new
-        return state[0] + 1, largest(new - old)
-
-    _, change = lax.while_loop(x_more, x_next, (jnp.int32(0), jnp.float32(1.0)))
+        rate = 2.0 * jnp.max(jnp.sum(jnp.abs(new), axis=1))
+        return state[0] + 1, jnp.where(rate <= 0.5, largest(new - old) * rate, 1.0)
+
+    _, ahead = lax.while_loop(x_more, x_next, (jnp.int32(0), jnp.float32(1.0)))
     x = x_ref[...]
     z_ref[...] = -x
 
@@ -385,7 +388,7 @@
 
     _, size = lax.while_loop(z_more, z_next, (jnp.int32(0), jnp.float32(1.0)))
     lowest = jnp.min(jnp.where(i == j, x, 0.0))
-    good = jnp.logical_and(jnp.logical_and(change <= TOL, size <= TOL), lowest > -0.5)
+    good = jnp.logical_and(jnp.logical_and(ahead <= TOL, size <= TOL), lowest > -0.5)
 
     @pl.when(jnp.logical_not(good))
     def _():

time: 96.4 us -> 94.7 us (0.982)
  Pallas kernels: 38.9 us -> 37.2 us
    pallas_call x1, Pallas kernels: 8.43 us -> 7.2 us  [chol_one_call(): pl.pallas_call(chol_one_kernel, out_shape=(jax.ShapeDtypeStruct((4 * K, K...]
where the time goes in v4:
time: 94.7 us; the launch traced here: 94.6 us
  Pallas kernels  37.2 us (39%)
  starting transfers between devices  32.4 us (34%)
  waiting for transfers between devices  24 us (25%)
    ppermute x22, starting transfers between devices, swap(): lax.ppermute(value, axis, [(i, i ^ distance) for i in range(lax.axis_size...  32.4 us
    ppermute x22, waiting for transfers between devices, swap(): lax.ppermute(value, axis, [(i, i ^ distance) for i in range(lax.axis_size...  24 us
    pallas_call x1, Pallas kernels, first_call(): pl.pallas_call(functools.partial(first_kernel, rows), out_shape=(jax.Shap...  12.6 us
    pallas_call x1, Pallas kernels, gram_call(): pl.pallas_call(functools.partial(gram_kernel, rows), out_shape=(half, hal...  7.95 us
    pallas_call x1, Pallas kernels, chol_one_call(): pl.pallas_call(chol_one_kernel, out_shape=(jax.ShapeDtypeStruct((4 * K, K...  7.2 us
    pallas_call x1, Pallas kernels, basis_call(): pl.pallas_call(functools.partial(basis_kernel, rows, scale), out_shape=ja...  5.71 us
    pallas_call x1, Pallas kernels, chol_two_call(): pl.pallas_call(functools.partial(chol_two_kernel, scale), out_shape=(jax....  3.71 us
  transfers between devices with their start and end apart: 22, of which 18 were waited for; matrix products, arithmetic and copies ran while one was open for 0% of the time, Pallas kernels for 0%

profile of v4, /device:TPU:1, one launch (start us, length us, event | category | flops | bytes accessed | tf_op | source)
XLA Modules:
  0.0 94.6 jit_solution(9254640750594734616)
XLA Ops:
  0.6 7.9 %gram_one.1 = (f32[136,128]{1,0:T(8,128)S(1)}, f32[136,128]{1,0:T(8,128)S(1)}) custom-call(f32[12288,256]{1,0:T(8,128)} %x_hbm.3), custom_call_target="tpu_custom_call" | custom-call | tf_op jit(solution)/shard_map/gram_one/pallas_call | solution.py:127
  8.6 1.5 %collective-permute-start = (f32[136,128]{1,0:T(8,128)S(1)}, f32[136,128]{1,0:T(8,128)S(1)}, u32[]{:S(2)}, u32[]{:S(2)}) collective-permute-start(f32[136,128]{1,0:T(8,128)S(1)} %get-tuple-element.13), channel_id=1, source_target_pairs={{0,1},{1,0},{2,3},{3,2},{4,5},{5,4},{6,7},{7,6},{8,9},{9,8},{10,11... | collective-permute-start | bytes 208904 | tf_op jit(solution)/shard_map/ppermute | solution.py:431
  10.0 0.9 collective-permute-done
  11.0 2.7 %collective-permute-start.3 = (f32[136,128]{1,0:T(8,128)S(1)}, f32[136,128]{1,0:T(8,128)S(1)}, u32[]{:S(2)}, u32[]{:S(2)}) collective-permute-start(f32[136,128]{1,0:T(8,128)S(1)} %add.60), channel_id=1, source_target_pairs={{0,6},{1,7},{2,4},{3,5},{4,2},{5,3},{6,0},{7,1},{8,14},{9,15},{10,... | collective-permute-start | bytes 208904 | tf_op jit(solution)/shard_map/ppermute | solution.py:431
  13.6 0.5 collective-permute-start.2
  14.2 0.1 collective-permute-start.1
  14.3 1.4 %collective-permute-done.3 = f32[136,128]{1,0:T(8,128)S(1)} collective-permute-done((f32[136,128]{1,0:T(8,128)S(1)}, f32[136,128]{1,0:T(8,128)S(1)}, u32[]{:S(2)}, u32[]{:S(2)}) %collective-permute-start.3) | collective-permute-done | bytes 69664 | tf_op jit(solution)/shard_map/ppermute | solution.py:431
  15.7 2.5 %collective-permute-done.2 = f32[136,128]{1,0:T(8,128)S(1)} collective-permute-done((f32[136,128]{1,0:T(8,128)S(1)}, f32[136,128]{1,0:T(8,128)S(1)}, u32[]{:S(2)}, u32[]{:S(2)}) %collective-permute-start.2) | collective-permute-done | bytes 69664 | tf_op jit(solution)/shard_map/ppermute | solution.py:431
  18.3 0.0 collective-permute-done.1
  18.3 3.8 %collective-permute-start.6 = (f32[136,128]{1,0:T(8,128)S(1)}, f32[136,128]{1,0:T(8,128)S(1)}, u32[]{:S(2)}, u32[]{:S(2)}) collective-permute-start(f32[136,128]{1,0:T(8,128)S(1)} %add_add_fusion.5), channel_id=1, source_target_pairs={{0,24},{8,16},{16,8},{24,0},{32,56},{40,48},{48,40},{56,32},{64,88... | collective-permute-start | bytes 208904 | tf_op jit(solution)/shard_map/ppermute | solution.py:431
  22.2 0.0 collective-permute-start.5
  22.2 0.7 collective-permute-start.4
  22.8 1.3 %collective-permute-done.6 = f32[136,128]{1,0:T(8,128)S(1)} collective-permute-done((f32[136,128]{1,0:T(8,128)S(1)}, f32[136,128]{1,0:T(8,128)S(1)}, u32[]{:S(2)}, u32[]{:S(2)}) %collective-permute-start.6) | collective-permute-done | bytes 69664 | tf_op jit(solution)/shard_map/ppermute | solution.py:431
  24.2 2.8 %collective-permute-done.5 = f32[136,128]{1,0:T(8,128)S(1)} collective-permute-done((f32[136,128]{1,0:T(8,128)S(1)}, f32[136,128]{1,0:T(8,128)S(1)}, u32[]{:S(2)}, u32[]{:S(2)}) %collective-permute-start.5) | collective-permute-done | bytes 69664 | tf_op jit(solution)/shard_map/ppermute | solution.py:431
  26.9 0.0 collective-permute-done.4
  26.9 2.8 %collective-permute-start.9 = (f32[136,128]{1,0:T(8,128)S(1)}, f32[136,128]{1,0:T(8,128)S(1)}, u32[]{:S(2)}, u32[]{:S(2)}) collective-permute-start(f32[136,128]{1,0:T(8,128)S(1)} %add_add_fusion.4), channel_id=1, source_target_pairs={{0,96},{8,104},{16,112},{24,120},{32,64},{40,72},{48,80},{56,88},{... | collective-permute-start | bytes 208904 | tf_op jit(solution)/shard_map/ppermute | solution.py:431
  29.8 0.4 collective-permute-start.8
  30.1 0.3 collective-permute-start.7
  30.4 1.3 %collective-permute-done.9 = f32[136,128]{1,0:T(8,128)S(1)} collective-permute-done((f32[136,128]{1,0:T(8,128)S(1)}, f32[136,128]{1,0:T(8,128)S(1)}, u32[]{:S(2)}, u32[]{:S(2)}) %collective-permute-start.9) | collective-permute-done | bytes 69664 | tf_op jit(solution)/shard_map/ppermute | solution.py:431
  31.8 2.7 %collective-permute-done.8 = f32[136,128]{1,0:T(8,128)S(1)} collective-permute-done((f32[136,128]{1,0:T(8,128)S(1)}, f32[136,128]{1,0:T(8,128)S(1)}, u32[]{:S(2)}, u32[]{:S(2)}) %collective-permute-start.8) | collective-permute-done | bytes 69664 | tf_op jit(solution)/shard_map/ppermute | solution.py:431
  34.4 5.0 %collective-permute-start.10 = (f32[136,128]{1,0:T(8,128)S(1)}, f32[136,128]{1,0:T(8,128)S(1)}, u32[]{:S(2)}, u32[]{:S(2)}) collective-permute-start(f32[136,128]{1,0:T(8,128)S(1)} %add_add_fusion.3.mine_ref), channel_id=1, source_target_pairs={{0,1},{1,0},{2,3},{3,2},{4,5},{5,4},{6,7},{7,6},{8,9},{9,8},{10,11... | collective-permute-start | bytes 208904 | tf_op jit(solution)/shard_map/ppermute | solution.py:431
  39.5 0.9 collective-permute-done.10.other_ref
  40.4 7.2 %factor_one.1 = (bf16[1024,256]{1,0:T(8,128)(2,1)S(1)}, f32[256,256]{1,0:T(8,128)S(1)}) custom-call(f32[136,128]{1,0:T(8,128)S(1)} %add_add_fusion.3.mine_ref, f32[136,128]{1,0:T(8,128)S(1)} %collective-permute-done.10.other_ref), custom_call_target="tpu_custom_call" | custom-call | tf_op jit(solution)/shard_map/factor_one/pallas_call | solution.py:326
  47.6 12.6 %first_and_gram_two.1 = (f32[12288,256]{1,0:T(8,128)S(1)}, f32[136,128]{1,0:T(8,128)S(1)}, f32[136,128]{1,0:T(8,128)S(1)}) custom-call(f32[12288,256]{1,0:T(8,128)} %x_hbm.3, bf16[1024,256]{1,0:T(8,128)(2,1)S(1)} %get-tuple-element.14.w_ref), custom_call_target="tpu_custom_call" | custom-call | tf_op jit(solution)/shard_map/first_and_gram_two/pallas_call | solution.py:178
  60.2 0.4 collective-permute-start.11
  60.6 0.9 collective-permute-done.11
  61.6 1.1 %collective-permute-start.14 = (f32[136,128]{1,0:T(8,128)S(1)}, f32[136,128]{1,0:T(8,128)S(1)}, u32[]{:S(2)}, u32[]{:S(2)}) collective-permute-start(f32[136,128]{1,0:T(8,128)S(1)} %add.70), channel_id=1, source_target_pairs={{0,6},{1,7},{2,4},{3,5},{4,2},{5,3},{6,0},{7,1},{8,14},{9,15},{10,... | collective-permute-start | bytes 208904 | tf_op jit(solution)/shard_map/ppermute | solution.py:431
  62.7 0.9 collective-permute-start.13
  63.5 1.4 %collective-permute-start.12 = (f32[136,128]{1,0:T(8,128)S(1)}, f32[136,128]{1,0:T(8,128)S(1)}, u32[]{:S(2)}, u32[]{:S(2)}) collective-permute-start(f32[136,128]{1,0:T(8,128)S(1)} %add.70), channel_id=1, source_target_pairs={{0,2},{1,3},{2,0},{3,1},{4,6},{5,7},{6,4},{7,5},{8,10},{9,11},{10,... | collective-permute-start | bytes 208904 | tf_op jit(solution)/shard_map/ppermute | solution.py:431
  64.9 1.1 %collective-permute-done.14 = f32[136,128]{1,0:T(8,128)S(1)} collective-permute-done((f32[136,128]{1,0:T(8,128)S(1)}, f32[136,128]{1,0:T(8,128)S(1)}, u32[]{:S(2)}, u32[]{:S(2)}) %collective-permute-start.14) | collective-permute-done | bytes 69664 | tf_op jit(solution)/shard_map/ppermute | solution.py:431
  66.0 1.4 %collective-permute-done.13 = f32[136,128]{1,0:T(8,128)S(1)} collective-permute-done((f32[136,128]{1,0:T(8,128)S(1)}, f32[136,128]{1,0:T(8,128)S(1)}, u32[]{:S(2)}, u32[]{:S(2)}) %collective-permute-start.13) | collective-permute-done | bytes 69664 | tf_op jit(solution)/shard_map/ppermute | solution.py:431
  67.4 0.6 collective-permute-done.12
  68.1 1.1 %collective-permute-start.17 = (f32[136,128]{1,0:T(8,128)S(1)}, f32[136,128]{1,0:T(8,128)S(1)}, u32[]{:S(2)}, u32[]{:S(2)}) collective-permute-start(f32[136,128]{1,0:T(8,128)S(1)} %add_add_fusion.2), channel_id=1, source_target_pairs={{0,24},{8,16},{16,8},{24,0},{32,56},{40,48},{48,40},{56,32},{64,88... | collective-permute-start | bytes 208904 | tf_op jit(solution)/shard_map/ppermute | solution.py:431
  69.2 1.0 %collective-permute-start.16 = (f32[136,128]{1,0:T(8,128)S(1)}, f32[136,128]{1,0:T(8,128)S(1)}, u32[]{:S(2)}, u32[]{:S(2)}) collective-permute-start(f32[136,128]{1,0:T(8,128)S(1)} %add_add_fusion.2), channel_id=1, source_target_pairs={{0,16},{8,24},{16,0},{24,8},{32,48},{40,56},{48,32},{56,40},{64,80... | collective-permute-start | bytes 208904 | tf_op jit(solution)/shard_map/ppermute | solution.py:431
  70.1 1.2 %collective-permute-start.15 = (f32[136,128]{1,0:T(8,128)S(1)}, f32[136,128]{1,0:T(8,128)S(1)}, u32[]{:S(2)}, u32[]{:S(2)}) collective-permute-start(f32[136,128]{1,0:T(8,128)S(1)} %add_add_fusion.2), channel_id=1, source_target_pairs={{0,8},{8,0},{16,24},{24,16},{32,40},{40,32},{48,56},{56,48},{64,72... | collective-permute-start | bytes 208904 | tf_op jit(solution)/shard_map/ppermute | solution.py:431
  71.4 1.1 %collective-permute-done.17 = f32[136,128]{1,0:T(8,128)S(1)} collective-permute-done((f32[136,128]{1,0:T(8,128)S(1)}, f32[136,128]{1,0:T(8,128)S(1)}, u32[]{:S(2)}, u32[]{:S(2)}) %collective-permute-start.17) | collective-permute-done | bytes 69664 | tf_op jit(solution)/shard_map/ppermute | solution.py:431
  72.5 1.3 %collective-permute-done.16 = f32[136,128]{1,0:T(8,128)S(1)} collective-permute-done((f32[136,128]{1,0:T(8,128)S(1)}, f32[136,128]{1,0:T(8,128)S(1)}, u32[]{:S(2)}, u32[]{:S(2)}) %collective-permute-start.16) | collective-permute-done | bytes 69664 | tf_op jit(solution)/shard_map/ppermute | solution.py:431
  73.8 0.3 collective-permute-done.15
  74.1 1.1 %collective-permute-start.20 = (f32[136,128]{1,0:T(8,128)S(1)}, f32[136,128]{1,0:T(8,128)S(1)}, u32[]{:S(2)}, u32[]{:S(2)}) collective-permute-start(f32[136,128]{1,0:T(8,128)S(1)} %add_add_fusion.1), channel_id=1, source_target_pairs={{0,96},{8,104},{16,112},{24,120},{32,64},{40,72},{48,80},{56,88},{... | collective-permute-start | bytes 208904 | tf_op jit(solution)/shard_map/ppermute | solution.py:431
  75.2 0.8 collective-permute-start.19
  76.1 1.4 %collective-permute-start.18 = (f32[136,128]{1,0:T(8,128)S(1)}, f32[136,128]{1,0:T(8,128)S(1)}, u32[]{:S(2)}, u32[]{:S(2)}) collective-permute-start(f32[136,128]{1,0:T(8,128)S(1)} %add_add_fusion.1), channel_id=1, source_target_pairs={{0,32},{8,40},{16,48},{24,56},{32,0},{40,8},{48,16},{56,24},{64,96... | collective-permute-start | bytes 208904 | tf_op jit(solution)/shard_map/ppermute | solution.py:431
  77.5 1.1 %collective-permute-done.20 = f32[136,128]{1,0:T(8,128)S(1)} collective-permute-done((f32[136,128]{1,0:T(8,128)S(1)}, f32[136,128]{1,0:T(8,128)S(1)}, u32[]{:S(2)}, u32[]{:S(2)}) %collective-permute-start.20) | collective-permute-done | bytes 69664 | tf_op jit(solution)/shard_map/ppermute | solution.py:431
  78.6 1.3 %collective-permute-done.19 = f32[136,128]{1,0:T(8,128)S(1)} collective-permute-done((f32[136,128]{1,0:T(8,128)S(1)}, f32[136,128]{1,0:T(8,128)S(1)}, u32[]{:S(2)}, u32[]{:S(2)}) %collective-permute-start.19) | collective-permute-done | bytes 69664 | tf_op jit(solution)/shard_map/ppermute | solution.py:431
  79.9 0.0 collective-permute-done.18
  79.9 4.1 %collective-permute-start.21 = (f32[136,128]{1,0:T(8,128)S(1)}, f32[136,128]{1,0:T(8,128)S(1)}, u32[]{:S(2)}, u32[]{:S(2)}) collective-permute-start(f32[136,128]{1,0:T(8,128)S(1)} %add_add_fusion.mine_ref), channel_id=1, source_target_pairs={{0,1},{1,0},{2,3},{3,2},{4,5},{5,4},{6,7},{7,6},{8,9},{9,8},{10,11... | collective-permute-start | bytes 208904 | tf_op jit(solution)/shard_map/ppermute | solution.py:431
  84.1 0.9 collective-permute-done.21.other_ref
  85.0 3.7 %factor_two.1 = (s32[1]{0:T(128)}, bf16[768,256]{1,0:T(8,128)(2,1)S(1)}, f32[256,256]{1,0:T(8,128)}) custom-call(f32[136,128]{1,0:T(8,128)S(1)} %add_add_fusion.mine_ref, f32[136,128]{1,0:T(8,128)S(1)} %collective-permute-done.21.other_ref, f32[256,256]{1,0:T(8,128)S(1)} %get-tuple-element.17.upper_ref), custom_call_target="tpu_custom_call" | custom-call | tf_op jit(solution)/shard_map/factor_two/pallas_call | solution.py:415
  88.7 5.7 %basis.1 = f32[12288,256]{1,0:T(8,128)} custom-call(s32[1]{0:T(128)} %get-tuple-element.18.small_ref, f32[12288,256]{1,0:T(8,128)S(1)} %get-tuple-element.19.f_ref, bf16[768,256]{1,0:T(8,128)(2,1)S(1)} %get-tuple-element.20.c_ref), custom_call_target="tpu_custom_call" | custom-call | tf_op jit(solution)/shard_map/basis/pallas_call | solution.py:231
  (9 shorter events, 0.1 us)
Async XLA Ops:
  8.6 2.4 %collective-permute-start = (f32[136,128]{1,0:T(8,128)S(1)}, f32[136,128]{1,0:T(8,128)S(1)}, u32[]{:S(2)}, u32[]{:S(2)}) collective-permute-start(f32[136,128]{1,0:T(8,128)S(1)} %get-tuple-element.13), channel_id=1, source_target_pairs={{0,1},{1,0},{2,3},{3,2},{4,5},{5,4},{6,7},{7,6},{8,9},{9,8},{10,11... | collective-permute-start | bytes 208904 | tf_op jit(solution)/shard_map/ppermute | solution.py:431
  11.0 4.8 %collective-permute-start.3 = (f32[136,128]{1,0:T(8,128)S(1)}, f32[136,128]{1,0:T(8,128)S(1)}, u32[]{:S(2)}, u32[]{:S(2)}) collective-permute-start(f32[136,128]{1,0:T(8,128)S(1)} %add.60), channel_id=1, source_target_pairs={{0,6},{1,7},{2,4},{3,5},{4,2},{5,3},{6,0},{7,1},{8,14},{9,15},{10,... | collective-permute-start | bytes 208904 | tf_op jit(solution)/shard_map/ppermute | solution.py:431
  13.6 4.7 %collective-permute-start.2 = (f32[136,128]{1,0:T(8,128)S(1)}, f32[136,128]{1,0:T(8,128)S(1)}, u32[]{:S(2)}, u32[]{:S(2)}) collective-permute-start(f32[136,128]{1,0:T(8,128)S(1)} %add.60), channel_id=1, source_target_pairs={{0,4},{1,5},{2,6},{3,7},{4,0},{5,1},{6,2},{7,3},{8,12},{9,13},{10,... | collective-permute-start | bytes 208904 | tf_op jit(solution)/shard_map/ppermute | solution.py:431
  14.2 4.1 %collective-permute-start.1 = (f32[136,128]{1,0:T(8,128)S(1)}, f32[136,128]{1,0:T(8,128)S(1)}, u32[]{:S(2)}, u32[]{:S(2)}) collective-permute-start(f32[136,128]{1,0:T(8,128)S(1)} %add.60), channel_id=1, source_target_pairs={{0,2},{1,3},{2,0},{3,1},{4,6},{5,7},{6,4},{7,5},{8,10},{9,11},{10,... | collective-permute-start | bytes 208904 | tf_op jit(solution)/shard_map/ppermute | solution.py:431
  18.3 5.8 %collective-permute-start.6 = (f32[136,128]{1,0:T(8,128)S(1)}, f32[136,128]{1,0:T(8,128)S(1)}, u32[]{:S(2)}, u32[]{:S(2)}) collective-permute-start(f32[136,128]{1,0:T(8,128)S(1)} %add_add_fusion.5), channel_id=1, source_target_pairs={{0,24},{8,16},{16,8},{24,0},{32,56},{40,48},{48,40},{56,32},{64,88... | collective-permute-start | bytes 208904 | tf_op jit(solution)/shard_map/ppermute | solution.py:431
  22.2 4.8 %collective-permute-start.5 = (f32[136,128]{1,0:T(8,128)S(1)}, f32[136,128]{1,0:T(8,128)S(1)}, u32[]{:S(2)}, u32[]{:S(2)}) collective-permute-start(f32[136,128]{1,0:T(8,128)S(1)} %add_add_fusion.5), channel_id=1, source_target_pairs={{0,16},{8,24},{16,0},{24,8},{32,48},{40,56},{48,32},{56,40},{64,80... | collective-permute-start | bytes 208904 | tf_op jit(solution)/shard_map/ppermute | solution.py:431
  22.2 4.8 %collective-permute-start.4 = (f32[136,128]{1,0:T(8,128)S(1)}, f32[136,128]{1,0:T(8,128)S(1)}, u32[]{:S(2)}, u32[]{:S(2)}) collective-permute-start(f32[136,128]{1,0:T(8,128)S(1)} %add_add_fusion.5), channel_id=1, source_target_pairs={{0,8},{8,0},{16,24},{24,16},{32,40},{40,32},{48,56},{56,48},{64,72... | collective-permute-start | bytes 208904 | tf_op jit(solution)/shard_map/ppermute | solution.py:431
  26.9 4.8 %collective-permute-start.9 = (f32[136,128]{1,0:T(8,128)S(1)}, f32[136,128]{1,0:T(8,128)S(1)}, u32[]{:S(2)}, u32[]{:S(2)}) collective-permute-start(f32[136,128]{1,0:T(8,128)S(1)} %add_add_fusion.4), channel_id=1, source_target_pairs={{0,96},{8,104},{16,112},{24,120},{32,64},{40,72},{48,80},{56,88},{... | collective-permute-start | bytes 208904 | tf_op jit(solution)/shard_map/ppermute | solution.py:431
  29.8 4.7 %collective-permute-start.8 = (f32[136,128]{1,0:T(8,128)S(1)}, f32[136,128]{1,0:T(8,128)S(1)}, u32[]{:S(2)}, u32[]{:S(2)}) collective-permute-start(f32[136,128]{1,0:T(8,128)S(1)} %add_add_fusion.4), channel_id=1, source_target_pairs={{0,64},{8,72},{16,80},{24,88},{32,96},{40,104},{48,112},{56,120},{... | collective-permute-start | bytes 208904 | tf_op jit(solution)/shard_map/ppermute | solution.py:431
  30.1 4.3 %collective-permute-start.7 = (f32[136,128]{1,0:T(8,128)S(1)}, f32[136,128]{1,0:T(8,128)S(1)}, u32[]{:S(2)}, u32[]{:S(2)}) collective-permute-start(f32[136,128]{1,0:T(8,128)S(1)} %add_add_fusion.4), channel_id=1, source_target_pairs={{0,32},{8,40},{16,48},{24,56},{32,0},{40,8},{48,16},{56,24},{64,96... | collective-permute-start | bytes 208904 | tf_op jit(solution)/shard_map/ppermute | solution.py:431
  34.4 5.9 %collective-permute-start.10 = (f32[136,128]{1,0:T(8,128)S(1)}, f32[136,128]{1,0:T(8,128)S(1)}, u32[]{:S(2)}, u32[]{:S(2)}) collective-permute-start(f32[136,128]{1,0:T(8,128)S(1)} %add_add_fusion.3.mine_ref), channel_id=1, source_target_pairs={{0,1},{1,0},{2,3},{3,2},{4,5},{5,4},{6,7},{7,6},{8,9},{9,8},{10,11... | collective-permute-start | bytes 208904 | tf_op jit(solution)/shard_map/ppermute | solution.py:431
  60.2 1.3 %collective-permute-start.11 = (f32[136,128]{1,0:T(8,128)S(1)}, f32[136,128]{1,0:T(8,128)S(1)}, u32[]{:S(2)}, u32[]{:S(2)}) collective-permute-start(f32[136,128]{1,0:T(8,128)S(1)} %get-tuple-element.16), channel_id=1, source_target_pairs={{0,1},{1,0},{2,3},{3,2},{4,5},{5,4},{6,7},{7,6},{8,9},{9,8},{10,11... | collective-permute-start | bytes 208904 | tf_op jit(solution)/shard_map/ppermute | solution.py:431
  61.6 4.5 %collective-permute-start.14 = (f32[136,128]{1,0:T(8,128)S(1)}, f32[136,128]{1,0:T(8,128)S(1)}, u32[]{:S(2)}, u32[]{:S(2)}) collective-permute-start(f32[136,128]{1,0:T(8,128)S(1)} %add.70), channel_id=1, source_target_pairs={{0,6},{1,7},{2,4},{3,5},{4,2},{5,3},{6,0},{7,1},{8,14},{9,15},{10,... | collective-permute-start | bytes 208904 | tf_op jit(solution)/shard_map/ppermute | solution.py:431
  62.7 4.8 %collective-permute-start.13 = (f32[136,128]{1,0:T(8,128)S(1)}, f32[136,128]{1,0:T(8,128)S(1)}, u32[]{:S(2)}, u32[]{:S(2)}) collective-permute-start(f32[136,128]{1,0:T(8,128)S(1)} %add.70), channel_id=1, source_target_pairs={{0,4},{1,5},{2,6},{3,7},{4,0},{5,1},{6,2},{7,3},{8,12},{9,13},{10,... | collective-permute-start | bytes 208904 | tf_op jit(solution)/shard_map/ppermute | solution.py:431
  63.5 4.5 %collective-permute-start.12 = (f32[136,128]{1,0:T(8,128)S(1)}, f32[136,128]{1,0:T(8,128)S(1)}, u32[]{:S(2)}, u32[]{:S(2)}) collective-permute-start(f32[136,128]{1,0:T(8,128)S(1)} %add.70), channel_id=1, source_target_pairs={{0,2},{1,3},{2,0},{3,1},{4,6},{5,7},{6,4},{7,5},{8,10},{9,11},{10,... | collective-permute-start | bytes 208904 | tf_op jit(solution)/shard_map/ppermute | solution.py:431
  68.1 4.5 %collective-permute-start.17 = (f32[136,128]{1,0:T(8,128)S(1)}, f32[136,128]{1,0:T(8,128)S(1)}, u32[]{:S(2)}, u32[]{:S(2)}) collective-permute-start(f32[136,128]{1,0:T(8,128)S(1)} %add_add_fusion.2), channel_id=1, source_target_pairs={{0,24},{8,16},{16,8},{24,0},{32,56},{40,48},{48,40},{56,32},{64,88... | collective-permute-start | bytes 208904 | tf_op jit(solution)/shard_map/ppermute | solution.py:431
  69.2 4.7 %collective-permute-start.16 = (f32[136,128]{1,0:T(8,128)S(1)}, f32[136,128]{1,0:T(8,128)S(1)}, u32[]{:S(2)}, u32[]{:S(2)}) collective-permute-start(f32[136,128]{1,0:T(8,128)S(1)} %add_add_fusion.2), channel_id=1, source_target_pairs={{0,16},{8,24},{16,0},{24,8},{32,48},{40,56},{48,32},{56,40},{64,80... | collective-permute-start | bytes 208904 | tf_op jit(solution)/shard_map/ppermute | solution.py:431
  70.1 4.0 %collective-permute-start.15 = (f32[136,128]{1,0:T(8,128)S(1)}, f32[136,128]{1,0:T(8,128)S(1)}, u32[]{:S(2)}, u32[]{:S(2)}) collective-permute-start(f32[136,128]{1,0:T(8,128)S(1)} %add_add_fusion.2), channel_id=1, source_target_pairs={{0,8},{8,0},{16,24},{24,16},{32,40},{40,32},{48,56},{56,48},{64,72... | collective-permute-start | bytes 208904 | tf_op jit(solution)/shard_map/ppermute | solution.py:431
  74.1 4.5 %collective-permute-start.20 = (f32[136,128]{1,0:T(8,128)S(1)}, f32[136,128]{1,0:T(8,128)S(1)}, u32[]{:S(2)}, u32[]{:S(2)}) collective-permute-start(f32[136,128]{1,0:T(8,128)S(1)} %add_add_fusion.1), channel_id=1, source_target_pairs={{0,96},{8,104},{16,112},{24,120},{32,64},{40,72},{48,80},{56,88},{... | collective-permute-start | bytes 208904 | tf_op jit(solution)/shard_map/ppermute | solution.py:431
  75.2 4.7 %collective-permute-start.19 = (f32[136,128]{1,0:T(8,128)S(1)}, f32[136,128]{1,0:T(8,128)S(1)}, u32[]{:S(2)}, u32[]{:S(2)}) collective-permute-start(f32[136,128]{1,0:T(8,128)S(1)} %add_add_fusion.1), channel_id=1, source_target_pairs={{0,64},{8,72},{16,80},{24,88},{32,96},{40,104},{48,112},{56,120},{... | collective-permute-start | bytes 208904 | tf_op jit(solution)/shard_map/ppermute | solution.py:431
  76.1 3.9 %collective-permute-start.18 = (f32[136,128]{1,0:T(8,128)S(1)}, f32[136,128]{1,0:T(8,128)S(1)}, u32[]{:S(2)}, u32[]{:S(2)}) collective-permute-start(f32[136,128]{1,0:T(8,128)S(1)} %add_add_fusion.1), channel_id=1, source_target_pairs={{0,32},{8,40},{16,48},{24,56},{32,0},{40,8},{48,16},{56,24},{64,96... | collective-permute-start | bytes 208904 | tf_op jit(solution)/shard_map/ppermute | solution.py:431
  79.9 5.0 %collective-permute-start.21 = (f32[136,128]{1,0:T(8,128)S(1)}, f32[136,128]{1,0:T(8,128)S(1)}, u32[]{:S(2)}, u32[]{:S(2)}) collective-permute-start(f32[136,128]{1,0:T(8,128)S(1)} %add_add_fusion.mine_ref), channel_id=1, source_target_pairs={{0,1},{1,0},{2,3},{3,2},{4,5},{5,4},{6,7},{7,6},{8,9},{9,8},{10,11... | collective-permute-start | bytes 208904 | tf_op jit(solution)/shard_map/ppermute | solution.py:431

commit v5 on v4

--- a/solution.py
+++ b/solution.py
@@ -444,7 +444,7 @@
     return value, swap(value, "col", 1)
 
 
-ROWS_PER_STEP = 2048
+ROWS_PER_STEP = 1536
 FIRST_ROWS_PER_STEP = 3072
 BASIS_ROWS_PER_STEP = 1536
 

time: 94.7 us -> 95 us (level)
  no operation moved by 1% of the time
where the time goes in v5:
time: 95 us; the launch traced here: 94.8 us
  Pallas kernels  37.5 us (39%)
  starting transfers between devices  32.4 us (34%)
  waiting for transfers between devices  24 us (25%)
    ppermute x22, starting transfers between devices, swap(): lax.ppermute(value, axis, [(i, i ^ distance) for i in range(lax.axis_size...  32.4 us
    ppermute x22, waiting for transfers between devices, swap(): lax.ppermute(value, axis, [(i, i ^ distance) for i in range(lax.axis_size...  24 us
    pallas_call x1, Pallas kernels, first_call(): pl.pallas_call(functools.partial(first_kernel, rows), out_shape=(jax.Shap...  12.6 us
    pallas_call x1, Pallas kernels, gram_call(): pl.pallas_call(functools.partial(gram_kernel, rows), out_shape=(half, hal...  8.22 us
    pallas_call x1, Pallas kernels, chol_one_call(): pl.pallas_call(chol_one_kernel, out_shape=(jax.ShapeDtypeStruct((4 * K, K...  7.2 us
    pallas_call x1, Pallas kernels, basis_call(): pl.pallas_call(functools.partial(basis_kernel, rows, scale), out_shape=ja...  5.72 us
    pallas_call x1, Pallas kernels, chol_two_call(): pl.pallas_call(functools.partial(chol_two_kernel, scale), out_shape=(jax....  3.71 us
  transfers between devices with their start and end apart: 22, of which 18 were waited for; matrix products, arithmetic and copies ran while one was open for 0% of the time, Pallas kernels for 0%

profile of v5, /device:TPU:1, one launch (start us, length us, event | category | flops | bytes accessed | tf_op | source)
XLA Modules:
  0.0 94.8 jit_solution(14031065370353036638)
XLA Ops:
  0.6 8.2 %gram_one.1 = (f32[136,128]{1,0:T(8,128)S(1)}, f32[136,128]{1,0:T(8,128)S(1)}) custom-call(f32[12288,256]{1,0:T(8,128)} %x_hbm.3), custom_call_target="tpu_custom_call" | custom-call | tf_op jit(solution)/shard_map/gram_one/pallas_call | solution.py:127
  8.9 1.5 %collective-permute-start = (f32[136,128]{1,0:T(8,128)S(1)}, f32[136,128]{1,0:T(8,128)S(1)}, u32[]{:S(2)}, u32[]{:S(2)}) collective-permute-start(f32[136,128]{1,0:T(8,128)S(1)} %get-tuple-element.13), channel_id=1, source_target_pairs={{0,1},{1,0},{2,3},{3,2},{4,5},{5,4},{6,7},{7,6},{8,9},{9,8},{10,11... | collective-permute-start | bytes 208904 | tf_op jit(solution)/shard_map/ppermute | solution.py:431
  10.3 0.9 collective-permute-done
  11.2 2.7 %collective-permute-start.3 = (f32[136,128]{1,0:T(8,128)S(1)}, f32[136,128]{1,0:T(8,128)S(1)}, u32[]{:S(2)}, u32[]{:S(2)}) collective-permute-start(f32[136,128]{1,0:T(8,128)S(1)} %add.60), channel_id=1, source_target_pairs={{0,6},{1,7},{2,4},{3,5},{4,2},{5,3},{6,0},{7,1},{8,14},{9,15},{10,... | collective-permute-start | bytes 208904 | tf_op jit(solution)/shard_map/ppermute | solution.py:431
  13.9 0.5 collective-permute-start.2
  14.4 0.2 collective-permute-start.1
  14.6 1.4 %collective-permute-done.3 = f32[136,128]{1,0:T(8,128)S(1)} collective-permute-done((f32[136,128]{1,0:T(8,128)S(1)}, f32[136,128]{1,0:T(8,128)S(1)}, u32[]{:S(2)}, u32[]{:S(2)}) %collective-permute-start.3) | collective-permute-done | bytes 69664 | tf_op jit(solution)/shard_map/ppermute | solution.py:431
  16.0 2.5 %collective-permute-done.2 = f32[136,128]{1,0:T(8,128)S(1)} collective-permute-done((f32[136,128]{1,0:T(8,128)S(1)}, f32[136,128]{1,0:T(8,128)S(1)}, u32[]{:S(2)}, u32[]{:S(2)}) %collective-permute-start.2) | collective-permute-done | bytes 69664 | tf_op jit(solution)/shard_map/ppermute | solution.py:431
  18.6 0.0 collective-permute-done.1
  18.6 3.8 %collective-permute-start.6 = (f32[136,128]{1,0:T(8,128)S(1)}, f32[136,128]{1,0:T(8,128)S(1)}, u32[]{:S(2)}, u32[]{:S(2)}) collective-permute-start(f32[136,128]{1,0:T(8,128)S(1)} %add_add_fusion.5), channel_id=1, source_target_pairs={{0,24},{8,16},{16,8},{24,0},{32,56},{40,48},{48,40},{56,32},{64,88... | collective-permute-start | bytes 208904 | tf_op jit(solution)/shard_map/ppermute | solution.py:431
  22.4 0.0 collective-permute-start.5
  22.4 0.7 collective-permute-start.4
  23.1 1.3 %collective-permute-done.6 = f32[136,128]{1,0:T(8,128)S(1)} collective-permute-done((f32[136,128]{1,0:T(8,128)S(1)}, f32[136,128]{1,0:T(8,128)S(1)}, u32[]{:S(2)}, u32[]{:S(2)}) %collective-permute-start.6) | collective-permute-done | bytes 69664 | tf_op jit(solution)/shard_map/ppermute | solution.py:431
  24.4 2.8 %collective-permute-done.5 = f32[136,128]{1,0:T(8,128)S(1)} collective-permute-done((f32[136,128]{1,0:T(8,128)S(1)}, f32[136,128]{1,0:T(8,128)S(1)}, u32[]{:S(2)}, u32[]{:S(2)}) %collective-permute-start.5) | collective-permute-done | bytes 69664 | tf_op jit(solution)/shard_map/ppermute | solution.py:431
  27.2 0.0 collective-permute-done.4
  27.2 2.8 %collective-permute-start.9 = (f32[136,128]{1,0:T(8,128)S(1)}, f32[136,128]{1,0:T(8,128)S(1)}, u32[]{:S(2)}, u32[]{:S(2)}) collective-permute-start(f32[136,128]{1,0:T(8,128)S(1)} %add_add_fusion.4), channel_id=1, source_target_pairs={{0,96},{8,104},{16,112},{24,120},{32,64},{40,72},{48,80},{56,88},{... | collective-permute-start | bytes 208904 | tf_op jit(solution)/shard_map/ppermute | solution.py:431
  30.0 0.3 collective-permute-start.8
  30.4 0.3 collective-permute-start.7
  30.7 1.3 %collective-permute-done.9 = f32[136,128]{1,0:T(8,128)S(1)} collective-permute-done((f32[136,128]{1,0:T(8,128)S(1)}, f32[136,128]{1,0:T(8,128)S(1)}, u32[]{:S(2)}, u32[]{:S(2)}) %collective-permute-start.9) | collective-permute-done | bytes 69664 | tf_op jit(solution)/shard_map/ppermute | solution.py:431
  32.0 2.7 %collective-permute-done.8 = f32[136,128]{1,0:T(8,128)S(1)} collective-permute-done((f32[136,128]{1,0:T(8,128)S(1)}, f32[136,128]{1,0:T(8,128)S(1)}, u32[]{:S(2)}, u32[]{:S(2)}) %collective-permute-start.8) | collective-permute-done | bytes 69664 | tf_op jit(solution)/shard_map/ppermute | solution.py:431
  34.7 5.0 %collective-permute-start.10 = (f32[136,128]{1,0:T(8,128)S(1)}, f32[136,128]{1,0:T(8,128)S(1)}, u32[]{:S(2)}, u32[]{:S(2)}) collective-permute-start(f32[136,128]{1,0:T(8,128)S(1)} %add_add_fusion.3.mine_ref), channel_id=1, source_target_pairs={{0,1},{1,0},{2,3},{3,2},{4,5},{5,4},{6,7},{7,6},{8,9},{9,8},{10,11... | collective-permute-start | bytes 208904 | tf_op jit(solution)/shard_map/ppermute | solution.py:431
  39.7 0.9 collective-permute-done.10.other_ref
  40.6 7.2 %factor_one.1 = (bf16[1024,256]{1,0:T(8,128)(2,1)S(1)}, f32[256,256]{1,0:T(8,128)S(1)}) custom-call(f32[136,128]{1,0:T(8,128)S(1)} %add_add_fusion.3.mine_ref, f32[136,128]{1,0:T(8,128)S(1)} %collective-permute-done.10.other_ref), custom_call_target="tpu_custom_call" | custom-call | tf_op jit(solution)/shard_map/factor_one/pallas_call | solution.py:326
  47.9 12.6 %first_and_gram_two.1 = (f32[12288,256]{1,0:T(8,128)S(1)}, f32[136,128]{1,0:T(8,128)S(1)}, f32[136,128]{1,0:T(8,128)S(1)}) custom-call(f32[12288,256]{1,0:T(8,128)} %x_hbm.3, bf16[1024,256]{1,0:T(8,128)(2,1)S(1)} %get-tuple-element.14.w_ref), custom_call_target="tpu_custom_call" | custom-call | tf_op jit(solution)/shard_map/first_and_gram_two/pallas_call | solution.py:178
  60.5 0.4 collective-permute-start.11
  60.9 0.9 collective-permute-done.11
  61.8 1.1 %collective-permute-start.14 = (f32[136,128]{1,0:T(8,128)S(1)}, f32[136,128]{1,0:T(8,128)S(1)}, u32[]{:S(2)}, u32[]{:S(2)}) collective-permute-start(f32[136,128]{1,0:T(8,128)S(1)} %add.70), channel_id=1, source_target_pairs={{0,6},{1,7},{2,4},{3,5},{4,2},{5,3},{6,0},{7,1},{8,14},{9,15},{10,... | collective-permute-start | bytes 208904 | tf_op jit(solution)/shard_map/ppermute | solution.py:431
  62.9 0.9 collective-permute-start.13
  63.8 1.4 %collective-permute-start.12 = (f32[136,128]{1,0:T(8,128)S(1)}, f32[136,128]{1,0:T(8,128)S(1)}, u32[]{:S(2)}, u32[]{:S(2)}) collective-permute-start(f32[136,128]{1,0:T(8,128)S(1)} %add.70), channel_id=1, source_target_pairs={{0,2},{1,3},{2,0},{3,1},{4,6},{5,7},{6,4},{7,5},{8,10},{9,11},{10,... | collective-permute-start | bytes 208904 | tf_op jit(solution)/shard_map/ppermute | solution.py:431
  65.2 1.1 %collective-permute-done.14 = f32[136,128]{1,0:T(8,128)S(1)} collective-permute-done((f32[136,128]{1,0:T(8,128)S(1)}, f32[136,128]{1,0:T(8,128)S(1)}, u32[]{:S(2)}, u32[]{:S(2)}) %collective-permute-start.14) | collective-permute-done | bytes 69664 | tf_op jit(solution)/shard_map/ppermute | solution.py:431
  66.3 1.4 %collective-permute-done.13 = f32[136,128]{1,0:T(8,128)S(1)} collective-permute-done((f32[136,128]{1,0:T(8,128)S(1)}, f32[136,128]{1,0:T(8,128)S(1)}, u32[]{:S(2)}, u32[]{:S(2)}) %collective-permute-start.13) | collective-permute-done | bytes 69664 | tf_op jit(solution)/shard_map/ppermute | solution.py:431
  67.7 0.6 collective-permute-done.12
  68.3 1.1 %collective-permute-start.17 = (f32[136,128]{1,0:T(8,128)S(1)}, f32[136,128]{1,0:T(8,128)S(1)}, u32[]{:S(2)}, u32[]{:S(2)}) collective-permute-start(f32[136,128]{1,0:T(8,128)S(1)} %add_add_fusion.2), channel_id=1, source_target_pairs={{0,24},{8,16},{16,8},{24,0},{32,56},{40,48},{48,40},{56,32},{64,88... | collective-permute-start | bytes 208904 | tf_op jit(solution)/shard_map/ppermute | solution.py:431
  69.4 1.0 %collective-permute-start.16 = (f32[136,128]{1,0:T(8,128)S(1)}, f32[136,128]{1,0:T(8,128)S(1)}, u32[]{:S(2)}, u32[]{:S(2)}) collective-permute-start(f32[136,128]{1,0:T(8,128)S(1)} %add_add_fusion.2), channel_id=1, source_target_pairs={{0,16},{8,24},{16,0},{24,8},{32,48},{40,56},{48,32},{56,40},{64,80... | collective-permute-start | bytes 208904 | tf_op jit(solution)/shard_map/ppermute | solution.py:431
  70.4 1.2 %collective-permute-start.15 = (f32[136,128]{1,0:T(8,128)S(1)}, f32[136,128]{1,0:T(8,128)S(1)}, u32[]{:S(2)}, u32[]{:S(2)}) collective-permute-start(f32[136,128]{1,0:T(8,128)S(1)} %add_add_fusion.2), channel_id=1, source_target_pairs={{0,8},{8,0},{16,24},{24,16},{32,40},{40,32},{48,56},{56,48},{64,72... | collective-permute-start | bytes 208904 | tf_op jit(solution)/shard_map/ppermute | solution.py:431
  71.7 1.1 %collective-permute-done.17 = f32[136,128]{1,0:T(8,128)S(1)} collective-permute-done((f32[136,128]{1,0:T(8,128)S(1)}, f32[136,128]{1,0:T(8,128)S(1)}, u32[]{:S(2)}, u32[]{:S(2)}) %collective-permute-start.17) | collective-permute-done | bytes 69664 | tf_op jit(solution)/shard_map/ppermute | solution.py:431
  72.8 1.3 %collective-permute-done.16 = f32[136,128]{1,0:T(8,128)S(1)} collective-permute-done((f32[136,128]{1,0:T(8,128)S(1)}, f32[136,128]{1,0:T(8,128)S(1)}, u32[]{:S(2)}, u32[]{:S(2)}) %collective-permute-start.16) | collective-permute-done | bytes 69664 | tf_op jit(solution)/shard_map/ppermute | solution.py:431
  74.1 0.3 collective-permute-done.15
  74.4 1.1 %collective-permute-start.20 = (f32[136,128]{1,0:T(8,128)S(1)}, f32[136,128]{1,0:T(8,128)S(1)}, u32[]{:S(2)}, u32[]{:S(2)}) collective-permute-start(f32[136,128]{1,0:T(8,128)S(1)} %add_add_fusion.1), channel_id=1, source_target_pairs={{0,96},{8,104},{16,112},{24,120},{32,64},{40,72},{48,80},{56,88},{... | collective-permute-start | bytes 208904 | tf_op jit(solution)/shard_map/ppermute | solution.py:431
  75.5 0.8 collective-permute-start.19
  76.3 1.4 %collective-permute-start.18 = (f32[136,128]{1,0:T(8,128)S(1)}, f32[136,128]{1,0:T(8,128)S(1)}, u32[]{:S(2)}, u32[]{:S(2)}) collective-permute-start(f32[136,128]{1,0:T(8,128)S(1)} %add_add_fusion.1), channel_id=1, source_target_pairs={{0,32},{8,40},{16,48},{24,56},{32,0},{40,8},{48,16},{56,24},{64,96... | collective-permute-start | bytes 208904 | tf_op jit(solution)/shard_map/ppermute | solution.py:431
  77.7 1.1 %collective-permute-done.20 = f32[136,128]{1,0:T(8,128)S(1)} collective-permute-done((f32[136,128]{1,0:T(8,128)S(1)}, f32[136,128]{1,0:T(8,128)S(1)}, u32[]{:S(2)}, u32[]{:S(2)}) %collective-permute-start.20) | collective-permute-done | bytes 69664 | tf_op jit(solution)/shard_map/ppermute | solution.py:431
  78.9 1.3 %collective-permute-done.19 = f32[136,128]{1,0:T(8,128)S(1)} collective-permute-done((f32[136,128]{1,0:T(8,128)S(1)}, f32[136,128]{1,0:T(8,128)S(1)}, u32[]{:S(2)}, u32[]{:S(2)}) %collective-permute-start.19) | collective-permute-done | bytes 69664 | tf_op jit(solution)/shard_map/ppermute | solution.py:431
  80.2 0.0 collective-permute-done.18
  80.2 4.1 %collective-permute-start.21 = (f32[136,128]{1,0:T(8,128)S(1)}, f32[136,128]{1,0:T(8,128)S(1)}, u32[]{:S(2)}, u32[]{:S(2)}) collective-permute-start(f32[136,128]{1,0:T(8,128)S(1)} %add_add_fusion.mine_ref), channel_id=1, source_target_pairs={{0,1},{1,0},{2,3},{3,2},{4,5},{5,4},{6,7},{7,6},{8,9},{9,8},{10,11... | collective-permute-start | bytes 208904 | tf_op jit(solution)/shard_map/ppermute | solution.py:431
  84.3 0.9 collective-permute-done.21.other_ref
  85.2 3.7 %factor_two.1 = (s32[1]{0:T(128)}, bf16[768,256]{1,0:T(8,128)(2,1)S(1)}, f32[256,256]{1,0:T(8,128)}) custom-call(f32[136,128]{1,0:T(8,128)S(1)} %add_add_fusion.mine_ref, f32[136,128]{1,0:T(8,128)S(1)} %collective-permute-done.21.other_ref, f32[256,256]{1,0:T(8,128)S(1)} %get-tuple-element.17.upper_ref), custom_call_target="tpu_custom_call" | custom-call | tf_op jit(solution)/shard_map/factor_two/pallas_call | solution.py:415
  89.0 5.7 %basis.1 = f32[12288,256]{1,0:T(8,128)} custom-call(s32[1]{0:T(128)} %get-tuple-element.18.small_ref, f32[12288,256]{1,0:T(8,128)S(1)} %get-tuple-element.19.f_ref, bf16[768,256]{1,0:T(8,128)(2,1)S(1)} %get-tuple-element.20.c_ref), custom_call_target="tpu_custom_call" | custom-call | tf_op jit(solution)/shard_map/basis/pallas_call | solution.py:231
  (9 shorter events, 0.1 us)
Async XLA Ops:
  8.9 2.4 %collective-permute-start = (f32[136,128]{1,0:T(8,128)S(1)}, f32[136,128]{1,0:T(8,128)S(1)}, u32[]{:S(2)}, u32[]{:S(2)}) collective-permute-start(f32[136,128]{1,0:T(8,128)S(1)} %get-tuple-element.13), channel_id=1, source_target_pairs={{0,1},{1,0},{2,3},{3,2},{4,5},{5,4},{6,7},{7,6},{8,9},{9,8},{10,11... | collective-permute-start | bytes 208904 | tf_op jit(solution)/shard_map/ppermute | solution.py:431
  11.2 4.8 %collective-permute-start.3 = (f32[136,128]{1,0:T(8,128)S(1)}, f32[136,128]{1,0:T(8,128)S(1)}, u32[]{:S(2)}, u32[]{:S(2)}) collective-permute-start(f32[136,128]{1,0:T(8,128)S(1)} %add.60), channel_id=1, source_target_pairs={{0,6},{1,7},{2,4},{3,5},{4,2},{5,3},{6,0},{7,1},{8,14},{9,15},{10,... | collective-permute-start | bytes 208904 | tf_op jit(solution)/shard_map/ppermute | solution.py:431
  13.9 4.7 %collective-permute-start.2 = (f32[136,128]{1,0:T(8,128)S(1)}, f32[136,128]{1,0:T(8,128)S(1)}, u32[]{:S(2)}, u32[]{:S(2)}) collective-permute-start(f32[136,128]{1,0:T(8,128)S(1)} %add.60), channel_id=1, source_target_pairs={{0,4},{1,5},{2,6},{3,7},{4,0},{5,1},{6,2},{7,3},{8,12},{9,13},{10,... | collective-permute-start | bytes 208904 | tf_op jit(solution)/shard_map/ppermute | solution.py:431
  14.4 4.2 %collective-permute-start.1 = (f32[136,128]{1,0:T(8,128)S(1)}, f32[136,128]{1,0:T(8,128)S(1)}, u32[]{:S(2)}, u32[]{:S(2)}) collective-permute-start(f32[136,128]{1,0:T(8,128)S(1)} %add.60), channel_id=1, source_target_pairs={{0,2},{1,3},{2,0},{3,1},{4,6},{5,7},{6,4},{7,5},{8,10},{9,11},{10,... | collective-permute-start | bytes 208904 | tf_op jit(solution)/shard_map/ppermute | solution.py:431
  18.6 5.8 %collective-permute-start.6 = (f32[136,128]{1,0:T(8,128)S(1)}, f32[136,128]{1,0:T(8,128)S(1)}, u32[]{:S(2)}, u32[]{:S(2)}) collective-permute-start(f32[136,128]{1,0:T(8,128)S(1)} %add_add_fusion.5), channel_id=1, source_target_pairs={{0,24},{8,16},{16,8},{24,0},{32,56},{40,48},{48,40},{56,32},{64,88... | collective-permute-start | bytes 208904 | tf_op jit(solution)/shard_map/ppermute | solution.py:431
  22.4 4.8 %collective-permute-start.5 = (f32[136,128]{1,0:T(8,128)S(1)}, f32[136,128]{1,0:T(8,128)S(1)}, u32[]{:S(2)}, u32[]{:S(2)}) collective-permute-start(f32[136,128]{1,0:T(8,128)S(1)} %add_add_fusion.5), channel_id=1, source_target_pairs={{0,16},{8,24},{16,0},{24,8},{32,48},{40,56},{48,32},{56,40},{64,80... | collective-permute-start | bytes 208904 | tf_op jit(solution)/shard_map/ppermute | solution.py:431
  22.4 4.8 %collective-permute-start.4 = (f32[136,128]{1,0:T(8,128)S(1)}, f32[136,128]{1,0:T(8,128)S(1)}, u32[]{:S(2)}, u32[]{:S(2)}) collective-permute-start(f32[136,128]{1,0:T(8,128)S(1)} %add_add_fusion.5), channel_id=1, source_target_pairs={{0,8},{8,0},{16,24},{24,16},{32,40},{40,32},{48,56},{56,48},{64,72... | collective-permute-start | bytes 208904 | tf_op jit(solution)/shard_map/ppermute | solution.py:431
  27.2 4.8 %collective-permute-start.9 = (f32[136,128]{1,0:T(8,128)S(1)}, f32[136,128]{1,0:T(8,128)S(1)}, u32[]{:S(2)}, u32[]{:S(2)}) collective-permute-start(f32[136,128]{1,0:T(8,128)S(1)} %add_add_fusion.4), channel_id=1, source_target_pairs={{0,96},{8,104},{16,112},{24,120},{32,64},{40,72},{48,80},{56,88},{... | collective-permute-start | bytes 208904 | tf_op jit(solution)/shard_map/ppermute | solution.py:431
  30.0 4.7 %collective-permute-start.8 = (f32[136,128]{1,0:T(8,128)S(1)}, f32[136,128]{1,0:T(8,128)S(1)}, u32[]{:S(2)}, u32[]{:S(2)}) collective-permute-start(f32[136,128]{1,0:T(8,128)S(1)} %add_add_fusion.4), channel_id=1, source_target_pairs={{0,64},{8,72},{16,80},{24,88},{32,96},{40,104},{48,112},{56,120},{... | collective-permute-start | bytes 208904 | tf_op jit(solution)/shard_map/ppermute | solution.py:431
  30.4 4.3 %collective-permute-start.7 = (f32[136,128]{1,0:T(8,128)S(1)}, f32[136,128]{1,0:T(8,128)S(1)}, u32[]{:S(2)}, u32[]{:S(2)}) collective-permute-start(f32[136,128]{1,0:T(8,128)S(1)} %add_add_fusion.4), channel_id=1, source_target_pairs={{0,32},{8,40},{16,48},{24,56},{32,0},{40,8},{48,16},{56,24},{64,96... | collective-permute-start | bytes 208904 | tf_op jit(solution)/shard_map/ppermute | solution.py:431
  34.7 5.9 %collective-permute-start.10 = (f32[136,128]{1,0:T(8,128)S(1)}, f32[136,128]{1,0:T(8,128)S(1)}, u32[]{:S(2)}, u32[]{:S(2)}) collective-permute-start(f32[136,128]{1,0:T(8,128)S(1)} %add_add_fusion.3.mine_ref), channel_id=1, source_target_pairs={{0,1},{1,0},{2,3},{3,2},{4,5},{5,4},{6,7},{7,6},{8,9},{9,8},{10,11... | collective-permute-start | bytes 208904 | tf_op jit(solution)/shard_map/ppermute | solution.py:431
  60.5 1.3 %collective-permute-start.11 = (f32[136,128]{1,0:T(8,128)S(1)}, f32[136,128]{1,0:T(8,128)S(1)}, u32[]{:S(2)}, u32[]{:S(2)}) collective-permute-start(f32[136,128]{1,0:T(8,128)S(1)} %get-tuple-element.16), channel_id=1, source_target_pairs={{0,1},{1,0},{2,3},{3,2},{4,5},{5,4},{6,7},{7,6},{8,9},{9,8},{10,11... | collective-permute-start | bytes 208904 | tf_op jit(solution)/shard_map/ppermute | solution.py:431
  61.8 4.5 %collective-permute-start.14 = (f32[136,128]{1,0:T(8,128)S(1)}, f32[136,128]{1,0:T(8,128)S(1)}, u32[]{:S(2)}, u32[]{:S(2)}) collective-permute-start(f32[136,128]{1,0:T(8,128)S(1)} %add.70), channel_id=1, source_target_pairs={{0,6},{1,7},{2,4},{3,5},{4,2},{5,3},{6,0},{7,1},{8,14},{9,15},{10,... | collective-permute-start | bytes 208904 | tf_op jit(solution)/shard_map/ppermute | solution.py:431
  62.9 4.8 %collective-permute-start.13 = (f32[136,128]{1,0:T(8,128)S(1)}, f32[136,128]{1,0:T(8,128)S(1)}, u32[]{:S(2)}, u32[]{:S(2)}) collective-permute-start(f32[136,128]{1,0:T(8,128)S(1)} %add.70), channel_id=1, source_target_pairs={{0,4},{1,5},{2,6},{3,7},{4,0},{5,1},{6,2},{7,3},{8,12},{9,13},{10,... | collective-permute-start | bytes 208904 | tf_op jit(solution)/shard_map/ppermute | solution.py:431
  63.8 4.5 %collective-permute-start.12 = (f32[136,128]{1,0:T(8,128)S(1)}, f32[136,128]{1,0:T(8,128)S(1)}, u32[]{:S(2)}, u32[]{:S(2)}) collective-permute-start(f32[136,128]{1,0:T(8,128)S(1)} %add.70), channel_id=1, source_target_pairs={{0,2},{1,3},{2,0},{3,1},{4,6},{5,7},{6,4},{7,5},{8,10},{9,11},{10,... | collective-permute-start | bytes 208904 | tf_op jit(solution)/shard_map/ppermute | solution.py:431
  68.3 4.5 %collective-permute-start.17 = (f32[136,128]{1,0:T(8,128)S(1)}, f32[136,128]{1,0:T(8,128)S(1)}, u32[]{:S(2)}, u32[]{:S(2)}) collective-permute-start(f32[136,128]{1,0:T(8,128)S(1)} %add_add_fusion.2), channel_id=1, source_target_pairs={{0,24},{8,16},{16,8},{24,0},{32,56},{40,48},{48,40},{56,32},{64,88... | collective-permute-start | bytes 208904 | tf_op jit(solution)/shard_map/ppermute | solution.py:431
  69.4 4.7 %collective-permute-start.16 = (f32[136,128]{1,0:T(8,128)S(1)}, f32[136,128]{1,0:T(8,128)S(1)}, u32[]{:S(2)}, u32[]{:S(2)}) collective-permute-start(f32[136,128]{1,0:T(8,128)S(1)} %add_add_fusion.2), channel_id=1, source_target_pairs={{0,16},{8,24},{16,0},{24,8},{32,48},{40,56},{48,32},{56,40},{64,80... | collective-permute-start | bytes 208904 | tf_op jit(solution)/shard_map/ppermute | solution.py:431
  70.4 4.0 %collective-permute-start.15 = (f32[136,128]{1,0:T(8,128)S(1)}, f32[136,128]{1,0:T(8,128)S(1)}, u32[]{:S(2)}, u32[]{:S(2)}) collective-permute-start(f32[136,128]{1,0:T(8,128)S(1)} %add_add_fusion.2), channel_id=1, source_target_pairs={{0,8},{8,0},{16,24},{24,16},{32,40},{40,32},{48,56},{56,48},{64,72... | collective-permute-start | bytes 208904 | tf_op jit(solution)/shard_map/ppermute | solution.py:431
  74.4 4.5 %collective-permute-start.20 = (f32[136,128]{1,0:T(8,128)S(1)}, f32[136,128]{1,0:T(8,128)S(1)}, u32[]{:S(2)}, u32[]{:S(2)}) collective-permute-start(f32[136,128]{1,0:T(8,128)S(1)} %add_add_fusion.1), channel_id=1, source_target_pairs={{0,96},{8,104},{16,112},{24,120},{32,64},{40,72},{48,80},{56,88},{... | collective-permute-start | bytes 208904 | tf_op jit(solution)/shard_map/ppermute | solution.py:431
  75.5 4.7 %collective-permute-start.19 = (f32[136,128]{1,0:T(8,128)S(1)}, f32[136,128]{1,0:T(8,128)S(1)}, u32[]{:S(2)}, u32[]{:S(2)}) collective-permute-start(f32[136,128]{1,0:T(8,128)S(1)} %add_add_fusion.1), channel_id=1, source_target_pairs={{0,64},{8,72},{16,80},{24,88},{32,96},{40,104},{48,112},{56,120},{... | collective-permute-start | bytes 208904 | tf_op jit(solution)/shard_map/ppermute | solution.py:431
  76.3 3.9 %collective-permute-start.18 = (f32[136,128]{1,0:T(8,128)S(1)}, f32[136,128]{1,0:T(8,128)S(1)}, u32[]{:S(2)}, u32[]{:S(2)}) collective-permute-start(f32[136,128]{1,0:T(8,128)S(1)} %add_add_fusion.1), channel_id=1, source_target_pairs={{0,32},{8,40},{16,48},{24,56},{32,0},{40,8},{48,16},{56,24},{64,96... | collective-permute-start | bytes 208904 | tf_op jit(solution)/shard_map/ppermute | solution.py:431
  80.2 5.0 %collective-permute-start.21 = (f32[136,128]{1,0:T(8,128)S(1)}, f32[136,128]{1,0:T(8,128)S(1)}, u32[]{:S(2)}, u32[]{:S(2)}) collective-permute-start(f32[136,128]{1,0:T(8,128)S(1)} %add_add_fusion.mine_ref), channel_id=1, source_target_pairs={{0,1},{1,0},{2,3},{3,2},{4,5},{5,4},{6,7},{7,6},{8,9},{9,8},{10,11... | collective-permute-start | bytes 208904 | tf_op jit(solution)/shard_map/ppermute | solution.py:431
